TPU v7x, 512 devices: a whole 4x4x16 slice. The times are simulated.
512 devices in a mesh: bead: 4 (over x), space: 128 (over z, y, core).
Axes of the slice: x: 4, y: 4, z: 16, core: 2. Of those that a mesh axis runs over, the one named last changes fastest.
Arguments:
- positions: float32 [16, 3, 8192], P('bead', None, 'space'), may hold values from -6 to 6
- momenta: float32 [16, 3, 8192], P('bead', None, 'space'), may hold values from -6 to 6
- forces: float32 [16, 3, 8192], P('bead', None, 'space'), may hold values from -6 to 6
- species: int32 [8192], P('space'), may hold values 0 or 1
- neighbours: int32 [16, 4, 8192], P('bead', None, 'space'), may hold values from 0 to 95
- counts: int32 [16, 8192], P('bead', 'space'), may hold values from 1 to 4, as said below
- ghost_rows: int32 [128, 2, 16], P('space'), may hold values from 0 to 63, as said below
- embed: float32 [2, 128], replicated, may hold values from -6 to 6
- radial_one: float32 [8, 128], replicated, may hold values from -2 to 2
- radial_two: float32 [8, 128], replicated, may hold values from -2 to 2
- mix_one: float32 [384, 128], replicated, may hold values from -0.3125 to 0.3125
- mix_two: float32 [384, 128], replicated, may hold values from -0.3125 to 0.3125
- projection: float32 [128, 128], replicated, may hold values from -0.5 to 0.5
- readout: float32 [2, 128], replicated, may hold values from -6 to 6
Outputs:
- positions_next: float32 [16, 3, 8192], P('bead', None, 'space')
- momenta_next: float32 [16, 3, 8192], P('bead', None, 'space')
- forces_next: float32 [16, 3, 8192], P('bead', None, 'space')
Inputs may be any that keep to these rules, and one draw needn't show every extreme that they name: `counts`: slots 0 to count - 1 of an atom are live. In every bead the first atom of every domain has 4 live slots. `ghost_rows`: each block names 16 distinct atoms of its own domain, given by their place among the domain's 64 atoms.
All inputs are finite; a program needn't handle non-finite values. No bound on the sum of `species` on one device may be relied on, other than what follows from the above.
Results may differ from a plain program's by a relative error of at most 0.0003.
Values sent between devices are 32-bit elements; how exact they have to be, the bound alone decides.
No kernel may reach another device: no remote copies, remote signals or barrier semaphores. Data moves between devices by JAX's collectives and lax.ppermute only.
A program may use at most 64 MiB of HBM per device.

v0:
```python
import math

import jax
import jax.numpy as jnp
from jax import lax
from jax.sharding import PartitionSpec as P

exact_prec = lax.Precision.HIGHEST
time_step = 1.0
cycle_freq = 0.75


def with_halo(cells, sides, width):
    for axis, dim in sides:
        count = lax.axis_size(axis)
        head = lax.slice_in_dim(cells, 0, width, axis=dim)
        tail = lax.slice_in_dim(cells, cells.shape[dim] - width, cells.shape[dim], axis=dim)
        cells = jnp.concatenate(
            [
                lax.ppermute(tail, axis, [(i, (i + 1) % count) for i in range(count)]),
                cells,
                lax.ppermute(head, axis, [((i + 1) % count, i) for i in range(count)]),
            ],
            axis=dim,
        )
    return cells


def mode_matrix(bead_count):
    mode_index = jnp.arange(bead_count, dtype=jnp.int32)
    phase_angle = (
        2.0 * math.pi * (mode_index[:, None] * mode_index[None, :]).astype(jnp.float32) / bead_count
    )
    cosine = math.sqrt(2.0 / bead_count) * jnp.cos(phase_angle)
    sine_part = math.sqrt(2.0 / bead_count) * jnp.sin(phase_angle)
    column = mode_index[None, :]
    half_mode = bead_count // 2
    alternating = jnp.where(mode_index % 2 == 0, 1.0, -1.0)[:, None] / math.sqrt(bead_count)
    inner_part = jnp.where(
        column < half_mode, cosine, jnp.where(column == half_mode, alternating, sine_part)
    )
    return jnp.where(column == 0, 1.0 / math.sqrt(bead_count), inner_part)


def propagate(normal, mode_ids, masses, bead_count):
    frequency = 2.0 * cycle_freq * jnp.sin(math.pi * mode_ids.astype(jnp.float32) / bead_count)
    phase_angle = frequency * time_step
    cosine = jnp.cos(phase_angle)[:, None, None]
    stiffness = (frequency * jnp.sin(phase_angle))[:, None, None]
    safe_freq = jnp.where(mode_ids == 0, 1.0, frequency)
    drift_gain = jnp.where(mode_ids == 0, time_step, jnp.sin(phase_angle) / safe_freq)[
        :, None, None
    ]
    coords = normal[:, 0]
    moment = normal[:, 1]
    new_coords = cosine * coords + drift_gain * moment / masses
    new_moment = cosine * moment - stiffness * masses * coords
    return jnp.stack([new_coords, new_moment], axis=1)


def radial_rates(count):
    return 0.25 * 16.0 ** (jnp.arange(count, dtype=jnp.float32) / (count - 1))


def harmonics(coord_x, coord_y, coord_z):
    sqrt_three = math.sqrt(3.0)
    dist_sq = coord_x * coord_x + coord_y * coord_y + coord_z * coord_z
    return [
        jnp.ones_like(coord_x),
        coord_x,
        coord_y,
        coord_z,
        sqrt_three * coord_x * coord_y,
        sqrt_three * coord_y * coord_z,
        0.5 * (3.0 * coord_z * coord_z - dist_sq),
        sqrt_three * coord_x * coord_z,
        0.5 * sqrt_three * (coord_x * coord_x - coord_y * coord_y),
    ]


def edge_geometry(pos_ext, neighbour_ids, live_slots, radial):
    atom_count = neighbour_ids.shape[1]
    offsets = pos_ext[:, neighbour_ids] - pos_ext[:, :atom_count][:, None, :]
    coord_x, coord_y, coord_z = (offsets[0], offsets[1], offsets[2])
    dist_sq = coord_x * coord_x + coord_y * coord_y + coord_z * coord_z
    harmonic = jnp.stack(harmonics(coord_x, coord_y, coord_z), axis=-1) * live_slots[..., None]
    gaussians = jnp.exp(-dist_sq[..., None] * radial_rates(radial.shape[0]))
    weights = jnp.einsum("kab,bc->kac", gaussians, radial, precision=exact_prec)
    return (harmonic, weights)


def invariants(harmonic, weights, values, neighbour_ids):
    gathered = values[neighbour_ids]
    moments = (
        jnp.einsum("kal,kac->alc", harmonic, weights * gathered, precision=exact_prec)
        / neighbour_ids.shape[0]
    )
    squares = moments * moments
    scalar_part = squares[:, 0]
    vector_part = jnp.sum(squares[:, 1:4], axis=1)
    tensor_part = jnp.sum(squares[:, 4:9], axis=1)
    return jnp.concatenate([scalar_part, vector_part, tensor_part], axis=1)


def layer_one(pos_ext, h0_ext, neighbour_ids, live_slots, radial, mixing):
    atom_count = neighbour_ids.shape[1]
    harmonic, weights = edge_geometry(pos_ext, neighbour_ids, live_slots, radial)
    feats = invariants(harmonic, weights, h0_ext, neighbour_ids)
    return h0_ext[:atom_count] + jax.nn.silu(jnp.dot(feats, mixing, precision=exact_prec))


def layer_two(pos_ext, hidden_one, u2_ext, neighbour_ids, live_slots, radial, mixing, readout):
    harmonic, weights = edge_geometry(pos_ext, neighbour_ids, live_slots, radial)
    feats = invariants(harmonic, weights, u2_ext, neighbour_ids)
    hidden_two = hidden_one + jax.nn.silu(jnp.dot(feats, mixing, precision=exact_prec))
    return jnp.sum(hidden_one * readout[0]) + jnp.sum(hidden_two * readout[1])


def on_device(
    positions,
    momenta,
    forces,
    species,
    neighbours,
    counts,
    ghost_rows,
    embed,
    radial_one,
    radial_two,
    mix_one,
    mix_two,
    projection,
    readout,
):
    bead_count = positions.shape[0]
    atom_count = positions.shape[2]
    ghosts = ghost_rows.shape[2]
    slot_count = neighbours.shape[1]
    total_beads = bead_count * lax.axis_size("bead")
    masses = 1.0 + 15.0 * species.astype(jnp.float32)
    half_kick = momenta + 0.5 * time_step * forces
    phase_space = jnp.stack([positions, half_kick], axis=1)
    matrix = mode_matrix(total_beads)
    first_mode = lax.axis_index("bead") * bead_count
    own_rows = lax.dynamic_slice_in_dim(matrix, first_mode, bead_count, 0)
    normal = lax.psum_scatter(
        jnp.einsum("bk,bsxa->ksxa", own_rows, phase_space, precision=exact_prec),
        "bead",
        scatter_dimension=0,
        tiled=True,
    )
    moved = propagate(
        normal, first_mode + jnp.arange(bead_count, dtype=jnp.int32), masses, total_beads
    )
    row_block = lax.dynamic_slice(
        matrix, (0, first_mode), (bead_count * lax.axis_size("bead"), bead_count)
    )
    phase_space = lax.psum_scatter(
        jnp.einsum("bk,ksxa->bsxa", row_block, moved, precision=exact_prec),
        "bead",
        scatter_dimension=0,
        tiled=True,
    )
    positions_next = phase_space[:, 0]
    momenta_mid = phase_space[:, 1]
    send_order = jnp.concatenate([ghost_rows[0, 1], ghost_rows[0, 0]])
    kinds = species.astype(jnp.float32)
    kind_rows = jnp.broadcast_to(kinds[send_order][None, None, :], (bead_count, 1, 2 * ghosts))
    outgoing = jnp.concatenate([positions_next[:, :, send_order], kind_rows], axis=1)
    widened = with_halo(outgoing, (("space", 2),), ghosts)
    incoming = jnp.concatenate([widened[:, :, :ghosts], widened[:, :, 3 * ghosts :]], axis=2)
    pos_ext = jnp.concatenate([positions_next, incoming[:, :3]], axis=2)
    kinds_ext = jnp.concatenate([kinds, incoming[0, 3]])
    h0_ext = embed[0][None, :] + kinds_ext[:, None] * (embed[1] - embed[0])[None, :]
    live = (jnp.arange(slot_count, dtype=jnp.int32)[None, :, None] < counts[:, None, :]).astype(
        jnp.float32
    )

    def run_first(pos_all):

        def single_bead(inputs):
            pos, ids, live_slots = inputs
            return layer_one(pos, h0_ext, ids, live_slots, radial_one, mix_one)

        return lax.map(jax.checkpoint(single_bead), (pos_all, neighbours, live))

    hidden_one, back_one = jax.vjp(run_first, pos_ext)
    wide_feats = with_halo(hidden_one[:, send_order], (("space", 1),), ghosts)
    ghost_feats = jnp.concatenate([wide_feats[:, :ghosts], wide_feats[:, 3 * ghosts :]], axis=1)
    u2_ext = jnp.einsum(
        "bac,cd->bad",
        jnp.concatenate([hidden_one, ghost_feats], axis=1),
        projection,
        precision=exact_prec,
    )

    def run_second(pos_all, hidden_all, u2_all):

        def single_bead(inputs):
            pos, hidden, u2_one, ids, live_slots = inputs
            return layer_two(pos, hidden, u2_one, ids, live_slots, radial_two, mix_two, readout)

        return lax.map(jax.checkpoint(single_bead), (pos_all, hidden_all, u2_all, neighbours, live))

    energies, back_two = jax.vjp(run_second, pos_ext, hidden_one, u2_ext)
    grad_pos_two, grad_hidden, grad_u2 = back_two(jnp.ones((bead_count,), jnp.float32))
    ext_grad = jnp.einsum("bad,cd->bac", grad_u2, projection, precision=exact_prec)
    ghost_grad = ext_grad[:, atom_count:]
    grad_hidden = grad_hidden + ext_grad[:, :atom_count]
    wide_grad = with_halo(ghost_grad, (("space", 1),), ghosts)
    owned_grad = jnp.zeros((bead_count, atom_count, ghost_grad.shape[2]), jnp.float32)
    owned_grad = owned_grad.at[:, ghost_rows[0, 1]].add(wide_grad[:, :ghosts])
    owned_grad = owned_grad.at[:, ghost_rows[0, 0]].add(wide_grad[:, 3 * ghosts :])
    grad_hidden = grad_hidden + owned_grad
    grad_pos_one = back_one(grad_hidden)[0]
    grad_pos = grad_pos_one + grad_pos_two
    wide_pos = with_halo(grad_pos[:, :, atom_count:], (("space", 2),), ghosts)
    local_grad = grad_pos[:, :, :atom_count]
    local_grad = local_grad.at[:, :, ghost_rows[0, 1]].add(wide_pos[:, :, :ghosts])
    local_grad = local_grad.at[:, :, ghost_rows[0, 0]].add(wide_pos[:, :, 3 * ghosts :])
    forces_next = -local_grad
    momenta_next = momenta_mid + 0.5 * time_step * forces_next
    return (positions_next, momenta_next, forces_next)


def solution(mesh):
    placed = (
        P("bead", None, "space"),
        P("bead", None, "space"),
        P("bead", None, "space"),
        P("space"),
        P("bead", None, "space"),
        P("bead", "space"),
        P("space", None, None),
        P(),
        P(),
        P(),
        P(),
        P(),
        P(),
        P(),
    )
    return jax.shard_map(
        on_device,
        mesh=mesh,
        in_specs=placed,
        out_specs=(P("bead", None, "space"), P("bead", None, "space"), P("bead", None, "space")),
        check_vma=False,
    )
```

profile of v0, /device:TPU:1, one launch (start us, length us, event | category | flops | bytes accessed | tf_op | source)
XLA Modules:
  0.0 203.9 jit_solution(2544548216908908344)
XLA Ops:
  2.6 14.6 %all-reduce.14 = f32[16,2,3,64]{3,0,2,1:T(8,128)S(1)} all-reduce(f32[16,2,3,64]{3,0,2,1:T(8,128)S(1)} %fusion.138), channel_id=2, replica_groups=mesh['bead'=4,'space'=128] {'bead'}, use_global_device_ids=true, to_apply=%region_0.1.clone | all-reduce | flops 6144 | bytes 49152
  19.5 11.2 %all-reduce.15 = f32[16,2,3,64]{3,0,2,1:T(8,128)S(1)} all-reduce(f32[16,2,3,64]{3,0,2,1:T(8,128)S(1)} %fusion.142), channel_id=3, replica_groups=mesh['bead'=4,'space'=128] {'bead'}, use_global_device_ids=true, to_apply=%region_1.2.clone | all-reduce | flops 6144 | bytes 49152
  33.0 11.0 %collective-permute-start = (f32[4,4,16]{2,1,0:T(4,128)S(1)}, f32[4,4,16]{2,1,0:T(4,128)S(1)}, u32[]{:S(2)}, u32[]{:S(2)}) collective-permute-start(f32[4,4,16]{2,1,0:T(4,128)S(1)} %get-tuple-element.1141), channel_id=1, source_target_pairs={{0,1},{1,2},{2,3},{3,4},{4,5},{5,6},{6,7},{7,8},{8,9},{9,10},{10,1... | collective-permute-start | bytes 3080 | tf_op jit(solution)/shard_map/ppermute | solution.py:20
  44.0 5.2 %collective-permute-start.1 = (f32[4,4,16]{2,1,0:T(4,128)S(1)}, f32[4,4,16]{2,1,0:T(4,128)S(1)}, u32[]{:S(2)}, u32[]{:S(2)}) collective-permute-start(f32[4,4,16]{2,1,0:T(4,128)S(1)} %get-tuple-element.1142), channel_id=1, source_target_pairs={{1,0},{2,1},{3,2},{4,3},{5,4},{6,5},{7,6},{8,7},{9,8},{10,9},{11,1... | collective-permute-start | bytes 3080 | tf_op jit(solution)/shard_map/ppermute | solution.py:22
  51.3 16.9 %while.45 = (s32[]{:T(128)}, f32[4,64,128]{2,1,0:T(8,128)S(1)}, f32[4,3,96]{1,2,0:T(8,128)S(1)}, s32[4,4,64]{2,1,0:T(4,128)S(1)}, f32[4,4,64]{2,1,0:T(4,128)S(1)...) while((s32[]{:T(128)}, f32[4,64,128]{2,1,0:T(8,128)S(1)}, ...), condition=%wide.region_5.6_spmd.clone, body=%wide.region_2.5_spmd.clone.sunk | while | flops 44790800 | bytes 1896005 | solution.py:185
  69.0 1.9 collective-permute-start.2
  70.9 7.7 %collective-permute-start.3 = (f32[4,16,128]{2,1,0:T(8,128)S(1)}, f32[4,16,128]{2,1,0:T(8,128)S(1)}, u32[]{:S(2)}, u32[]{:S(2)}) collective-permute-start(f32[4,16,128]{2,1,0:T(8,128)S(1)} %get-tuple-element.1138), channel_id=1, source_target_pairs={{1,0},{2,1},{3,2},{4,3},{5,4},{6,5},{7,6},{8,7},{9,8},{10,9},{11,1... | collective-permute-start | bytes 98312 | tf_op jit(solution)/shard_map/ppermute | solution.py:22
  80.5 51.6 %while.44 = (s32[]{:T(128)}, f32[4,3,96]{1,0,2:T(4,128)S(1)}, f32[4,64,128]{2,1,0:T(8,128)S(1)}, f32[4,96,128]{2,1,0:T(8,128)S(1)}, f32[4,3,96]{1,2,0:T(8,128)S(...) while((s32[]{:T(128)}, f32[4,3,96]{1,0,2:T(4,128)S(1)}, ...), condition=%wide.region_13.14_spmd, body=%wide.region_6.13_spmd.sunk | while | flops 93635088 | bytes 5588653 | solution.py:203
  86.0 1.4 scatter_custom_fusion.15
  89.4 1.9 scatter_fusion
  91.4 2.0 dynamic_update_slice.54
  99.0 1.4 scatter_custom_fusion.15
  102.4 1.9 scatter_fusion
  104.3 2.0 dynamic_update_slice.54
  115.3 1.9 scatter_fusion
  117.2 2.0 dynamic_update_slice.54
  124.8 1.4 scatter_custom_fusion.15
  128.2 1.9 scatter_fusion
  130.1 2.0 dynamic_update_slice.54
  132.5 1.9 collective-permute-start.4
  134.4 7.9 %collective-permute-start.5 = (f32[4,16,128]{2,1,0:T(8,128)S(1)}, f32[4,16,128]{2,1,0:T(8,128)S(1)}, u32[]{:S(2)}, u32[]{:S(2)}) collective-permute-start(f32[4,16,128]{2,1,0:T(8,128)S(1)} %get-tuple-element.1135), channel_id=1, source_target_pairs={{1,0},{2,1},{3,2},{4,3},{5,4},{6,5},{7,6},{8,7},{9,8},{10,9},{11,1... | collective-permute-start | bytes 98312 | tf_op jit(solution)/shard_map/ppermute | solution.py:22
  145.2 46.0 %while.46 = (s32[]{:T(128)}, f32[4,3,96]{1,0,2:T(4,128)S(1)}, f32[4,3,96]{1,2,0:T(8,128)S(1)}, s32[4,4,64]{2,1,0:T(4,128)S(1)}, f32[4,4,64]{2,1,0:T(4,128)S(1)},...) while((s32[]{:T(128)}, f32[4,3,96]{1,0,2:T(4,128)S(1)}, ...), condition=%wide.region_22.23_spmd.clone, body=%wide.region_16.22_spmd.clone.sunk | while | flops 93593616 | bytes 4931089 | solution.py:185
  152.8 1.9 scatter_fusion.1
  154.7 2.0 dynamic_update_slice.56
  164.2 1.9 scatter_fusion.1
  166.2 2.0 dynamic_update_slice.56
  175.7 1.9 scatter_fusion.1
  177.7 2.0 dynamic_update_slice.56
  187.2 1.9 scatter_fusion.1
  189.2 2.0 dynamic_update_slice.56
  191.3 1.9 collective-permute-start.6
  193.2 7.7 %collective-permute-start.7 = (f32[4,3,16]{1,0,2:T(4,128)S(1)}, f32[4,3,16]{1,0,2:T(4,128)S(1)}, u32[]{:S(2)}, u32[]{:S(2)}) collective-permute-start(f32[4,3,16]{1,0,2:T(4,128)S(1)} %get-tuple-element.1133), channel_id=1, source_target_pairs={{1,0},{2,1},{3,2},{4,3},{5,4},{6,5},{7,6},{8,7},{9,8},{10,9},{11,1... | collective-permute-start | bytes 2312 | tf_op jit(solution)/shard_map/ppermute | solution.py:22
  (631 shorter events, 92.6 us)
Async XLA Ops:
  0.6 78.6 %copy-start = (f32[128,128]{1,0:T(8,128)S(1)}, f32[128,128]{1,0:T(8,128)}, u32[]{:S(2)}) copy-start(f32[128,128]{1,0:T(8,128)} %param.32) | copy-start | bytes 196612
  0.9 0.7 copy-start.14
  0.9 0.7 copy-start.8
  0.9 0.7 copy-start.9
  1.6 0.7 copy-start.10
  30.7 0.7 copy-start.11
  33.0 16.2 %copy-start.13 = (f32[2,128]{1,0:T(2,128)S(1)}, f32[2,128]{1,0:T(2,128)}, u32[]{:S(2)}) copy-start(f32[2,128]{1,0:T(2,128)} %param.27) | copy-start | bytes 3076
  33.0 16.3 %copy-start.12 = (s32[4,64]{1,0:T(4,128)S(1)}, s32[4,64]{1,0:T(4,128)}, u32[]{:S(2)}) copy-start(s32[4,64]{1,0:T(4,128)} %param.25) | copy-start | bytes 3076
  33.0 16.3 %collective-permute-start = (f32[4,4,16]{2,1,0:T(4,128)S(1)}, f32[4,4,16]{2,1,0:T(4,128)S(1)}, u32[]{:S(2)}, u32[]{:S(2)}) collective-permute-start(f32[4,4,16]{2,1,0:T(4,128)S(1)} %get-tuple-element.1141), channel_id=1, source_target_pairs={{0,1},{1,2},{2,3},{3,4},{4,5},{5,6},{6,7},{7,8},{8,9},{9,10},{10,1... | collective-permute-start | bytes 3080 | tf_op jit(solution)/shard_map/ppermute | solution.py:20
  44.0 6.0 %collective-permute-start.1 = (f32[4,4,16]{2,1,0:T(4,128)S(1)}, f32[4,4,16]{2,1,0:T(4,128)S(1)}, u32[]{:S(2)}, u32[]{:S(2)}) collective-permute-start(f32[4,4,16]{2,1,0:T(4,128)S(1)} %get-tuple-element.1142), channel_id=1, source_target_pairs={{1,0},{2,1},{3,2},{4,3},{5,4},{6,5},{7,6},{8,7},{9,8},{10,9},{11,1... | collective-permute-start | bytes 3080 | tf_op jit(solution)/shard_map/ppermute | solution.py:22
  49.3 1.0 copy-start.7
  50.3 0.9 copy-start.1
  50.6 0.7 copy-start.3
  50.6 0.7 copy-start.5
  69.0 9.6 %collective-permute-start.2 = (f32[4,16,128]{2,1,0:T(8,128)S(1)}, f32[4,16,128]{2,1,0:T(8,128)S(1)}, u32[]{:S(2)}, u32[]{:S(2)}) collective-permute-start(f32[4,16,128]{2,1,0:T(8,128)S(1)} %get-tuple-element.1137), channel_id=1, source_target_pairs={{0,1},{1,2},{2,3},{3,4},{4,5},{5,6},{6,7},{7,8},{8,9},{9,10},{10,1... | collective-permute-start | bytes 98312 | tf_op jit(solution)/shard_map/ppermute | solution.py:20
  70.9 8.3 %collective-permute-start.3 = (f32[4,16,128]{2,1,0:T(8,128)S(1)}, f32[4,16,128]{2,1,0:T(8,128)S(1)}, u32[]{:S(2)}, u32[]{:S(2)}) collective-permute-start(f32[4,16,128]{2,1,0:T(8,128)S(1)} %get-tuple-element.1138), channel_id=1, source_target_pairs={{1,0},{2,1},{3,2},{4,3},{5,4},{6,5},{7,6},{8,7},{9,8},{10,9},{11,1... | collective-permute-start | bytes 98312 | tf_op jit(solution)/shard_map/ppermute | solution.py:22
  79.6 0.9 copy-start.2
  79.6 0.9 copy-start.4
  79.7 0.9 copy-start.6
  132.5 10.0 %collective-permute-start.4 = (f32[4,16,128]{2,1,0:T(8,128)S(1)}, f32[4,16,128]{2,1,0:T(8,128)S(1)}, u32[]{:S(2)}, u32[]{:S(2)}) collective-permute-start(f32[4,16,128]{2,1,0:T(8,128)S(1)} %get-tuple-element.1136), channel_id=1, source_target_pairs={{0,1},{1,2},{2,3},{3,4},{4,5},{5,6},{6,7},{7,8},{8,9},{9,10},{10,1... | collective-permute-start | bytes 98312 | tf_op jit(solution)/shard_map/ppermute | solution.py:20
  134.4 8.5 %collective-permute-start.5 = (f32[4,16,128]{2,1,0:T(8,128)S(1)}, f32[4,16,128]{2,1,0:T(8,128)S(1)}, u32[]{:S(2)}, u32[]{:S(2)}) collective-permute-start(f32[4,16,128]{2,1,0:T(8,128)S(1)} %get-tuple-element.1135), channel_id=1, source_target_pairs={{1,0},{2,1},{3,2},{4,3},{5,4},{6,5},{7,6},{8,7},{9,8},{10,9},{11,1... | collective-permute-start | bytes 98312 | tf_op jit(solution)/shard_map/ppermute | solution.py:22
  191.3 9.7 %collective-permute-start.6 = (f32[4,3,16]{1,0,2:T(4,128)S(1)}, f32[4,3,16]{1,0,2:T(4,128)S(1)}, u32[]{:S(2)}, u32[]{:S(2)}) collective-permute-start(f32[4,3,16]{1,0,2:T(4,128)S(1)} %get-tuple-element.1134), channel_id=1, source_target_pairs={{0,1},{1,2},{2,3},{3,4},{4,5},{5,6},{6,7},{7,8},{8,9},{9,10},{10,1... | collective-permute-start | bytes 2312 | tf_op jit(solution)/shard_map/ppermute | solution.py:20
  193.2 8.8 %collective-permute-start.7 = (f32[4,3,16]{1,0,2:T(4,128)S(1)}, f32[4,3,16]{1,0,2:T(4,128)S(1)}, u32[]{:S(2)}, u32[]{:S(2)}) collective-permute-start(f32[4,3,16]{1,0,2:T(4,128)S(1)} %get-tuple-element.1133), channel_id=1, source_target_pairs={{1,0},{2,1},{3,2},{4,3},{5,4},{6,5},{7,6},{8,7},{9,8},{10,9},{11,1... | collective-permute-start | bytes 2312 | tf_op jit(solution)/shard_map/ppermute | solution.py:22
where the time goes:
time: 207 us; the launch traced here: 204 us
  local copies, waits for them, and re-layouts  49.7 us (24%)
  starting transfers between devices  45.3 us (22%)
  matrix products  44.8 us (22%)
  other arithmetic  32 us (15%)
  blocking collectives  25.8 us (12%)
  loops' own time  2.61 us (1%)
    ppermute x4, starting transfers between devices, with_halo(): lax.ppermute(head, axis, [((i + 1) % count, i) for i in range(count)])  28.5 us
    dot_general x28, matrix products, invariants(): jnp.einsum('kal,kac->alc', harmonic, weights * gathered, precision=exact_...  28 us
    unnamed x2, blocking collectives  25.8 us
    ppermute x4, starting transfers between devices, with_halo(): lax.ppermute(tail, axis, [(i, (i + 1) % count) for i in range(count)])  16.7 us
    dynamic_update_slice x12, local copies, waits for them, and re-layouts, run_second(): lax.map(jax.checkpoint(single_bead), (pos_all, hidden_all, u2_all, neighb...  16 us
    scatter-add x8, other arithmetic, edge_geometry(): offsets = pos_ext[:, neighbour_ids] - pos_ext[:, :atom_count][:, None, :]  15.5 us
    gather x24, local copies, waits for them, and re-layouts, edge_geometry(): offsets = pos_ext[:, neighbour_ids] - pos_ext[:, :atom_count][:, None, :]  9.83 us
    dot_general x20, matrix products, edge_geometry(): weights = jnp.einsum('kab,bc->kac', gaussians, radial, precision=exact_prec)  9.52 us
  transfers between devices with their start and end apart: 8, of which 3 were waited for; matrix products, arithmetic and copies ran while one was open for 1% of the time, Pallas kernels for 0%

commit v1 on v0

v1 whole, which is shorter than its diff:
```python
import numpy as np

import jax
import jax.numpy as jnp
from jax import lax
from jax.experimental import pallas as pl
from jax.experimental.pallas import tpu as pltpu
from jax.sharding import PartitionSpec as P


F32 = jnp.float32
BF16 = jnp.bfloat16
BEADS = 16
TILES = 6
ROOT3 = float(np.sqrt(3.0))
VM = pl.BlockSpec(memory_space=pltpu.VMEM)
SM = pl.BlockSpec(memory_space=pltpu.SMEM)
RATES = 0.25 * 16.0 ** (np.arange(8) / 7.0)


def propagators():
    n = BEADS
    b = np.arange(n)
    phase = 2.0 * np.pi * np.outer(b, b) / n
    matrix = np.where(b[None] < n // 2, np.cos(phase), np.sin(phase)) * np.sqrt(2.0 / n)
    matrix[:, n // 2] = np.where(b % 2 == 0, 1.0, -1.0) / np.sqrt(n)
    matrix[:, 0] = 1.0 / np.sqrt(n)
    w = 1.5 * np.sin(np.pi * b / n)
    drift = np.where(b == 0, 1.0, np.sin(w) / np.where(b == 0, 1.0, w))
    return [(matrix * d) @ matrix.T for d in (np.cos(w), drift, w * np.sin(w))]


def mode_tables():
    cosine, drift, stiff = propagators()
    one = np.zeros((BEADS, 2, 8, 64), np.float32)
    four = np.zeros((4, 64, 64), np.float32)
    for bead in range(BEADS):
        for src in range(BEADS):
            for c in range(3):
                col = (src // 4) * 16 + (src % 4) * 3 + c
                one[bead, 0, c, col] = cosine[bead, src]
                one[bead, 1, c, col] = drift[bead, src]
                row = (bead % 4) * 4 + c
                four[bead // 4, row, col] = cosine[bead, src]
                four[bead // 4, 16 + row, col] = drift[bead, src]
                four[bead // 4, 32 + row, col] = cosine[bead, src]
                four[bead // 4, 48 + row, col] = stiff[bead, src]
    return one, four


def split(x):
    high = x.astype(BF16)
    return high, (x - high.astype(F32)).astype(BF16)


def dot(a, b):
    return lax.dot_general(a, b, (((1,), (0,)), ((), ())), preferred_element_type=F32)


def dot_t(a, b):
    return lax.dot_general(a, b, (((1,), (1,)), ((), ())), preferred_element_type=F32)


def dot3(a, b):
    return dot(a[0], b[0]) + (dot(a[0], b[1]) + dot(a[1], b[0]))


def lanes(rows):
    return lax.broadcasted_iota(jnp.int32, (rows, 128), 1)


def turn(x):
    return pltpu.roll(x, 64, 1)


def pack_kernel(place, pos, mom, force, species, nbr, counts, ghost, out):
    side = place[2]
    raw = [jnp.concatenate([pos[b], mom[b] + 0.5 * force[b]], axis=1) for b in range(4)]
    kind = species[...].astype(F32)
    ghosts = ghost[0].astype(F32)
    last = jnp.concatenate([ghosts[0:1], ghosts[1:2], jnp.zeros((1, 96), F32)], axis=1)
    for i in range(4):
        bead = i ^ (2 * side)
        e = nbr[bead].astype(F32)
        n = counts[pl.ds(bead, 1), :].astype(F32)
        rows = raw + [
            jnp.concatenate([e[0:1], e[1:2]], axis=1),
            jnp.concatenate([e[2:3], e[3:4]], axis=1),
            jnp.concatenate([n, kind], axis=1),
            last,
        ]
        block = jnp.concatenate(rows, axis=0)
        for r in range(4):
            out[r * 4 + i] = block


def modes_kernel(place, got, one, four, packed, pos_out, mom_out):
    r, dom, side = place[0], place[1], place[2]
    bead = 4 * r + (dom ^ (2 * side))
    low = lanes(8) < 64

    def stacked(d):
        return jnp.concatenate([got[s * 4 + d] for s in range(4)], axis=0)

    def exact(a, b):
        return jnp.dot(a, b, precision=lax.Precision.HIGHEST, preferred_element_type=F32)

    for t in range(2):
        even, odd = stacked(2 * t), stacked(2 * t + 1)
        info_even = got[r * 4 + 2 * t][8:16]
        info_odd = got[r * 4 + 2 * t + 1][8:16]
        left = jnp.where(low, info_even, turn(info_odd))
        right = jnp.where(low, turn(info_even), info_odd)
        kind = right[6:7]
        mass = 1.0 + 15.0 * kind
        cos_part = jnp.where(low, exact(one[bead, 0], even), turn(exact(one[bead, 0], odd)))
        drift_part = jnp.where(low, turn(exact(one[bead, 1], even)), exact(one[bead, 1], odd))
        coords = cos_part + drift_part / mass
        row = lax.broadcasted_iota(jnp.int32, (8, 128), 0)
        packed[t, 0:8] = jnp.where(row == 3, jnp.broadcast_to(kind, (8, 128)), coords)
        packed[t, 8:12] = left[4:8]
        packed[t, 12:16] = right[4:8]
    own = exact(four[r], stacked(dom))
    mass = 1.0 + 15.0 * turn(got[r * 4 + dom][8:16])[6:7]
    coords = own[0:16] + turn(own[16:32]) / mass
    moment = turn(own[32:48]) - mass * own[48:64]
    for b in range(4):
        pos_out[b] = coords[4 * b : 4 * b + 3, 0:64]
        mom_out[b] = moment[4 * b : 4 * b + 3, 0:64]


def force_kernel(
    place, own, plane_half, next_half, embed, radial_one, radial_two, mix_one, mix_two, proj, readout,
    out,
    pk, hot, ys, gp, mom_one, slope_one, u_two, du_two, tk, gk, rk, mom_two, dp, dyq,
):
    side = place[2]
    low = lanes(8) < 64
    low1 = lanes(1) < 64
    low_wide = lanes(128) < 64

    in_plane, across = plane_half[...], next_half[...]
    before = jnp.where(side == 1, in_plane, across)
    after = jnp.where(side == 1, across, in_plane)
    pk[0] = before[0]
    pk[1:3] = before
    pk[3:5] = own[...]
    pk[5:7] = after
    pk[7] = after[1]

    def column(row):
        return jnp.broadcast_to(row, (128, 128)).T

    base, step = embed[0:1], embed[1:2] - embed[0:1]
    base_col, step_col = column(base), column(step)
    top_col = column(readout[1:2])
    both_col = column(readout[0:1] + readout[1:2])
    w_one = jnp.concatenate([radial_one[...] * base, radial_one[...] * step], axis=0)
    w_one2 = split(w_one)
    w_one_cat = jnp.concatenate([w_one2[0], w_one2[0], w_one2[1]], axis=0).astype(F32).T.astype(BF16)
    w_two2 = split(radial_two[...])
    wh, wl = w_two2[0].astype(F32), w_two2[1].astype(F32)
    w_two_cat = jnp.concatenate([wh, wh, wl, jnp.zeros((8, 128), F32)], axis=0).T.astype(BF16)
    mix1, mix2, prj = split(mix_one[...]), split(mix_two[...]), split(proj[...])
    mix1_t = split(mix_one[...].T)
    mix2_t = split(mix_two[...].T)
    prj_t = split(proj[...].T)
    rate_row = lax.broadcasted_iota(jnp.int32, (8, 128), 0)
    rate = jnp.zeros((8, 128), F32)
    for n in range(8):
        rate = jnp.where(rate_row == n, float(RATES[n]), rate)
    spot = lax.broadcasted_iota(jnp.int32, (256, 128), 0).astype(F32)
    ghost_spot = lax.broadcasted_iota(jnp.int32, (32, 128), 0).astype(F32) + 64.0

    def sigmoid(v):
        return 1.0 / (1.0 + jnp.exp(-v))

    def first(t, _):
        here = pk[t + 1, 0:8]
        info = pk[t + 1, 8:16]
        beside = jnp.where(low, pk[t + 2, 0:8], pk[t, 0:8])
        wide = jnp.concatenate([here, beside], axis=1)
        a = wide.astype(BF16).astype(F32)
        b = (wide - a).astype(BF16).astype(F32)
        c = (wide - a - b).astype(BF16).astype(F32)
        parts = jnp.concatenate([a, b, c, jnp.zeros((8, 256), F32)], axis=0).astype(BF16)
        g_prev, g_here, g_next = pk[t, 11:12], info[3:4], pk[t + 2, 11:12]
        head = lanes(1) < 16
        table = jnp.concatenate(
            [
                jnp.where(head, turn(g_prev) + 192.0, turn(g_here) + 64.0),
                jnp.where(head, g_here, g_next + 128.0),
                jnp.zeros((14, 128), F32),
            ],
            axis=0,
        )[:, 0:32].astype(BF16)
        count = info[2:3]
        sums = [None] * 9
        for k, row in enumerate((0, 4, 1, 5)):
            e = info[row : row + 1]
            hit = jnp.where(ghost_spot == e, 1.0, 0.0).astype(BF16)
            far = dot(table, hit)
            n = jnp.where(
                e < 64.0, e + jnp.where(low1, 0.0, 64.0), jnp.where(low1, far[0:1], far[1:2])
            )
            one_hot = jnp.where(spot == n, 1.0, 0.0).astype(BF16)
            hot[t, :, k * 128 : (k + 1) * 128] = one_hot
            got = dot(parts, one_hot)
            there = got[0:8] + (got[8:16] + got[16:24])
            off = there - here
            x, y, z = off[0:1], off[1:2], off[2:3]
            q = x * x + y * y + z * z
            live = jnp.where(count > float(k), 0.25, 0.0)
            g = jnp.exp(-rate * q) * live
            both = jnp.concatenate([g, g * there[3:4]], axis=0)
            harmonic = [
                None, x, y, z, ROOT3 * x * y, ROOT3 * y * z, 0.5 * (3.0 * z * z - q), ROOT3 * x * z,
                (0.5 * ROOT3) * (x * x - y * y),
            ]
            gp[t, k] = both
            ys[t, k, 0:8] = jnp.concatenate(harmonic[1:9], axis=0)
            for l in range(9):
                term = both if l == 0 else harmonic[l] * both
                sums[l] = term if sums[l] is None else sums[l] + term
        high, lo = split(jnp.concatenate(sums, axis=1))
        moments = dot(w_one_cat, jnp.concatenate([high, lo, high], axis=0))
        m = [moments[:, l * 128 : (l + 1) * 128] for l in range(9)]
        for l in range(9):
            mom_one[t, l] = m[l]
        inv = jnp.concatenate(
            [m[0] * m[0], sum(m[l] * m[l] for l in (1, 2, 3)), sum(m[l] * m[l] for l in range(4, 9))],
            axis=0,
        )
        v = dot3(mix1_t, split(inv))
        sig = sigmoid(v)
        slope_one[t] = sig * (1.0 + v * (1.0 - sig))
        h = base_col + here[3:4] * step_col + v * sig
        u_two[t] = dot3(prj_t, split(h))
        return 0

    lax.fori_loop(0, TILES, first, 0)

    du_two[...] = jnp.zeros_like(du_two)
    dp[...] = jnp.zeros_like(dp)

    def second(t, _):
        near = u_two[t]
        beside = jnp.where(low_wide, u_two[t + 1], u_two[t - 1])
        high, lo = split(jnp.concatenate([near, beside], axis=1))
        parts = jnp.concatenate([high, lo], axis=0)
        for k in range(4):
            got = dot(parts, hot[t, :, k * 128 : (k + 1) * 128])
            nodes = got[0:128] + got[128:256]
            g = gp[t, k, 0:8]
            gh = g.astype(BF16).astype(F32)
            rows = jnp.concatenate([gh, g - gh, gh, jnp.zeros((8, 128), F32)], axis=0).astype(BF16)
            weight = dot(w_two_cat, rows)
            gk[k] = nodes
            rk[k] = weight
            tk[k] = nodes * weight
        squares = [None] * 3
        for l in range(9):
            m = None
            for k in range(4):
                term = tk[k] if l == 0 else ys[t, k, l - 1 : l] * tk[k]
                m = term if m is None else m + term
            mom_two[l] = m
            part = 0 if l == 0 else 1 if l < 4 else 2
            squares[part] = m * m if squares[part] is None else squares[part] + m * m
        v = dot3(mix2_t, split(jnp.concatenate(squares, axis=0)))
        sig = sigmoid(v)
        dv = top_col * (sig * (1.0 + v * (1.0 - sig)))
        dinv = 2.0 * dot3(mix2, split(dv))
        for l in range(9):
            part = 0 if l == 0 else 1 if l < 4 else 2
            mom_two[l] = mom_two[l] * dinv[part * 128 : (part + 1) * 128]
        back = None
        for k in range(4):
            dt = mom_two[0]
            dys = []
            for l in range(1, 9):
                dm = mom_two[l]
                dt = dt + ys[t, k, l - 1 : l] * dm
                dys.append(jnp.sum(dm * tk[k], axis=0, keepdims=True))
            g = gp[t, k, 0:8]
            dg = dot3(w_two2, split(dt * gk[k]))
            dq = jnp.sum(-rate * g * dg, axis=0, keepdims=True)
            dyq[t, k, 0:8] = jnp.concatenate(dys, axis=0)
            dyq[t, k, 8:16] = jnp.broadcast_to(dq, (8, 128))
            high, lo = split(dt * rk[k])
            term = dot_t(jnp.concatenate([high, lo], axis=0), hot[t, :, k * 128 : (k + 1) * 128])
            back = term if back is None else back + term
        back = back[0:128] + back[128:256]
        du_two[t] += back[:, 0:128]
        aside = back[:, 128:256]
        du_two[t + 1] += jnp.where(low_wide, aside, 0.0)
        du_two[t - 1] += jnp.where(low_wide, 0.0, aside)
        return 0

    lax.fori_loop(1, TILES - 1, second, 0)

    def third(t, _):
        dh = both_col + dot3(prj, split(du_two[t]))
        dinv = 2.0 * dot3(mix1, split(dh * slope_one[t]))
        parts = []
        for l in range(9):
            part = 0 if l == 0 else 1 if l < 4 else 2
            parts.append(mom_one[t, l] * dinv[part * 128 : (part + 1) * 128])
        dm = dot3(w_one2, split(jnp.concatenate(parts, axis=1)))
        dm = [dm[:, l * 128 : (l + 1) * 128] for l in range(9)]
        rate2 = jnp.concatenate([rate, rate], axis=0)
        back = None
        centre = None
        for k in range(4):
            g = gp[t, k]
            dg = dm[0]
            dys = []
            for l in range(1, 9):
                dg = dg + ys[t, k, l - 1 : l] * dm[l]
                dys.append(dyq[t, k, l - 1 : l] + jnp.sum(g * dm[l], axis=0, keepdims=True))
            dq = dyq[t, k, 8:9] - jnp.sum(rate2 * g * dg, axis=0, keepdims=True)
            x, y, z = ys[t, k, 0:1], ys[t, k, 1:2], ys[t, k, 2:3]
            d1, d2, d3, d4, d5, d6, d7, d8 = dys
            dx = d1 + ROOT3 * (y * d4 + z * d7 + x * d8) + x * (2.0 * dq - d6)
            dy = d2 + ROOT3 * (x * d4 + z * d5 - y * d8) + y * (2.0 * dq - d6)
            dz = d3 + ROOT3 * (y * d5 + x * d7) + 2.0 * z * (dq + d6)
            d = jnp.concatenate([dx, dy, dz, jnp.zeros((5, 128), F32)], axis=0)
            centre = d if centre is None else centre + d
            dh_ = d.astype(BF16).astype(F32)
            rows = jnp.concatenate([dh_, d - dh_], axis=0).astype(BF16)
            term = dot_t(rows, hot[t, :, k * 128 : (k + 1) * 128])
            back = term if back is None else back + term
        back = back[0:8] + back[8:16]
        dp[t] += back[:, 0:128] - centre
        aside = back[:, 128:256]
        dp[t + 1] += jnp.where(low, aside, 0.0)
        dp[t - 1] += jnp.where(low, 0.0, aside)
        return 0

    lax.fori_loop(1, TILES - 1, third, 0)

    for t in range(2):
        f = -dp[t + 2]
        out[2 * t] = f
        out[2 * t + 1] = turn(f)


def finish_kernel(place, got, mid, force_out, mom_out):
    side = place[2]
    for b in range(4):
        f = got[b ^ (2 * side)][0:3, 0:64]
        force_out[b] = f
        mom_out[b] = mid[b] + 0.5 * f


def shape(*dims):
    return jax.ShapeDtypeStruct(dims, F32)


def on_device(
    positions, momenta, forces, species, neighbours, counts, ghost_rows,
    embed, radial_one, radial_two, mix_one, mix_two, projection, readout,
):
    count = lax.axis_size("space")
    r = lax.axis_index("bead")
    s = lax.axis_index("space")
    place = jnp.stack([r, s % 4, (s // 4) % 2]).astype(jnp.int32)
    both = ("bead", "space")
    halves = [[b * count + h * 4 + i for b in range(4) for i in range(4)] for h in range(count // 4)]
    quads = [[b * count + h * 4 + i for i in range(4)] for b in range(4) for h in range(count // 4)]
    in_plane, across = [], []
    for b in range(4):
        for z in range(count // 8):
            for i in range(4):
                here = b * count + z * 8 + i
                mate = b * count + z * 8 + 4 + (i ^ 2)
                back = b * count + (z * 8 - 4) % count + (i ^ 2)
                in_plane += [(here, mate), (mate, here)]
                across += [(here, back), (back, here)]

    sent = pl.pallas_call(
        pack_kernel, out_shape=shape(16, 16, 128), in_specs=[SM] + [VM] * 7, out_specs=VM, name="pack",
    )(place, positions, momenta, forces, species[None, :], neighbours, counts, ghost_rows)
    got = lax.all_to_all(sent, both, 0, 0, axis_index_groups=halves)
    one, four = mode_tables()
    own, positions_next, mid = pl.pallas_call(
        modes_kernel,
        out_shape=(shape(2, 16, 128), shape(4, 3, 64), shape(4, 3, 64)),
        in_specs=[SM] + [VM] * 3,
        out_specs=(VM, VM, VM),
        name="modes",
    )(place, got, jnp.asarray(one), jnp.asarray(four))
    next_half = lax.ppermute(own, both, across)
    plane_half = lax.ppermute(own, both, in_plane)
    block = lambda *dims: pltpu.VMEM(dims, F32)
    grad = pl.pallas_call(
        force_kernel,
        out_shape=shape(4, 8, 128),
        in_specs=[SM] + [VM] * 10,
        out_specs=VM,
        scratch_shapes=[
            block(8, 16, 128),
            pltpu.VMEM((TILES, 256, 512), BF16),
            block(TILES, 4, 8, 128),
            block(TILES, 4, 16, 128),
            block(TILES, 9, 128, 128),
            block(TILES, 128, 128),
            block(TILES, 128, 128),
            block(TILES, 128, 128),
            block(4, 128, 128),
            block(4, 128, 128),
            block(4, 128, 128),
            block(9, 128, 128),
            block(TILES, 8, 128),
            block(TILES, 4, 16, 128),
        ],
        name="force",
    )(place, own, plane_half, next_half, embed, radial_one, radial_two, mix_one, mix_two, projection, readout)
    back = lax.all_to_all(grad, both, 0, 0, axis_index_groups=quads)
    forces_next, momenta_next = pl.pallas_call(
        finish_kernel,
        out_shape=(shape(4, 3, 64), shape(4, 3, 64)),
        in_specs=[SM] + [VM] * 2,
        out_specs=(VM, VM),
        name="finish",
    )(place, back, mid)
    return positions_next, momenta_next, forces_next


def solution(mesh):
    spread = P("bead", None, "space")
    placed = (
        spread, spread, spread, P("space"), spread, P("bead", "space"), P("space", None, None),
    ) + (P(),) * 7
    return jax.shard_map(
        on_device, mesh=mesh, in_specs=placed, out_specs=(spread,) * 3, check_vma=False
    )
```

time: 207 us -> 73 us (0.35); the launches traced: 204 us -> 72.4 us
  matrix products: 44.8 us -> 0 us
  local copies, waits for them, and re-layouts: 49.7 us -> 6.38 us
  other arithmetic: 32 us -> 0.61 us
  starting transfers between devices: 45.3 us -> 15.8 us
  Pallas kernels: 0 us -> 25.4 us
  blocking collectives: 25.8 us -> 17 us
  waiting for transfers between devices: 1.83 us -> 6.49 us
  loops' own time: 2.61 us -> 0 us
    dot_general x72 -> x0, matrix products: 44.8 us -> none  [the longest x28 28 us: invariants(): jnp.einsum('kal,kac->alc', harmonic, weights * gathered, precision=exact_...]
    ppermute x8 -> x2, starting transfers between devices: 45.3 us -> 10.7 us  [the longest x1 8.76 us: on_device(): next_half = lax.ppermute(own, both, across)]
    unnamed x2 -> x0, blocking collectives: 25.8 us -> none
    scatter-add x16 -> x0, other arithmetic: 25.5 us -> none  [the longest x8 15.5 us: edge_geometry(): offsets = pos_ext[:, neighbour_ids] - pos_ext[:, :atom_count][:, None, :]]
    pallas_call x0 -> x4, Pallas kernels: none -> 25.4 us  [the longest x1 20.4 us: on_device(): pl.pallas_call(force_kernel, out_shape=shape(4, 8, 128), in_specs=[SM] +...]
    gather x41 -> x0, local copies, waits for them, and re-layouts: 20.7 us -> none  [the longest x24 9.83 us: edge_geometry(): offsets = pos_ext[:, neighbour_ids] - pos_ext[:, :atom_count][:, None, :]]
    all_to_all x0 -> x1, blocking collectives: none -> 17 us  [on_device(): got = lax.all_to_all(sent, both, 0, 0, axis_index_groups=halves)]
    dynamic_update_slice x16 -> x0, local copies, waits for them, and re-layouts: 16.1 us -> none  [the longest x12 16 us: run_second(): lax.map(jax.checkpoint(single_bead), (pos_all, hidden_all, u2_all, neighb...]
  transfers between devices with their start and end apart: 8 -> 3, of which waited for: 3 -> 2; matrix products, arithmetic and copies ran while one was open for 1% -> 1% of each run, Pallas kernels for 0% -> 0%
where the time goes in v1:
time: 73 us; the launch traced here: 72.4 us
  Pallas kernels  25.4 us (35%)
  blocking collectives  17 us (23%)
  starting transfers between devices  15.8 us (22%)
  waiting for transfers between devices  6.49 us (9%)
  local copies, waits for them, and re-layouts  6.38 us (9%)
    pallas_call x1, Pallas kernels, on_device(): pl.pallas_call(force_kernel, out_shape=shape(4, 8, 128), in_specs=[SM] +...  20.4 us
    all_to_all x1, blocking collectives, on_device(): got = lax.all_to_all(sent, both, 0, 0, axis_index_groups=halves)  17 us
    ppermute x1, starting transfers between devices, on_device(): next_half = lax.ppermute(own, both, across)  8.76 us
    unnamed x22, local copies, waits for them, and re-layouts  6.38 us
    all_to_all x1, starting transfers between devices, on_device(): back = lax.all_to_all(grad, both, 0, 0, axis_index_groups=quads)  5.09 us
    ppermute x1, waiting for transfers between devices, on_device(): plane_half = lax.ppermute(own, both, in_plane)  3.96 us
    all_to_all x1, waiting for transfers between devices, on_device(): back = lax.all_to_all(grad, both, 0, 0, axis_index_groups=quads)  2.53 us
    pallas_call x1, Pallas kernels, on_device(): pl.pallas_call(modes_kernel, out_shape=(shape(2, 16, 128), shape(4, 3, 64...  2.07 us
  transfers between devices with their start and end apart: 3, of which 2 were waited for; matrix products, arithmetic and copies ran while one was open for 1% of the time, Pallas kernels for 0%

profile of v1, /device:TPU:1, one launch (start us, length us, event | category | flops | bytes accessed | tf_op | source)
XLA Modules:
  0.0 72.4 jit_solution(13858932011593509757)
XLA Ops:
  0.7 0.0 copy-start.5
  0.7 0.7 copy-done.5
  1.4 0.0 copy-start.6
  1.4 0.6 copy.19.pos
  1.9 0.1 copy-done.6
  2.0 0.0 copy-start.7
  2.0 0.6 copy.20.mom
  2.6 0.1 copy-done.7
  2.7 0.6 copy.21.force
  3.3 0.6 pad_add_fusion.place
  4.0 1.5 %pack.1 = f32[16,16,128]{2,1,0:T(8,128)} custom-call(s32[3]{0:T(128)} %pad_add_fusion.place, f32[4,3,64]{2,1,0:T(4,128)} %copy.19.pos, f32[4,3,64]{2,1,0:T(4,128)} %copy.20.mom, f32[4,3,64]{2,1,0:T(4,128)} %copy.21.force, s32[1,64]{1,0:T(1,128)} %bitcast.4, s32[4,4,64]{2,1,0:T(4,128)} %nbr.1, s32[4,64]{1,0:T(4,128)} %counts.1, s32[1,2,16]{2,1,0:T(2,128)} %ghost.1), custom_call_target="tpu_custom_call" | custom-call | tf_op jit(solution)/shard_map/pack/pallas_call | solution.py:381
  5.5 17.0 %all_to_all.10.got = f32[16,16,128]{2,1,0:T(8,128)} all-to-all(f32[16,16,128]{2,1,0:T(8,128)} %pack.1), channel_id=1, replica_groups={{0,1,2,3,128,129,130,131,256,257,258,259,384,385,386,387},{4,5,6,7,132,..., dimensions={0} | all-to-all | bytes 262144 | tf_op jit(solution)/shard_map/all_to_all | solution.py:384
  22.5 2.1 %modes.1 = (f32[2,16,128]{2,1,0:T(8,128)}, f32[4,3,64]{2,1,0:T(4,128)}, f32[4,3,64]{2,1,0:T(4,128)}) custom-call(s32[3]{0:T(128)} %pad_add_fusion.place, f32[16,16,128]{2,1,0:T(8,128)} %all_to_all.10.got, f32[16,2,8,64]{3,2,1,0:T(8,128)} %constant.47.clone.one, f32[4,64,64]{2,1,0:T(8,128)} %constant.48.clone.four), custom_call_target="tpu_custom_call" | custom-call | tf_op jit(solution)/shard_map/modes/pallas_call | solution.py:386
  24.6 8.8 %collective-permute-start.1 = (f32[2,16,128]{2,1,0:T(8,128)}, f32[2,16,128]{2,1,0:T(8,128)S(1)}, u32[]{:S(2)}, u32[]{:S(2)}) collective-permute-start(f32[2,16,128]{2,1,0:T(8,128)} %get-tuple-element.9.own), channel_id=1, source_target_pairs={{0,126},{126,0},{1,127},{127,1},{2,124},{124,2},{3,125},{125,3},{8... | collective-permute-start | bytes 49160 | tf_op jit(solution)/shard_map/ppermute | solution.py:393
  33.4 1.9 %collective-permute-start = (f32[2,16,128]{2,1,0:T(8,128)}, f32[2,16,128]{2,1,0:T(8,128)S(1)}, u32[]{:S(2)}, u32[]{:S(2)}) collective-permute-start(f32[2,16,128]{2,1,0:T(8,128)} %get-tuple-element.9.own), channel_id=1, source_target_pairs={{0,6},{6,0},{1,7},{7,1},{2,4},{4,2},{3,5},{5,3},{8,14},{14,8},{9,1... | collective-permute-start | bytes 49160 | tf_op jit(solution)/shard_map/ppermute | solution.py:394
  35.3 0.0 collective-permute-done.1.next_half
  35.3 0.0 copy-start.1
  35.3 4.0 %collective-permute-done.plane_half = f32[2,16,128]{2,1,0:T(8,128)S(1)} collective-permute-done((f32[2,16,128]{2,1,0:T(8,128)}, f32[2,16,128]{2,1,0:T(8,128)S(1)}, u32[]{:S(2)}, u32[]{:S(2)}) %collective-permute-start) | collective-permute-done | bytes 16416 | tf_op jit(solution)/shard_map/ppermute | solution.py:394
  39.3 0.0 copy-done.1
  39.3 0.0 copy-start.2
  39.3 0.6 copy-done.2
  39.9 20.4 %force.2 = f32[4,8,128]{2,1,0:T(8,128)} custom-call(s32[3]{0:T(128)} %pad_add_fusion.place, f32[2,16,128]{2,1,0:T(8,128)} %get-tuple-element.9.own, f32[2,16,128]{2,1,0:T(8,128)} %copy-done.2, f32[2,16,128]{2,1,0:T(8,128)} %copy-done.1, f32[2,128]{1,0:T(2,128)} %embed.1, f32[8,128]{1,0:T(8,128)} %radial_one.1, f32[8,128]{1,0:T(8,128)} %radial_two.1, ...), custom_call_target="tpu_custom_call" | custom-call | tf_op jit(solution)/shard_map/force/pallas_call | solution.py:396
  60.3 0.0 copy-start.3
  60.3 5.1 %all-to-all-start.1 = ((f32[4,8,128]{2,1,0:T(8,128)}), f32[4,8,128]{2,1,0:T(8,128)S(1)}, u32[]{:S(2)}, u32[]{:S(2)}) async-start(f32[4,8,128]{2,1,0:T(8,128)} %force.2), calls=%async_computation.1 | async-start | bytes 32768 | tf_op jit(solution)/shard_map/all_to_all | solution.py:419
  65.4 0.0 copy-done.3
  65.4 0.6 copy.22
  66.0 2.5 %all-to-all-done.1.got = f32[4,8,128]{2,1,0:T(8,128)S(1)} async-done(((f32[4,8,128]{2,1,0:T(8,128)}), f32[4,8,128]{2,1,0:T(8,128)S(1)}, u32[]{:S(2)}, u32[]{:S(2)}) %all-to-all-start.1) | async-done | bytes 16416 | tf_op jit(solution)/shard_map/all_to_all | solution.py:419
  68.5 0.6 copy-done
  69.1 1.3 %finish.1 = (f32[4,3,64]{2,1,0:T(4,128)}, f32[4,3,64]{2,1,0:T(4,128)}) custom-call(s32[3]{0:T(128)} %pad_add_fusion.place, f32[4,8,128]{2,1,0:T(8,128)} %copy-done, f32[4,3,64]{2,1,0:T(4,128)} %get-tuple-element.10.mid), custom_call_target="tpu_custom_call" | custom-call | tf_op jit(solution)/shard_map/finish/pallas_call | solution.py:420
  70.5 1.3 %copy.23 = f32[4,3,64]{2,0,1:T(4,128)} copy(f32[4,3,64]{2,1,0:T(4,128)} %get-tuple-element.14) | data formatting | bytes 6144
  71.8 0.0 copy-done.4
  71.8 0.6 copy.24
  (2 shorter events, 0.0 us)
Async XLA Ops:
  0.7 0.7 copy-start.5
  1.4 0.7 copy-start.6
  2.0 0.7 copy-start.7
  24.6 10.7 %collective-permute-start.1 = (f32[2,16,128]{2,1,0:T(8,128)}, f32[2,16,128]{2,1,0:T(8,128)S(1)}, u32[]{:S(2)}, u32[]{:S(2)}) collective-permute-start(f32[2,16,128]{2,1,0:T(8,128)} %get-tuple-element.9.own), channel_id=1, source_target_pairs={{0,126},{126,0},{1,127},{127,1},{2,124},{124,2},{3,125},{125,3},{8... | collective-permute-start | bytes 49160 | tf_op jit(solution)/shard_map/ppermute | solution.py:393
  33.4 5.9 %collective-permute-start = (f32[2,16,128]{2,1,0:T(8,128)}, f32[2,16,128]{2,1,0:T(8,128)S(1)}, u32[]{:S(2)}, u32[]{:S(2)}) collective-permute-start(f32[2,16,128]{2,1,0:T(8,128)} %get-tuple-element.9.own), channel_id=1, source_target_pairs={{0,6},{6,0},{1,7},{7,1},{2,4},{4,2},{3,5},{5,3},{8,14},{14,8},{9,1... | collective-permute-start | bytes 49160 | tf_op jit(solution)/shard_map/ppermute | solution.py:394
  35.3 4.0 %copy-start.1 = (f32[2,16,128]{2,1,0:T(8,128)}, f32[2,16,128]{2,1,0:T(8,128)S(1)}, u32[]{:S(2)}) copy-start(f32[2,16,128]{2,1,0:T(8,128)S(1)} %collective-permute-done.1.next_half) | copy-start | bytes 49156
  39.3 0.6 copy-start.2
  60.3 5.1 %copy-start.3 = (f32[4,3,64]{2,1,0:T(4,128)S(1)}, f32[4,3,64]{2,1,0:T(4,128)}, u32[]{:S(2)}) copy-start(f32[4,3,64]{2,1,0:T(4,128)} %get-tuple-element.13) | copy-start | bytes 9220
  60.3 8.2 %all-to-all-start.1 = ((f32[4,8,128]{2,1,0:T(8,128)}), f32[4,8,128]{2,1,0:T(8,128)S(1)}, u32[]{:S(2)}, u32[]{:S(2)}) async-start(f32[4,8,128]{2,1,0:T(8,128)} %force.2), calls=%async_computation.1 | async-start | bytes 32768 | tf_op jit(solution)/shard_map/all_to_all | solution.py:419
  68.5 0.6 copy-start
  70.5 1.3 %copy-start.4 = (f32[4,3,64]{2,1,0:T(4,128)S(1)}, f32[4,3,64]{2,1,0:T(4,128)}, u32[]{:S(2)}) copy-start(f32[4,3,64]{2,1,0:T(4,128)} %get-tuple-element.15) | copy-start | bytes 9220

commit v2 on v1

v2 whole, which is shorter than its diff:
```python
import numpy as np

import jax
import jax.numpy as jnp
from jax import lax
from jax.experimental import pallas as pl
from jax.experimental.pallas import tpu as pltpu
from jax.sharding import PartitionSpec as P


F32 = jnp.float32
BF16 = jnp.bfloat16
BEADS = 16
TILES = 6
ROOT3 = float(np.sqrt(3.0))
VM = pl.BlockSpec(memory_space=pltpu.VMEM)
SM = pl.BlockSpec(memory_space=pltpu.SMEM)
RATES = 0.25 * 16.0 ** (np.arange(8) / 7.0)


def propagators():
    n = BEADS
    b = np.arange(n)
    phase = 2.0 * np.pi * np.outer(b, b) / n
    matrix = np.where(b[None] < n // 2, np.cos(phase), np.sin(phase)) * np.sqrt(2.0 / n)
    matrix[:, n // 2] = np.where(b % 2 == 0, 1.0, -1.0) / np.sqrt(n)
    matrix[:, 0] = 1.0 / np.sqrt(n)
    w = 1.5 * np.sin(np.pi * b / n)
    drift = np.where(b == 0, 1.0, np.sin(w) / np.where(b == 0, 1.0, w))
    return [(matrix * d) @ matrix.T for d in (np.cos(w), drift, w * np.sin(w))]


def mode_tables():
    cosine, drift, stiff = propagators()
    one = np.zeros((BEADS, 16, 64), np.float32)
    four = np.zeros((4, 64, 64), np.float32)
    for bead in range(BEADS):
        for src in range(BEADS):
            for c in range(3):
                col = (src // 4) * 16 + c * 4 + src % 4
                one[bead, c, col] = cosine[bead, src]
                one[bead, 8 + c, col] = drift[bead, src]
                row = c * 4 + bead % 4
                four[bead // 4, row, col] = cosine[bead, src]
                four[bead // 4, 16 + row, col] = drift[bead, src]
                four[bead // 4, 32 + row, col] = cosine[bead, src]
                four[bead // 4, 48 + row, col] = stiff[bead, src]
    return one, four

def split(x):
    high = x.astype(BF16)
    return high, (x - high.astype(F32)).astype(BF16)


def dot(a, b):
    return lax.dot_general(a, b, (((1,), (0,)), ((), ())), preferred_element_type=F32)


def dot_t(a, b):
    return lax.dot_general(a, b, (((1,), (1,)), ((), ())), preferred_element_type=F32)


def dot3(a, b):
    return dot(a[0], b[0]) + (dot(a[0], b[1]) + dot(a[1], b[0]))


def lanes(rows):
    return lax.broadcasted_iota(jnp.int32, (rows, 128), 1)


def turn(x):
    return pltpu.roll(x, 64, 1)


def exact(a, b):
    return jnp.dot(a, b, precision=lax.Precision.HIGHEST, preferred_element_type=F32)


def pick(y):
    return (y % 4) ^ (2 * (y // 4))


def pack_kernel(pos, mom, force, species, nbr, counts, ghost, out):
    raw = [jnp.concatenate([pos[c], mom[c] + 0.5 * force[c]], axis=1) for c in range(3)]
    kind = species[...].astype(F32)
    ghosts = ghost[0].astype(F32)
    last = jnp.concatenate([ghosts[0:1], ghosts[1:2], jnp.zeros((1, 96), F32)], axis=1)
    for bead in range(4):
        e = nbr[bead].astype(F32)
        rows = raw + [
            jnp.concatenate([e[0:1], e[1:2]], axis=1),
            jnp.concatenate([e[2:3], e[3:4]], axis=1),
            jnp.concatenate([counts[bead : bead + 1].astype(F32), kind], axis=1),
            last,
        ]
        block = jnp.concatenate(rows, axis=0)
        for r in range(4):
            for y in range(8):
                if pick(y) == bead:
                    out[r * 8 + y] = block


def modes_kernel(place, got, one, packed, own):
    r, side, local = place[0], place[1], place[2]
    low = lanes(8) < 64
    wide = jnp.concatenate(
        [jnp.concatenate([got[s * 8 + d] for s in range(4)], axis=0) for d in range(8)], axis=1
    )
    parts = exact(one[4 * r + local], wide)
    row = lax.broadcasted_iota(jnp.int32, (8, 128), 0)
    for t in range(4):
        info_even = got[r * 8 + 2 * t][8:16]
        info_odd = got[r * 8 + 2 * t + 1][8:16]
        left = jnp.where(low, info_even, turn(info_odd))
        right = jnp.where(low, turn(info_even), info_odd)
        kind = right[6:7]
        even, odd = parts[:, 256 * t : 256 * t + 128], parts[:, 256 * t + 128 : 256 * t + 256]
        cos_part = jnp.where(low, even[0:8], turn(odd[0:8]))
        drift_part = jnp.where(low, turn(even[8:16]), odd[8:16])
        coords = cos_part + drift_part / (1.0 + 15.0 * kind)
        packed[t, 0:8] = jnp.where(row == 3, jnp.broadcast_to(kind, (8, 128)), coords)
        packed[t, 8:12] = left[4:8]
        packed[t, 12:16] = right[4:8]
    own[...] = packed[pl.ds(2 * side, 2)]


def rates():
    row = lax.broadcasted_iota(jnp.int32, (8, 128), 0)
    rate = jnp.zeros((8, 128), F32)
    for n in range(8):
        rate = jnp.where(row == n, float(RATES[n]), rate)
    return rate


def sigmoid(v):
    return 1.0 / (1.0 + jnp.exp(-v))


def layer_one(pk, tiles, weights, hot, ys, gp, mom_one, slope_one, u_two):
    w_one_cat, mix1_t, prj_t, base_col, step_col = weights
    low = lanes(8) < 64
    low1 = lanes(1) < 64
    head = lanes(1) < 16
    rate = rates()
    spot = lax.broadcasted_iota(jnp.int32, (256, 128), 0).astype(F32)
    ghost_spot = lax.broadcasted_iota(jnp.int32, (32, 128), 0).astype(F32) + 64.0
    for t in tiles:
        here = pk[t + 1, 0:8]
        info = pk[t + 1, 8:16]
        beside = jnp.where(low, pk[t + 2, 0:8], pk[t, 0:8])
        wide = jnp.concatenate([here, beside], axis=1)
        a = wide.astype(BF16).astype(F32)
        b = (wide - a).astype(BF16).astype(F32)
        c = (wide - a - b).astype(BF16).astype(F32)
        parts = jnp.concatenate([a, b, c, jnp.zeros((8, 256), F32)], axis=0).astype(BF16)
        g_prev, g_here, g_next = pk[t, 11:12], info[3:4], pk[t + 2, 11:12]
        table = jnp.concatenate(
            [
                jnp.where(head, turn(g_prev) + 192.0, turn(g_here) + 64.0),
                jnp.where(head, g_here, g_next + 128.0),
                jnp.zeros((14, 128), F32),
            ],
            axis=0,
        )[:, 0:32].astype(BF16)
        count = info[2:3]
        sums = [None] * 9
        for k, row in enumerate((0, 4, 1, 5)):
            e = info[row : row + 1]
            hit = jnp.where(ghost_spot == e, 1.0, 0.0).astype(BF16)
            far = dot(table, hit)
            n = jnp.where(
                e < 64.0, e + jnp.where(low1, 0.0, 64.0), jnp.where(low1, far[0:1], far[1:2])
            )
            one_hot = jnp.where(spot == n, 1.0, 0.0).astype(BF16)
            hot[t, :, k * 128 : (k + 1) * 128] = one_hot
            got = dot(parts, one_hot)
            there = got[0:8] + (got[8:16] + got[16:24])
            off = there - here
            x, y, z = off[0:1], off[1:2], off[2:3]
            q = x * x + y * y + z * z
            live = jnp.where(count > float(k), 0.25, 0.0)
            g = jnp.exp(-rate * q) * live
            both = jnp.concatenate([g, g * there[3:4]], axis=0)
            harmonic = [
                None, x, y, z, ROOT3 * x * y, ROOT3 * y * z, 0.5 * (3.0 * z * z - q), ROOT3 * x * z,
                (0.5 * ROOT3) * (x * x - y * y),
            ]
            gp[t, k] = both
            ys[t, k] = jnp.concatenate(harmonic[1:9], axis=0)
            for l in range(9):
                term = both if l == 0 else harmonic[l] * both
                sums[l] = term if sums[l] is None else sums[l] + term
        high, lo = split(jnp.concatenate(sums, axis=1))
        moments = dot(w_one_cat, jnp.concatenate([high, lo, high], axis=0))
        m = [moments[:, l * 128 : (l + 1) * 128] for l in range(9)]
        for l in range(9):
            mom_one[t, l] = m[l]
        inv = jnp.concatenate(
            [m[0] * m[0], sum(m[l] * m[l] for l in (1, 2, 3)), sum(m[l] * m[l] for l in range(4, 9))],
            axis=0,
        )
        v = dot3(mix1_t, split(inv))
        sig = sigmoid(v)
        slope_one[t] = sig * (1.0 + v * (1.0 - sig))
        h = base_col + here[3:4] * step_col + v * sig
        u_two[t] = dot3(prj_t, split(h))


def forms_kernel(
    sent, one, four, embed, radial_one, radial_two, mix_one, mix_two, proj, readout,
    one_out, four_out, mix_back, mix_fwd, prj_all, columns, first_cat, first_parts, second_cat, second_parts,
):
    del sent

    def column(row):
        return jnp.broadcast_to(row, (128, 128)).T

    one_out[...] = one[...]
    four_out[...] = four[...]
    columns[0] = column(embed[0:1])
    columns[1] = column(embed[1:2] - embed[0:1])
    columns[2] = column(readout[1:2])
    columns[3] = column(readout[0:1] + readout[1:2])
    for n, mix in enumerate((mix_one, mix_two)):
        mix_back[2 * n], mix_back[2 * n + 1] = split(mix[...])
        mix_fwd[2 * n], mix_fwd[2 * n + 1] = split(mix[...].T)
    prj_all[0], prj_all[1] = split(proj[...])
    prj_all[2], prj_all[3] = split(proj[...].T)
    base, step = embed[0:1], embed[1:2] - embed[0:1]
    high, lo = split(jnp.concatenate([radial_one[...] * base, radial_one[...] * step], axis=0))
    first_parts[0], first_parts[1] = high, lo
    first_cat[...] = jnp.concatenate([high, high, lo], axis=0).astype(F32).T.astype(BF16)
    high, lo = split(radial_two[...])
    second_parts[0], second_parts[1] = high, lo
    high, lo = high.astype(F32), lo.astype(F32)
    second_cat[...] = jnp.concatenate([high, high, lo, jnp.zeros((8, 128), F32)], axis=0).T.astype(BF16)


def plane_kernel(
    place, packed, got, four, mix_fwd, prj_all, columns, first_cat,
    pos_out, mom_out, hot, ys, gp, mom_one, slope_one, u_two,
    pk,
):
    r, side, y = place[0], place[1], place[3]

    first = 2 * (1 - side)
    for t in range(2):
        pk[t] = packed[0]
        pk[6 + t] = packed[3]
    pk[pl.ds(first + 1, 4)] = packed[...]
    weights = (first_cat[...], (mix_fwd[0], mix_fwd[1]), (prj_all[2], prj_all[3]), columns[0], columns[1])
    start = 3 * (1 - side)
    layer_one(pk, [start + i for i in range(3)], weights, hot, ys, gp, mom_one, slope_one, u_two)

    own = exact(four[r], jnp.concatenate([got[s * 8 + y] for s in range(4)], axis=0))
    mass = 1.0 + 15.0 * turn(got[r * 8 + y][8:16])[6:7]
    coords = own[0:16] + turn(own[16:32]) / mass
    moment = turn(own[32:48]) - mass * own[48:64]
    for c in range(3):
        pos_out[c] = coords[4 * c : 4 * c + 4, 0:64]
        mom_out[c] = moment[4 * c : 4 * c + 4, 0:64]


def force_kernel(
    place, packed, across, hot_in, ys_in, gp_in, mom_in, slope_in, u_in, mix_back, mix_fwd, prj_all, columns,
    first_cat, first_parts, second_cat, second_parts,
    out, hot, ys, gp, mom_one, slope_one, u_two,
    pk, du_two, tk, gk, rk, v_one, v_two, dvec,
):
    side = place[1]
    low = lanes(8) < 64
    low1 = lanes(1) < 64
    low_wide = lanes(128) < 64
    first = 2 * (1 - side)
    other = 4 * side
    pk[0] = across[0]
    pk[7] = across[1]
    pk[pl.ds(first + 1, 4)] = packed[...]
    pk[pl.ds(other + 1, 2)] = across[...]
    w_one2 = (first_parts[0], first_parts[1])
    w_two2 = (second_parts[0], second_parts[1])
    w_two_cat = second_cat[...]
    weights = (first_cat[...], (mix_fwd[0], mix_fwd[1]), (prj_all[2], prj_all[3]), columns[0], columns[1])
    start = 3 * side
    layer_one(pk, [start + i for i in range(3)], weights, hot, ys, gp, mom_one, slope_one, u_two)
    rate = rates()
    pairs = [(i, j) for i in range(4) for j in range(i, 4)]

    du_two[...] = jnp.zeros_like(du_two)

    def second(t, _):
        near = u_two[t]
        beside = jnp.where(low_wide, u_two[t + 1], u_two[t - 1])
        high, lo = split(jnp.concatenate([near, beside], axis=1))
        parts = jnp.concatenate([high, lo], axis=0)
        for k in range(4):
            got = dot(parts, hot[t, :, k * 128 : (k + 1) * 128])
            nodes = got[0:128] + got[128:256]
            g = gp[t, k, 0:8]
            gh = g.astype(BF16).astype(F32)
            rows = jnp.concatenate([gh, g - gh, gh, jnp.zeros((8, 128), F32)], axis=0).astype(BF16)
            weight = dot(w_two_cat, rows)
            gk[k] = nodes
            rk[k] = weight
            tk[k] = nodes * weight
        edge = [[ys[t, k, c : c + 1] for c in range(3)] for k in range(4)]
        scalar = {}
        for i, j in pairs:
            scalar[i, j] = scalar[j, i] = sum(edge[i][c] * edge[j][c] for c in range(3))
        legendre = {}
        for i, j in pairs:
            legendre[i, j] = legendre[j, i] = 1.5 * scalar[i, j] * scalar[i, j] - 0.5 * scalar[i, i] * scalar[j, j]
        total = (tk[0] + tk[1]) + (tk[2] + tk[3])
        inv1 = inv2 = None
        for i in range(4):
            va = sum(scalar[i, j] * tk[j] for j in range(4))
            vb = sum(legendre[i, j] * tk[j] for j in range(4))
            v_one[i], v_two[i] = va, vb
            inv1 = va * tk[i] if inv1 is None else inv1 + va * tk[i]
            inv2 = vb * tk[i] if inv2 is None else inv2 + vb * tk[i]
        inv = jnp.concatenate([total * total, inv1, inv2], axis=0)
        v = dot3((mix_fwd[2], mix_fwd[3]), split(inv))
        sig = sigmoid(v)
        dv = columns[2] * (sig * (1.0 + v * (1.0 - sig)))
        dinv = 2.0 * dot3((mix_back[2], mix_back[3]), split(dv))
        d0, d1, d2 = dinv[0:128] * total, dinv[128:256], dinv[256:384]
        pull, bend = {}, {}
        for i in range(4):
            wa, wb = d1 * tk[i], d2 * tk[i]
            for j in range(i, 4):
                pull[i, j] = pull[j, i] = jnp.sum(wa * tk[j], axis=0, keepdims=True)
                bend[i, j] = bend[j, i] = jnp.sum(wb * tk[j], axis=0, keepdims=True)
        back = None
        for k in range(4):
            dt = d0 + d1 * v_one[k] + d2 * v_two[k]
            g = gp[t, k, 0:8]
            dg = dot3(w_two2, split(dt * gk[k]))
            dq = 0.5 * pull[k, k] + bend[k, k] * scalar[k, k] - jnp.sum(rate * g * dg, axis=0, keepdims=True)
            d = [None] * 3
            for j in range(4):
                if j != k:
                    dq = dq - 0.5 * bend[k, j] * scalar[j, j]
                    tie = pull[k, j] + 3.0 * bend[k, j] * scalar[k, j]
                    d = [tie * edge[j][c] if d[c] is None else d[c] + tie * edge[j][c] for c in range(3)]
            d = [d[c] + 2.0 * dq * edge[k][c] for c in range(3)]
            dvec[t, k] = jnp.concatenate(d + [jnp.zeros((5, 128), F32)], axis=0)
            high, lo = split(dt * rk[k])
            term = dot_t(jnp.concatenate([high, lo], axis=0), hot[t, :, k * 128 : (k + 1) * 128])
            back = term if back is None else back + term
        back = back[0:128] + back[128:256]
        du_two[t] += back[:, 0:128]
        aside = back[:, 128:256]
        du_two[t + 1] += jnp.where(low_wide, aside, 0.0)
        du_two[t - 1] += jnp.where(low_wide, 0.0, aside)
        return 0

    for t in range(1, TILES - 1):
        second(t, 0)

    def third(du, slope, mom, gs, harmonics, pushes, spots):
        dh = columns[3] + dot3((prj_all[0], prj_all[1]), split(du))
        dinv = 2.0 * dot3((mix_back[0], mix_back[1]), split(dh * slope))
        parts = []
        for l in range(9):
            part = 0 if l == 0 else 1 if l < 4 else 2
            parts.append(mom(l) * dinv[part * 128 : (part + 1) * 128])
        dm = dot3(w_one2, split(jnp.concatenate(parts, axis=1)))
        dm = [dm[:, l * 128 : (l + 1) * 128] for l in range(9)]
        rate2 = jnp.concatenate([rate, rate], axis=0)
        back = None
        centre = None
        for k in range(4):
            g, yk, push = gs(k), harmonics(k), pushes(k)
            dg = dm[0]
            dys = []
            for l in range(1, 9):
                dg = dg + yk[l - 1 : l] * dm[l]
                dys.append(jnp.sum(g * dm[l], axis=0, keepdims=True))
            dq = -jnp.sum(rate2 * g * dg, axis=0, keepdims=True)
            x, y, z = yk[0:1], yk[1:2], yk[2:3]
            e1, e2, e3, e4, e5, e6, e7, e8 = dys
            dx = e1 + ROOT3 * (y * e4 + z * e7 + x * e8) + x * (2.0 * dq - e6)
            dy = e2 + ROOT3 * (x * e4 + z * e5 - y * e8) + y * (2.0 * dq - e6)
            dz = e3 + ROOT3 * (y * e5 + x * e7) + 2.0 * z * (dq + e6)
            d = push + jnp.concatenate([dx, dy, dz, jnp.zeros((5, 128), F32)], axis=0)
            centre = d if centre is None else centre + d
            d_high = d.astype(BF16).astype(F32)
            rows = jnp.concatenate([d_high, d - d_high], axis=0).astype(BF16)
            term = dot_t(rows, spots(k))
            back = term if back is None else back + term
        return back[0:8] + back[8:16], centre

    def own_tile(t):
        return third(
            du_two[t], slope_one[t], lambda l: mom_one[t, l], lambda k: gp[t, k], lambda k: ys[t, k],
            lambda k: dvec[t, k], lambda k: hot[t, :, k * 128 : (k + 1) * 128],
        )

    def mixed(ref, *at):
        right, left = ref[(4,) + at], ref[(1,) + at]
        keep = lax.broadcasted_iota(jnp.int32, right.shape, 1) < 64
        return jnp.where(keep, right, left)

    def mixed_spots(k):
        at = (slice(128, 256), slice(k * 128, (k + 1) * 128))
        keep = lanes(128) < 64
        return jnp.where(keep, hot[(4,) + at].astype(F32), hot[(1,) + at].astype(F32)).astype(BF16)

    back2, centre2 = own_tile(2)
    back3, centre3 = own_tile(3)
    rim, _ = third(
        mixed(du_two), mixed(slope_one), lambda l: mixed(mom_one, l), lambda k: mixed(gp, k), lambda k: mixed(ys, k),
        lambda k: mixed(dvec, k), mixed_spots,
    )
    f2 = centre2 - back2[:, 0:128] - jnp.where(low, rim, back3[:, 128:256])
    f3 = centre3 - back3[:, 0:128] - jnp.where(low, back2[:, 128:256], rim)
    for t, f in enumerate((f2, f3)):
        out[2 * t] = f
        out[2 * t + 1] = turn(f)


def finish_kernel(place, got, mid, force_out, mom_out):
    side = place[1]
    for b in range(4):
        f = got[b ^ (2 * side)]
        for c in range(3):
            force_out[c, b : b + 1] = f[c : c + 1, 0:64]
    mom_out[...] = mid[...] + 0.5 * force_out[...]


def shape(*dims):
    return jax.ShapeDtypeStruct(dims, F32)


def room(mib):
    return pltpu.CompilerParams(vmem_limit_bytes=mib << 20)


def near(*dims, dtype=F32):
    return pltpu.VMEM(dims, dtype)


def far(x):
    return pltpu.with_memory_space_constraint(x, pltpu.HBM)


def keep(x):
    return pltpu.with_memory_space_constraint(x, pltpu.VMEM)


def on_device(
    positions, momenta, forces, species, neighbours, counts, ghost_rows,
    embed, radial_one, radial_two, mix_one, mix_two, projection, readout,
):
    count = lax.axis_size("space")
    r = lax.axis_index("bead")
    s = lax.axis_index("space")
    y = s & 7
    side = y >> 2
    place = jnp.stack([r, side, (y & 3) ^ (2 * side), y]).astype(jnp.int32)
    both = ("bead", "space")
    planes = [[b * count + z * 8 + i for b in range(4) for i in range(8)] for z in range(count // 8)]
    quads = [[b * count + h * 4 + i for i in range(4)] for b in range(4) for h in range(count // 4)]
    beside = []
    for b in range(4):
        for z in range(count // 8):
            for i in range(4):
                here = b * count + z * 8 + i
                back = b * count + (z * 8 - 4) % count + (i ^ 2)
                beside += [(here, back), (back, here)]

    turned = [jnp.transpose(x, (1, 0, 2)) for x in (positions, momenta, forces)]
    sent = pl.pallas_call(
        pack_kernel, out_shape=shape(32, 16, 128), in_specs=[VM] * 7, out_specs=VM, name="pack",
    )(*[far(x) for x in (*turned, species[None, :], neighbours, counts, ghost_rows)])
    got = keep(lax.all_to_all(sent, both, 0, 0, axis_index_groups=planes))
    one, four = mode_tables()
    one, four, *forms = pl.pallas_call(
        forms_kernel,
        out_shape=(
            near(BEADS, 16, 64), near(4, 64, 64), near(4, 384, 128, dtype=BF16), near(4, 128, 384, dtype=BF16),
            near(4, 128, 128, dtype=BF16), near(4, 128, 128), near(128, 48, dtype=BF16),
            near(2, 16, 128, dtype=BF16), near(128, 32, dtype=BF16), near(2, 8, 128, dtype=BF16),
        ),
        in_specs=[pl.BlockSpec(memory_space=pl.ANY)] + [VM] * 9,
        out_specs=(VM,) * 10,
        compiler_params=room(8),
        cost_estimate=pl.CostEstimate(flops=2_000_000_000, bytes_accessed=4_000_000, transcendentals=0),
        name="forms",
    )(*[far(x) for x in (
        sent, jnp.asarray(one), jnp.asarray(four), embed, radial_one, radial_two, mix_one, mix_two, projection, readout,
    )])
    mix_back, mix_fwd, prj_all, columns, first_cat, first_parts, second_cat, second_parts = forms
    packed, own = pl.pallas_call(
        modes_kernel,
        out_shape=(near(4, 16, 128), near(2, 16, 128)),
        in_specs=[SM] + [VM] * 2,
        out_specs=(VM,) * 2,
        compiler_params=room(16),
        name="modes",
    )(place, got, one)
    across = keep(lax.ppermute(own, both, beside))
    saved = (
        near(TILES, 256, 512, dtype=BF16),
        near(TILES, 4, 8, 128),
        near(TILES, 4, 16, 128),
        near(TILES, 9, 128, 128),
        near(TILES, 128, 128),
        near(TILES, 128, 128),
    )
    res = pl.pallas_call(
        plane_kernel,
        out_shape=(shape(3, 4, 64), near(3, 4, 64)) + saved,
        in_specs=[SM] + [VM] * 7,
        out_specs=(VM,) * 8,
        scratch_shapes=[near(8, 16, 128)],
        compiler_params=room(24),
        cost_estimate=pl.CostEstimate(flops=4_000_000_000, bytes_accessed=8_000_000, transcendentals=0),
        name="plane",
    )(place, packed, got, four, mix_fwd, prj_all, columns, first_cat)
    positions_next, mid, kept = res[0], res[1], res[2:8]
    grad = pl.pallas_call(
        force_kernel,
        out_shape=(near(4, 8, 128),) + saved,
        in_specs=[SM] + [VM] * 16,
        out_specs=(VM,) * 7,
        scratch_shapes=[
            near(8, 16, 128),
            near(TILES, 128, 128),
            near(4, 128, 128),
            near(4, 128, 128),
            near(4, 128, 128),
            near(4, 128, 128),
            near(4, 128, 128),
            near(TILES, 4, 8, 128),
        ],
        input_output_aliases={3 + i: 1 + i for i in range(6)},
        compiler_params=room(24), name="force",
    )(place, packed, across, *kept, *forms)[0]
    back = keep(lax.all_to_all(grad, both, 0, 0, axis_index_groups=quads))
    forces_next, momenta_next = pl.pallas_call(
        finish_kernel,
        out_shape=(shape(3, 4, 64), shape(3, 4, 64)),
        in_specs=[SM] + [VM] * 2,
        out_specs=(VM, VM),
        compiler_params=room(8), name="finish",
    )(place, back, mid)
    return tuple(jnp.transpose(x, (1, 0, 2)) for x in (positions_next, momenta_next, forces_next))


def solution(mesh):
    spread = P("bead", None, "space")
    placed = (
        spread, spread, spread, P("space"), spread, P("bead", "space"), P("space", None, None),
    ) + (P(),) * 7
    return jax.shard_map(
        on_device, mesh=mesh, in_specs=placed, out_specs=(spread,) * 3, check_vma=False
    )
```

time: 73 us -> 55.3 us (0.76)
  blocking collectives: 17 us -> 5.9 us
  local copies, waits for them, and re-layouts: 6.38 us -> 0 us
  Pallas kernels: 25.4 us -> 20.6 us
  starting transfers between devices: 15.8 us -> 20.3 us
  waiting for transfers between devices: 6.49 us -> 7.37 us
    all_to_all x1, blocking collectives: 17 us -> 5.9 us  [on_device(): back = keep(lax.all_to_all(grad, both, 0, 0, axis_index_groups=quads))]
    unnamed x22 -> x0, local copies, waits for them, and re-layouts: 6.38 us -> none
    all_to_all x1, starting transfers between devices: 5.09 us -> 10.4 us  [on_device(): got = keep(lax.all_to_all(sent, both, 0, 0, axis_index_groups=planes))]
    all_to_all x1, waiting for transfers between devices: 2.53 us -> 7.36 us  [on_device(): got = keep(lax.all_to_all(sent, both, 0, 0, axis_index_groups=planes))]
    pallas_call x4 -> x6, Pallas kernels: 25.4 us -> 20.6 us  [the longest x1 11.3 us: on_device(): pl.pallas_call(force_kernel, out_shape=(near(4, 8, 128),) + saved, in_spe...]
    ppermute x2 -> x1, waiting for transfers between devices: 3.96 us -> 0.01 us  [on_device(): across = keep(lax.ppermute(own, both, beside))]
    ppermute x2 -> x1, starting transfers between devices: 10.7 us -> 9.94 us  [on_device(): across = keep(lax.ppermute(own, both, beside))]
  transfers between devices with their start and end apart: 3 -> 2, of which waited for: 2 -> 1; matrix products, arithmetic and copies ran while one was open for 1% -> 0% of each run, Pallas kernels for 0% -> 11%
where the time goes in v2:
time: 55.3 us; the launch traced here: 55 us
  Pallas kernels  20.6 us (37%)
  starting transfers between devices  20.3 us (37%)
  waiting for transfers between devices  7.37 us (13%)
  blocking collectives  5.9 us (11%)
  between operations  0.67 us (1%)
    pallas_call x1, Pallas kernels, on_device(): pl.pallas_call(force_kernel, out_shape=(near(4, 8, 128),) + saved, in_spe...  11.3 us
    all_to_all x1, starting transfers between devices, on_device(): got = keep(lax.all_to_all(sent, both, 0, 0, axis_index_groups=planes))  10.4 us
    ppermute x1, starting transfers between devices, on_device(): across = keep(lax.ppermute(own, both, beside))  9.94 us
    all_to_all x1, waiting for transfers between devices, on_device(): got = keep(lax.all_to_all(sent, both, 0, 0, axis_index_groups=planes))  7.36 us
    all_to_all x1, blocking collectives, on_device(): back = keep(lax.all_to_all(grad, both, 0, 0, axis_index_groups=quads))  5.9 us
    pallas_call x1, Pallas kernels, on_device(): pl.pallas_call(plane_kernel, out_shape=(shape(3, 4, 64), near(3, 4, 64))...  4.16 us
    pallas_call x1, Pallas kernels, on_device(): pl.pallas_call(forms_kernel, out_shape=(near(BEADS, 16, 64), near(4, 64,...  1.62 us
    pallas_call x1, Pallas kernels, on_device(): pl.pallas_call(pack_kernel, out_shape=shape(32, 16, 128), in_specs=[VM] *...  1.58 us
  transfers between devices with their start and end apart: 2, of which 1 were waited for; matrix products, arithmetic and copies ran while one was open for 0% of the time, Pallas kernels for 11%

profile of v2, /device:TPU:1, one launch (start us, length us, event | category | flops | bytes accessed | tf_op | source)
XLA Modules:
  0.0 55.0 jit_solution(4944872206315180294)
XLA Ops:
  0.6 1.6 %pack.1.sent = f32[32,16,128]{2,1,0:T(8,128)} custom-call(f32[3,4,64]{2,1,0:T(4,128)} %bitcast.11, f32[3,4,64]{2,1,0:T(4,128)} %bitcast.12, f32[3,4,64]{2,1,0:T(4,128)} %bitcast.13, s32[1,64]{1,0:T(1,128)} %bitcast.14, s32[4,4,64]{2,1,0:T(4,128)} %nbr.1, s32[4,64]{1,0:T(4,128)} %counts.1, s32[1,2,16]{2,1,0:T(2,128)} %ghost.1), custom_call_target="tpu_custom_call" | custom-call | tf_op jit(solution)/shard_map/pack/pallas_call | solution.py:473
  2.2 10.4 %all-to-all-start = ((f32[32,16,128]{2,1,0:T(8,128)}), f32[32,16,128]{2,1,0:T(8,128)S(1)}, u32[]{:S(2)}, u32[]{:S(2)}) async-start(f32[32,16,128]{2,1,0:T(8,128)} %pack.1.sent), calls=%async_computation | async-start | bytes 524288 | tf_op jit(solution)/shard_map/all_to_all | solution.py:476
  12.6 0.1 pad_add_fusion.place
  12.7 1.6 %forms.1 = (f32[16,16,64]{2,1,0:T(8,128)S(1)}, f32[4,64,64]{2,1,0:T(8,128)S(1)}, bf16[4,384,128]{2,1,0:T(8,128)(2,1)S(1)}, bf16[4,128,384]{2,1,0:T(8,128)(2,1)S(...) custom-call(f32[32,16,128]{2,1,0:T(8,128)} %pack.1.sent, ...), custom_call_target="tpu_custom_call" | custom-call | flops 2000000000 | bytes 4000000 | tf_op jit(solution)/shard_map/forms/pallas_call | solution.py:478
  14.3 7.4 %all-to-all-done.got = f32[32,16,128]{2,1,0:T(8,128)S(1)} async-done(((f32[32,16,128]{2,1,0:T(8,128)}), f32[32,16,128]{2,1,0:T(8,128)S(1)}, u32[]{:S(2)}, u32[]{:S(2)}) %all-to-all-start) | async-done | bytes 262176 | tf_op jit(solution)/shard_map/all_to_all | solution.py:476
  21.7 0.8 %modes.1 = (f32[4,16,128]{2,1,0:T(8,128)S(1)}, f32[2,16,128]{2,1,0:T(8,128)S(1)}) custom-call(s32[4]{0:T(128)S(1)} %pad_add_fusion.place, f32[32,16,128]{2,1,0:T(8,128)S(1)} %all-to-all-done.got, f32[16,16,64]{2,1,0:T(8,128)S(1)} %get-tuple-element.26.one), custom_call_target="tpu_custom_call" | custom-call | tf_op jit(solution)/shard_map/modes/pallas_call | solution.py:494
  22.5 9.9 %collective-permute-start = (f32[2,16,128]{2,1,0:T(8,128)S(1)}, f32[2,16,128]{2,1,0:T(8,128)S(1)}, u32[]{:S(2)}, u32[]{:S(2)}) collective-permute-start(f32[2,16,128]{2,1,0:T(8,128)S(1)} %get-tuple-element.34), channel_id=1, source_target_pairs={{0,126},{126,0},{1,127},{127,1},{2,124},{124,2},{3,125},{125,3},{8... | collective-permute-start | bytes 49160 | tf_op jit(solution)/shard_map/ppermute | solution.py:502
  32.4 4.2 %plane.1 = (f32[3,4,64]{2,1,0:T(4,128)}, f32[3,4,64]{2,1,0:T(4,128)S(1)}, bf16[6,256,512]{2,1,0:T(8,128)(2,1)S(1)}, f32[6,4,8,128]{3,2,1,0:T(8,128)S(1)}, f32[6,...) custom-call(s32[4]{0:T(128)S(1)} %pad_add_fusion.place, ...), custom_call_target="tpu_custom_call" | custom-call | flops 4000000000 | bytes 8000000 | tf_op jit(solution)/shard_map/plane/pallas_call | solution.py:511
  36.6 0.0 collective-permute-done.across
  36.6 11.3 %force.1 = (f32[4,8,128]{2,1,0:T(8,128)S(1)}, bf16[6,256,512]{2,1,0:T(8,128)(2,1)S(1)}, f32[6,4,8,128]{3,2,1,0:T(8,128)S(1)}, f32[6,4,16,128]{3,2,1,0:T(8,128)S(...) custom-call(s32[4]{0:T(128)S(1)} %pad_add_fusion.place, ...), custom_call_target="tpu_custom_call", output_to_operand_aliasing={{1}: (3, {}), {2}: (4, {}), {3}: (5, {}), {4}: (6, {}), {5}... | custom-call | tf_op jit(solution)/shard_map/force/pallas_call | solution.py:522
  47.9 5.9 %all_to_all.10.got = f32[4,8,128]{2,1,0:T(8,128)S(1)} all-to-all(f32[4,8,128]{2,1,0:T(8,128)S(1)} %get-tuple-element.45), channel_id=1, replica_groups={{0,1,2,3},{4,5,6,7},{8,9,10,11},{12,13,14,15},{16,17,18,19},{20,21,22,2..., dimensions={0} | all-to-all | bytes 32768 | tf_op jit(solution)/shard_map/all_to_all | solution.py:540
  53.8 1.2 %finish.1 = (f32[3,4,64]{2,1,0:T(4,128)}, f32[3,4,64]{2,1,0:T(4,128)}) custom-call(s32[4]{0:T(128)S(1)} %pad_add_fusion.place, f32[4,8,128]{2,1,0:T(8,128)S(1)} %all_to_all.10.got, f32[3,4,64]{2,1,0:T(4,128)S(1)} %get-tuple-element.46.mid), custom_call_target="tpu_custom_call" | custom-call | tf_op jit(solution)/shard_map/finish/pallas_call | solution.py:541
Async XLA Ops:
  2.2 19.4 %all-to-all-start = ((f32[32,16,128]{2,1,0:T(8,128)}), f32[32,16,128]{2,1,0:T(8,128)S(1)}, u32[]{:S(2)}, u32[]{:S(2)}) async-start(f32[32,16,128]{2,1,0:T(8,128)} %pack.1.sent), calls=%async_computation | async-start | bytes 524288 | tf_op jit(solution)/shard_map/all_to_all | solution.py:476
  22.5 14.1 %collective-permute-start = (f32[2,16,128]{2,1,0:T(8,128)S(1)}, f32[2,16,128]{2,1,0:T(8,128)S(1)}, u32[]{:S(2)}, u32[]{:S(2)}) collective-permute-start(f32[2,16,128]{2,1,0:T(8,128)S(1)} %get-tuple-element.34), channel_id=1, source_target_pairs={{0,126},{126,0},{1,127},{127,1},{2,124},{124,2},{3,125},{125,3},{8... | collective-permute-start | bytes 49160 | tf_op jit(solution)/shard_map/ppermute | solution.py:502

commit v3 on v2

v3 whole, which is shorter than its diff:
```python
import numpy as np

import jax
import jax.numpy as jnp
from jax import lax
from jax.experimental import pallas as pl
from jax.experimental.pallas import tpu as pltpu
from jax.sharding import PartitionSpec as P


F32 = jnp.float32
BF16 = jnp.bfloat16
BEADS = 16
TILES = 6
ROOT3 = float(np.sqrt(3.0))
VM = pl.BlockSpec(memory_space=pltpu.VMEM)
RATES = 0.25 * 16.0 ** (np.arange(8) / 7.0)


def propagators():
    n = BEADS
    b = np.arange(n)
    phase = 2.0 * np.pi * np.outer(b, b) / n
    matrix = np.where(b[None] < n // 2, np.cos(phase), np.sin(phase)) * np.sqrt(2.0 / n)
    matrix[:, n // 2] = np.where(b % 2 == 0, 1.0, -1.0) / np.sqrt(n)
    matrix[:, 0] = 1.0 / np.sqrt(n)
    w = 1.5 * np.sin(np.pi * b / n)
    drift = np.where(b == 0, 1.0, np.sin(w) / np.where(b == 0, 1.0, w))
    return [(matrix * d) @ matrix.T for d in (np.cos(w), drift, w * np.sin(w))]


def mode_tables():
    cosine, drift, stiff = propagators()
    rows = np.zeros((4, 4, 64, 16))
    for sender in range(4):
        for bead in range(BEADS):
            for c in range(3):
                for b in range(4):
                    for n, values in enumerate((cosine, drift, cosine, stiff)):
                        rows[sender, n, 4 * bead + c, 4 * c + b] = values[bead, 4 * sender + b]
    rows = rows.astype(np.float32).reshape(4, 2, 128, 16)
    one = rows.astype(BF16)
    two = (rows - one.astype(np.float32)).astype(BF16)
    three = (rows - one.astype(np.float32) - two.astype(np.float32)).astype(BF16)
    return np.concatenate([one, one, two, two, one, three], axis=-1)


def parts_of(x):
    one = x.astype(BF16)
    rest = x - one.astype(F32)
    two = rest.astype(BF16)
    three = (rest - two.astype(F32)).astype(BF16)
    return jnp.concatenate([one, two, one, two, three, one], axis=0)

def split(x):
    high = x.astype(BF16)
    return high, (x - high.astype(F32)).astype(BF16)


def dot(a, b):
    return lax.dot_general(a, b, (((1,), (0,)), ((), ())), preferred_element_type=F32)


def dot_t(a, b):
    return lax.dot_general(a, b, (((1,), (1,)), ((), ())), preferred_element_type=F32)


def dot3(a, b):
    return dot(a[0], b[0]) + (dot(a[0], b[1]) + dot(a[1], b[0]))


def lanes(rows):
    return lax.broadcasted_iota(jnp.int32, (rows, 128), 1)


def turn(x):
    return pltpu.roll(x, 64, 1)


def pick(y):
    return (y % 4) ^ (2 * (y // 4))


def whereabouts():
    s = lax.axis_index("space")
    return lax.axis_index("bead"), (s & 7) >> 2, s


def pack_kernel(table, pos, mom, force, species, nbr, counts, ghost, out):
    r, _, _ = whereabouts()
    low = lanes(64) < 64
    kind = species[...].astype(F32)
    mass = 1.0 + 15.0 * kind
    blank = jnp.zeros((4, 64), F32)
    coords = jnp.concatenate([pos[0], pos[1], pos[2], blank], axis=0)
    kicked = jnp.concatenate([mom[c] + 0.5 * force[c] for c in range(3)] + [blank], axis=0)
    moved = dot(table[r, 0], parts_of(jnp.concatenate([coords, kicked / mass], axis=1)))
    driven = dot(table[r, 1], parts_of(jnp.concatenate([mass * coords, kicked], axis=1)))
    shares = jnp.where(low, moved[0:64] + turn(moved[64:128]), driven[0:64] - turn(driven[64:128]))
    ghosts = ghost[0].astype(F32)
    last = jnp.concatenate([ghosts[0:1], ghosts[1:2], jnp.zeros((1, 96), F32)], axis=1)
    row = lax.broadcasted_iota(jnp.int32, (8, 128), 0)
    for bead in range(4):
        e = nbr[bead].astype(F32)
        info = jnp.concatenate(
            [
                jnp.zeros((3, 128), F32),
                jnp.concatenate([counts[bead : bead + 1].astype(F32), kind], axis=1),
                jnp.concatenate([e[0:1], e[1:2]], axis=1),
                jnp.concatenate([e[2:3], e[3:4]], axis=1),
                last,
                jnp.zeros((1, 128), F32),
            ],
            axis=0,
        )
        for to in range(4):
            n = (4 * to + bead) // 2
            share = shares[8 * n : 8 * n + 8]
            if bead % 2:
                share = pltpu.roll(share, 4, 0)
            block = jnp.where(row < 3, share, info)
            for y in range(8):
                if pick(y) == bead:
                    out[to * 8 + y] = block


def modes_kernel(got, packed, own, moment):
    r, side, _ = whereabouts()
    low = lanes(8) < 64
    row = lax.broadcasted_iota(jnp.int32, (8, 128), 0)
    moments = []
    for t in range(4):
        even, odd = (
            (got[d] + got[8 + d]) + (got[16 + d] + got[24 + d]) for d in (2 * t, 2 * t + 1)
        )
        info_even, info_odd = got[r * 8 + 2 * t], got[r * 8 + 2 * t + 1]
        left = jnp.where(low, info_even, turn(info_odd))
        right = jnp.where(low, turn(info_even), info_odd)
        coords = jnp.where(low, even, turn(odd))
        moments.append(jnp.where(low, turn(even), odd))
        packed[t, 0:8] = jnp.where(row < 3, coords, jnp.broadcast_to(right[3:4], (8, 128)))
        packed[t, 8:16] = jnp.where(row < 3, pltpu.roll(right, 5, 0), left)
    for t in range(2):
        moment[t] = jnp.where(side == 1, moments[2 + t], moments[t])
    own[...] = packed[pl.ds(2 * side, 2)]


ORDER = ((0, 0), (0, 1), (1, 0), (2, 0), (0, 2), (1, 1), (2, 1), (3, 0), (1, 2), (2, 2), (3, 1), (3, 2))


def rates():
    row = lax.broadcasted_iota(jnp.int32, (8, 128), 0)
    rate = jnp.zeros((8, 128), F32)
    for n in range(8):
        rate = jnp.where(row == n, float(RATES[n]), rate)
    return rate


def sigmoid(v):
    return 1.0 / (1.0 + jnp.exp(-v))


def layer_one(pk, tiles, weights, hot, ys, gp, mom_one, slope_one, u_two):
    w_one_cat, mix1_t, prj_t, base_col, step_col = weights
    low = lanes(8) < 64
    low1 = lanes(1) < 64
    head = lanes(1) < 16
    rate = rates()
    spot = lax.broadcasted_iota(jnp.int32, (256, 128), 0).astype(F32)
    ghost_spot = lax.broadcasted_iota(jnp.int32, (32, 128), 0).astype(F32) + 64.0
    for t in tiles:
        here = pk[t + 1, 0:8]
        info = pk[t + 1, 8:16]
        beside = jnp.where(low, pk[t + 2, 0:8], pk[t, 0:8])
        wide = jnp.concatenate([here, beside], axis=1)
        a = wide.astype(BF16).astype(F32)
        b = (wide - a).astype(BF16).astype(F32)
        c = (wide - a - b).astype(BF16).astype(F32)
        parts = jnp.concatenate([a, b, c, jnp.zeros((8, 256), F32)], axis=0).astype(BF16)
        g_prev, g_here, g_next = pk[t, 14:15], info[6:7], pk[t + 2, 14:15]
        table = jnp.concatenate(
            [
                jnp.where(head, turn(g_prev) + 192.0, turn(g_here) + 64.0),
                jnp.where(head, g_here, g_next + 128.0),
                jnp.zeros((14, 128), F32),
            ],
            axis=0,
        )[:, 0:32].astype(BF16)
        count = info[3:4]
        sums = [None] * 9
        for k, row in enumerate((4, 1, 5, 2)):
            e = info[row : row + 1]
            hit = jnp.where(ghost_spot == e, 1.0, 0.0).astype(BF16)
            far = dot(table, hit)
            n = jnp.where(
                e < 64.0, e + jnp.where(low1, 0.0, 64.0), jnp.where(low1, far[0:1], far[1:2])
            )
            one_hot = jnp.where(spot == n, 1.0, 0.0).astype(BF16)
            hot[t, :, k * 128 : (k + 1) * 128] = one_hot
            got = dot(parts, one_hot)
            there = got[0:8] + (got[8:16] + got[16:24])
            off = there - here
            x, y, z = off[0:1], off[1:2], off[2:3]
            q = x * x + y * y + z * z
            live = jnp.where(count > float(k), 0.25, 0.0)
            g = jnp.exp(-rate * q) * live
            both = jnp.concatenate([g, g * there[3:4]], axis=0)
            harmonic = [
                None, x, y, z, ROOT3 * x * y, ROOT3 * y * z, 0.5 * (3.0 * z * z - q), ROOT3 * x * z,
                (0.5 * ROOT3) * (x * x - y * y),
            ]
            gp[t, k] = both
            ys[t, k] = jnp.concatenate(harmonic[1:9], axis=0)
            for l in range(9):
                term = both if l == 0 else harmonic[l] * both
                sums[l] = term if sums[l] is None else sums[l] + term
        high, lo = split(jnp.concatenate(sums, axis=1))
        moments = dot(w_one_cat, jnp.concatenate([high, lo, high], axis=0))
        m = [moments[:, l * 128 : (l + 1) * 128] for l in range(9)]
        for l in range(9):
            mom_one[t, l] = m[l]
        inv = jnp.concatenate(
            [m[0] * m[0], sum(m[l] * m[l] for l in (1, 2, 3)), sum(m[l] * m[l] for l in range(4, 9))],
            axis=0,
        )
        v = dot3(mix1_t, split(inv))
        sig = sigmoid(v)
        slope_one[t] = sig * (1.0 + v * (1.0 - sig))
        h = base_col + here[3:4] * step_col + v * sig
        u_two[t] = dot3(prj_t, split(h))


def forms_kernel(
    sent, embed, radial_one, radial_two, mix_one, mix_two, proj, readout,
    mix_back, mix_fwd, prj_all, columns, first_cat, first_parts, second_cat, second_parts,
):
    del sent

    def column(row):
        return jnp.broadcast_to(row, (128, 128)).T

    columns[0] = column(embed[0:1])
    columns[1] = column(embed[1:2] - embed[0:1])
    columns[2] = column(readout[1:2])
    columns[3] = column(readout[0:1] + readout[1:2])
    for n, mix in enumerate((mix_one, mix_two)):
        mix_back[2 * n], mix_back[2 * n + 1] = split(mix[...])
        mix_fwd[2 * n], mix_fwd[2 * n + 1] = split(mix[...].T)
    prj_all[0], prj_all[1] = split(proj[...])
    prj_all[2], prj_all[3] = split(proj[...].T)
    base, step = embed[0:1], embed[1:2] - embed[0:1]
    high, lo = split(jnp.concatenate([radial_one[...] * base, radial_one[...] * step], axis=0))
    first_parts[0], first_parts[1] = high, lo
    first_cat[...] = jnp.concatenate([high, high, lo], axis=0).astype(F32).T.astype(BF16)
    high, lo = split(radial_two[...])
    second_parts[0], second_parts[1] = high, lo
    high, lo = high.astype(F32), lo.astype(F32)
    second_cat[...] = jnp.concatenate([high, high, lo, jnp.zeros((8, 128), F32)], axis=0).T.astype(BF16)


def nodes_of_edges(t, m, hot, gp, u_two, second_cat, tk, gk, rk):
    low_wide = lanes(128) < 64
    beside = jnp.where(low_wide, u_two[t + 1], u_two[t - 1])
    high, lo = split(jnp.concatenate([u_two[t], beside], axis=1))
    parts = jnp.concatenate([high, lo], axis=0)
    for k in range(4):
        got = dot(parts, hot[t, :, k * 128 : (k + 1) * 128])
        nodes = got[0:128] + got[128:256]
        g = gp[t, k, 0:8]
        gh = g.astype(BF16).astype(F32)
        rows = jnp.concatenate([gh, g - gh, gh, jnp.zeros((8, 128), F32)], axis=0).astype(BF16)
        weight = dot(second_cat[...], rows)
        gk[m, k] = nodes
        rk[m, k] = weight
        tk[m, k] = nodes * weight


def edge_sums(t, ys):
    edge = [[ys[t, k, c : c + 1] for c in range(3)] for k in range(4)]
    scalar, legendre = {}, {}
    for i in range(4):
        for j in range(i, 4):
            scalar[i, j] = scalar[j, i] = sum(edge[i][c] * edge[j][c] for c in range(3))
    for i in range(4):
        for j in range(i, 4):
            legendre[i, j] = legendre[j, i] = 1.5 * scalar[i, j] * scalar[i, j] - 0.5 * scalar[i, i] * scalar[j, j]
    return edge, scalar, legendre


def invariants_two(t, m, ys, tk, v_one, v_two):
    _, scalar, legendre = edge_sums(t, ys)
    total = (tk[m, 0] + tk[m, 1]) + (tk[m, 2] + tk[m, 3])
    inv1 = inv2 = None
    for i in range(4):
        va = sum(scalar[i, j] * tk[m, j] for j in range(4))
        vb = sum(legendre[i, j] * tk[m, j] for j in range(4))
        v_one[m, i], v_two[m, i] = va, vb
        inv1 = va * tk[m, i] if inv1 is None else inv1 + va * tk[m, i]
        inv2 = vb * tk[m, i] if inv2 is None else inv2 + vb * tk[m, i]
    return split(jnp.concatenate([total * total, inv1, inv2], axis=0))


def mixing_back(m, inv, mix_back, mix_fwd, columns, dinv):
    v = dot3((mix_fwd[2], mix_fwd[3]), inv)
    sig = sigmoid(v)
    dv = columns[2] * (sig * (1.0 + v * (1.0 - sig)))
    dinv[m] = 2.0 * dot3((mix_back[2], mix_back[3]), split(dv))


def edges_back(t, m, hot, ys, gp, second_parts, tk, gk, rk, v_one, v_two, dinv, du_two, dvec):
    low_wide = lanes(128) < 64
    edge, scalar, _ = edge_sums(t, ys)
    rate = rates()
    w_two2 = (second_parts[0], second_parts[1])
    d1, d2 = dinv[m, 128:256], dinv[m, 256:384]
    d0 = dinv[m, 0:128] * ((tk[m, 0] + tk[m, 1]) + (tk[m, 2] + tk[m, 3]))
    pull, bend = {}, {}
    for i in range(4):
        wa, wb = d1 * tk[m, i], d2 * tk[m, i]
        for j in range(i, 4):
            pull[i, j] = pull[j, i] = jnp.sum(wa * tk[m, j], axis=0, keepdims=True)
            bend[i, j] = bend[j, i] = jnp.sum(wb * tk[m, j], axis=0, keepdims=True)
    back = None
    for k in range(4):
        dt = d0 + d1 * v_one[m, k] + d2 * v_two[m, k]
        dg = dot3(w_two2, split(dt * gk[m, k]))
        high, lo = split(dt * rk[m, k])
        term = dot_t(jnp.concatenate([high, lo], axis=0), hot[t, :, k * 128 : (k + 1) * 128])
        back = term if back is None else back + term
        dq = 0.5 * pull[k, k] + bend[k, k] * scalar[k, k] - jnp.sum(rate * gp[t, k, 0:8] * dg, axis=0, keepdims=True)
        d = [None] * 3
        for j in range(4):
            if j != k:
                dq = dq - 0.5 * bend[k, j] * scalar[j, j]
                tie = pull[k, j] + 3.0 * bend[k, j] * scalar[k, j]
                d = [tie * edge[j][c] if d[c] is None else d[c] + tie * edge[j][c] for c in range(3)]
        d = [d[c] + 2.0 * dq * edge[k][c] for c in range(3)]
        dvec[t, k] = jnp.concatenate(d + [jnp.zeros((5, 128), F32)], axis=0)
    back = back[0:128] + back[128:256]
    du_two[t] += back[:, 0:128]
    aside = back[:, 128:256]
    du_two[t + 1] += jnp.where(low_wide, aside, 0.0)
    du_two[t - 1] += jnp.where(low_wide, 0.0, aside)


def plane_work(
    packed, forms, hot, ys, gp, mom_one, slope_one, u_two, du_two, dvec,
    pk, tk, gk, rk, v_one, v_two, dinv,
):
    mix_back, mix_fwd, prj_all, columns, first_cat, first_parts, second_cat, second_parts = forms
    _, side, _ = whereabouts()
    first = 2 * (1 - side)
    for t in range(2):
        pk[t] = packed[0]
        pk[6 + t] = packed[3]
    pk[pl.ds(first + 1, 4)] = packed[...]
    weights = (first_cat[...], (mix_fwd[0], mix_fwd[1]), (prj_all[2], prj_all[3]), columns[0], columns[1])
    start = 3 * (1 - side)
    layer_one(pk, [start + i for i in range(3)], weights, hot, ys, gp, mom_one, slope_one, u_two)

    du_two[...] = jnp.zeros_like(du_two)
    t = start + 1
    nodes_of_edges(t, 0, hot, gp, u_two, second_cat, tk, gk, rk)
    inv = invariants_two(t, 0, ys, tk, v_one, v_two)
    mixing_back(0, inv, mix_back, mix_fwd, columns, dinv)
    edges_back(t, 0, hot, ys, gp, second_parts, tk, gk, rk, v_one, v_two, dinv, du_two, dvec)


def is_early(s):
    return s < 4


def early_kernel(packed, *refs):
    forms, rest = refs[0:8], refs[10:]

    @pl.when(is_early(whereabouts()[2]))
    def _():
        plane_work(packed, forms, *rest)


def late_kernel(packed, *refs):
    forms, rest = refs[0:8], refs[16:]

    @pl.when(jnp.logical_not(is_early(whereabouts()[2])))
    def _():
        plane_work(packed, forms, *rest)


def force_kernel(packed, across, moment, *refs):
    mix_back, mix_fwd, prj_all, columns, first_cat, first_parts, second_cat, second_parts = refs[0:8]
    out, hot, ys, gp, mom_one, slope_one, u_two, du_two, dvec, pk, tk, gk, rk, v_one, v_two, dinv = refs[16:]
    _, side, _ = whereabouts()
    low = lanes(8) < 64
    first = 2 * (1 - side)
    other = 4 * side
    pk[0] = across[0]
    pk[7] = across[1]
    pk[pl.ds(first + 1, 4)] = packed[...]
    pk[pl.ds(other + 1, 2)] = across[...]
    w_one2 = (first_parts[0], first_parts[1])
    weights = (first_cat[...], (mix_fwd[0], mix_fwd[1]), (prj_all[2], prj_all[3]), columns[0], columns[1])
    start = 3 * side
    layer_one(pk, [start + i for i in range(3)], weights, hot, ys, gp, mom_one, slope_one, u_two)
    rate = rates()

    turns = [side + 1 + i for i in range(3)]
    inv = {}

    def stage(n, m):
        t = turns[m]
        if n == 0:
            nodes_of_edges(t, m, hot, gp, u_two, second_cat, tk, gk, rk)
        elif n == 1:
            inv[m] = invariants_two(t, m, ys, tk, v_one, v_two)
        elif n == 2:
            mixing_back(m, inv[m], mix_back, mix_fwd, columns, dinv)
        else:
            edges_back(t, m, hot, ys, gp, second_parts, tk, gk, rk, v_one, v_two, dinv, du_two, dvec)

    for n, m in ORDER:
        stage(n, m)

    def third(du, slope, mom, gs, harmonics, pushes, spots):
        dh = columns[3] + dot3((prj_all[0], prj_all[1]), split(du))
        dinv = 2.0 * dot3((mix_back[0], mix_back[1]), split(dh * slope))
        parts = []
        for l in range(9):
            part = 0 if l == 0 else 1 if l < 4 else 2
            parts.append(mom(l) * dinv[part * 128 : (part + 1) * 128])
        dm = dot3(w_one2, split(jnp.concatenate(parts, axis=1)))
        dm = [dm[:, l * 128 : (l + 1) * 128] for l in range(9)]
        rate2 = jnp.concatenate([rate, rate], axis=0)
        back = None
        centre = None
        for k in range(4):
            g, yk, push = gs(k), harmonics(k), pushes(k)
            dg = dm[0]
            dys = []
            for l in range(1, 9):
                dg = dg + yk[l - 1 : l] * dm[l]
                dys.append(jnp.sum(g * dm[l], axis=0, keepdims=True))
            dq = -jnp.sum(rate2 * g * dg, axis=0, keepdims=True)
            x, y, z = yk[0:1], yk[1:2], yk[2:3]
            e1, e2, e3, e4, e5, e6, e7, e8 = dys
            dx = e1 + ROOT3 * (y * e4 + z * e7 + x * e8) + x * (2.0 * dq - e6)
            dy = e2 + ROOT3 * (x * e4 + z * e5 - y * e8) + y * (2.0 * dq - e6)
            dz = e3 + ROOT3 * (y * e5 + x * e7) + 2.0 * z * (dq + e6)
            d = push + jnp.concatenate([dx, dy, dz, jnp.zeros((5, 128), F32)], axis=0)
            centre = d if centre is None else centre + d
            d_high = d.astype(BF16).astype(F32)
            rows = jnp.concatenate([d_high, d - d_high], axis=0).astype(BF16)
            term = dot_t(rows, spots(k))
            back = term if back is None else back + term
        return back[0:8] + back[8:16], centre

    def own_tile(t):
        return third(
            du_two[t], slope_one[t], lambda l: mom_one[t, l], lambda k: gp[t, k], lambda k: ys[t, k],
            lambda k: dvec[t, k], lambda k: hot[t, :, k * 128 : (k + 1) * 128],
        )

    def mixed(ref, *at):
        right, left = ref[(4,) + at], ref[(1,) + at]
        keep = lax.broadcasted_iota(jnp.int32, right.shape, 1) < 64
        return jnp.where(keep, right, left)

    def mixed_spots(k):
        at = (slice(128, 256), slice(k * 128, (k + 1) * 128))
        keep = lanes(128) < 64
        return jnp.where(keep, hot[(4,) + at].astype(F32), hot[(1,) + at].astype(F32)).astype(BF16)

    back2, centre2 = own_tile(2)
    back3, centre3 = own_tile(3)
    rim, _ = third(
        mixed(du_two), mixed(slope_one), lambda l: mixed(mom_one, l), lambda k: mixed(gp, k), lambda k: mixed(ys, k),
        lambda k: mixed(dvec, k), mixed_spots,
    )
    f2 = centre2 - back2[:, 0:128] - jnp.where(low, rim, back3[:, 128:256])
    f3 = centre3 - back3[:, 0:128] - jnp.where(low, back2[:, 128:256], rim)
    row = lax.broadcasted_iota(jnp.int32, (8, 128), 0)
    for t, f in enumerate((f2, f3)):
        coords, drift = pk[t + 3, 0:8], pltpu.roll(moment[t], 3, 0)
        out[2 * t] = jnp.where(row < 3, jnp.where(low, f, turn(coords)), drift)
        out[2 * t + 1] = jnp.where(row < 3, jnp.where(low, turn(f), coords), turn(drift))


def finish_kernel(got, pos_out, mom_out, force_out):
    _, side, _ = whereabouts()
    for b in range(4):
        block = got[b ^ (2 * side)]
        turned = turn(block)
        for c in range(3):
            force = block[c : c + 1, 0:64]
            pos_out[c, b : b + 1] = turned[c : c + 1, 0:64]
            mom_out[c, b : b + 1] = block[3 + c : 4 + c, 0:64] + 0.5 * force
            force_out[c, b : b + 1] = force


def shape(*dims):
    return jax.ShapeDtypeStruct(dims, F32)


def room(mib):
    return pltpu.CompilerParams(vmem_limit_bytes=mib << 20)


def near(*dims, dtype=F32):
    return pltpu.VMEM(dims, dtype)


def far(x):
    return pltpu.with_memory_space_constraint(x, pltpu.HBM)


def keep(x):
    return pltpu.with_memory_space_constraint(x, pltpu.VMEM)


def on_device(
    positions, momenta, forces, species, neighbours, counts, ghost_rows,
    embed, radial_one, radial_two, mix_one, mix_two, projection, readout,
):
    count = lax.axis_size("space")
    both = ("bead", "space")
    planes = [[b * count + z * 8 + i for b in range(4) for i in range(8)] for z in range(count // 8)]
    quads = [[b * count + h * 4 + i for i in range(4)] for b in range(4) for h in range(count // 4)]
    beside = []
    for b in range(4):
        for z in range(count // 8):
            for i in range(4):
                here = b * count + z * 8 + i
                back = b * count + (z * 8 - 4) % count + (i ^ 2)
                beside += [(here, back), (back, here)]

    turned = [jnp.transpose(x, (1, 0, 2)) for x in (positions, momenta, forces)]
    sent = pl.pallas_call(
        pack_kernel, out_shape=shape(32, 8, 128), in_specs=[VM] * 8, out_specs=VM, name="pack",
    )(*[far(x) for x in (jnp.asarray(mode_tables()), *turned, species[None, :], neighbours, counts, ghost_rows)])
    got = keep(lax.all_to_all(sent, both, 0, 0, axis_index_groups=planes))
    forms = pl.pallas_call(
        forms_kernel,
        out_shape=(
            near(4, 384, 128, dtype=BF16), near(4, 128, 384, dtype=BF16),
            near(4, 128, 128, dtype=BF16), near(4, 128, 128), near(128, 48, dtype=BF16),
            near(2, 16, 128, dtype=BF16), near(128, 32, dtype=BF16), near(2, 8, 128, dtype=BF16),
        ),
        in_specs=[pl.BlockSpec(memory_space=pl.ANY)] + [VM] * 7,
        out_specs=(VM,) * 8,
        compiler_params=room(8),
        cost_estimate=pl.CostEstimate(flops=2_000_000_000, bytes_accessed=4_000_000, transcendentals=0),
        name="forms",
    )(*[far(x) for x in (sent, embed, radial_one, radial_two, mix_one, mix_two, projection, readout)])
    packed, own, moment = pl.pallas_call(
        modes_kernel,
        out_shape=(near(4, 16, 128), near(2, 16, 128), near(2, 8, 128)),
        in_specs=[VM],
        out_specs=(VM,) * 3,
        compiler_params=room(16),
        name="modes",
    )(got)
    kept = (
        near(TILES, 256, 512, dtype=BF16),
        near(TILES, 4, 8, 128),
        near(TILES, 4, 16, 128),
        near(TILES, 9, 128, 128),
        near(TILES, 128, 128),
        near(TILES, 128, 128),
        near(TILES, 128, 128),
        near(TILES, 4, 8, 128),
    )

    def scratch(n):
        return [near(8, 16, 128)] + [near(n, 4, 128, 128)] * 5 + [near(n, 384, 128)]

    own, *state = pl.pallas_call(
        early_kernel,
        out_shape=(near(2, 16, 128),) + kept,
        in_specs=[VM] * 10,
        out_specs=(VM,) * 9,
        scratch_shapes=scratch(1),
        input_output_aliases={9: 0},
        compiler_params=room(24),
        name="early",
    )(packed, *forms, own)
    across = keep(lax.ppermute(own, both, beside))
    state = pl.pallas_call(
        late_kernel,
        out_shape=kept,
        in_specs=[VM] * 17,
        out_specs=(VM,) * 8,
        scratch_shapes=scratch(1),
        input_output_aliases={9 + i: i for i in range(8)},
        compiler_params=room(24),
        cost_estimate=pl.CostEstimate(flops=4_000_000_000, bytes_accessed=8_000_000, transcendentals=0),
        name="late",
    )(packed, *forms, *state)
    grad = pl.pallas_call(
        force_kernel,
        out_shape=(near(4, 8, 128),) + kept,
        in_specs=[VM] * 19,
        out_specs=(VM,) * 9,
        scratch_shapes=scratch(3),
        input_output_aliases={11 + i: 1 + i for i in range(8)},
        compiler_params=room(24),
        name="force",
    )(packed, across, moment, *forms, *state)[0]
    back = keep(lax.all_to_all(grad, both, 0, 0, axis_index_groups=quads))
    outs = pl.pallas_call(
        finish_kernel,
        out_shape=(shape(3, 4, 64),) * 3,
        in_specs=[VM],
        out_specs=(VM,) * 3,
        compiler_params=room(8),
        name="finish",
    )(back)
    return tuple(jnp.transpose(x, (1, 0, 2)) for x in outs)


def solution(mesh):
    spread = P("bead", None, "space")
    placed = (
        spread, spread, spread, P("space"), spread, P("bead", "space"), P("space", None, None),
    ) + (P(),) * 7
    return jax.shard_map(
        on_device, mesh=mesh, in_specs=placed, out_specs=(spread,) * 3, check_vma=False
    )
```

time: 55.3 us -> 49.6 us (0.90)
  starting transfers between devices: 20.3 us -> 15.8 us
  Pallas kernels: 20.6 us -> 17.2 us
  waiting for transfers between devices: 7.37 us -> 8.62 us
  blocking collectives: 5.9 us -> 7.02 us
    ppermute x1, starting transfers between devices: 9.94 us -> 5.46 us  [on_device(): across = keep(lax.ppermute(own, both, beside))]
    pallas_call x5 -> x6, Pallas kernels: 19.9 us -> 17.2 us  [the longest x1 8.58 us: on_device(): pl.pallas_call(force_kernel, out_shape=(near(4, 8, 128),) + kept, in_spec...]
    ppermute x1, waiting for transfers between devices: 0.01 us -> 2.31 us  [on_device(): across = keep(lax.ppermute(own, both, beside))]
    all_to_all x1, blocking collectives: 5.9 us -> 7.02 us  [on_device(): back = keep(lax.all_to_all(grad, both, 0, 0, axis_index_groups=quads))]
    all_to_all x1, waiting for transfers between devices: 7.36 us -> 6.31 us  [on_device(): got = keep(lax.all_to_all(sent, both, 0, 0, axis_index_groups=planes))]
    pallas_call x1, Pallas kernels: 0.8 us -> 0.09 us  [on_device(): pl.pallas_call(modes_kernel, out_shape=(near(4, 16, 128), near(2, 16, 128...]
  transfers between devices with their start and end apart: 2 -> 2, of which waited for: 1 -> 2; matrix products, arithmetic and copies ran while one was open for 0% -> 0% of each run, Pallas kernels for 11% -> 3%
where the time goes in v3:
time: 49.6 us; the launch traced here: 49.4 us
  Pallas kernels  17.2 us (35%)
  starting transfers between devices  15.8 us (32%)
  waiting for transfers between devices  8.62 us (17%)
  blocking collectives  7.02 us (14%)
  between operations  0.68 us (1%)
    all_to_all x1, starting transfers between devices, on_device(): got = keep(lax.all_to_all(sent, both, 0, 0, axis_index_groups=planes))  10.3 us
    pallas_call x1, Pallas kernels, on_device(): pl.pallas_call(force_kernel, out_shape=(near(4, 8, 128),) + kept, in_spec...  8.58 us
    all_to_all x1, blocking collectives, on_device(): back = keep(lax.all_to_all(grad, both, 0, 0, axis_index_groups=quads))  7.02 us
    all_to_all x1, waiting for transfers between devices, on_device(): got = keep(lax.all_to_all(sent, both, 0, 0, axis_index_groups=planes))  6.31 us
    ppermute x1, starting transfers between devices, on_device(): across = keep(lax.ppermute(own, both, beside))  5.46 us
    pallas_call x1, Pallas kernels, on_device(): pl.pallas_call(early_kernel, out_shape=(near(2, 16, 128),) + kept, in_spe...  4.44 us
    ppermute x1, waiting for transfers between devices, on_device(): across = keep(lax.ppermute(own, both, beside))  2.31 us
    pallas_call x1, Pallas kernels, on_device(): pl.pallas_call(pack_kernel, out_shape=shape(32, 8, 128), in_specs=[VM] *...  1.97 us
  transfers between devices with their start and end apart: 2, of which 2 were waited for; matrix products, arithmetic and copies ran while one was open for 0% of the time, Pallas kernels for 3%

profile of v3, /device:TPU:1, one launch (start us, length us, event | category | flops | bytes accessed | tf_op | source)
XLA Modules:
  0.0 49.4 jit_solution(7352225360347273724)
XLA Ops:
  0.6 2.0 %pack.1.sent = f32[32,8,128]{2,1,0:T(8,128)} custom-call(bf16[4,2,128,96]{3,2,1,0:T(8,128)(2,1)} %constant.2.clone.table, f32[3,4,64]{2,1,0:T(4,128)} %bitcast.7, f32[3,4,64]{2,1,0:T(4,128)} %bitcast.8, f32[3,4,64]{2,1,0:T(4,128)} %bitcast.9, s32[1,64]{1,0:T(1,128)} %bitcast.10, s32[4,4,64]{2,1,0:T(4,128)} %nbr.1, s32[4,64]{1,0:T(4,128)} %counts.1, ...), custom_call_target="tpu_custom_call" | custom-call | tf_op jit(solution)/shard_map/pack/pallas_call | solution.py:536
  2.6 10.3 %all-to-all-start = ((f32[32,8,128]{2,1,0:T(8,128)}), f32[32,8,128]{2,1,0:T(8,128)S(1)}, u32[]{:S(2)}, u32[]{:S(2)}) async-start(f32[32,8,128]{2,1,0:T(8,128)} %pack.1.sent), calls=%async_computation | async-start | bytes 262144 | tf_op jit(solution)/shard_map/all_to_all | solution.py:539
  13.0 1.5 %forms.1 = (bf16[4,384,128]{2,1,0:T(8,128)(2,1)S(1)}, bf16[4,128,384]{2,1,0:T(8,128)(2,1)S(1)}, bf16[4,128,128]{2,1,0:T(8,128)(2,1)S(1)}, f32[4,128,128]{2,1,0:T...) custom-call(f32[32,8,128]{2,1,0:T(8,128)} %pack.1.sent, ...), custom_call_target="tpu_custom_call" | custom-call | flops 2000000000 | bytes 4000000 | tf_op jit(solution)/shard_map/forms/pallas_call | solution.py:540
  14.4 6.3 %all-to-all-done.got = f32[32,8,128]{2,1,0:T(8,128)S(1)} async-done(((f32[32,8,128]{2,1,0:T(8,128)}), f32[32,8,128]{2,1,0:T(8,128)S(1)}, u32[]{:S(2)}, u32[]{:S(2)}) %all-to-all-start) | async-done | bytes 131104 | tf_op jit(solution)/shard_map/all_to_all | solution.py:539
  20.7 0.1 modes.1
  20.8 4.4 %early.1 = (f32[2,16,128]{2,1,0:T(8,128)S(1)}, bf16[6,256,512]{2,1,0:T(8,128)(2,1)S(1)}, f32[6,4,8,128]{3,2,1,0:T(8,128)S(1)}, f32[6,4,16,128]{3,2,1,0:T(8,128)S...) custom-call(f32[4,16,128]{2,1,0:T(8,128)S(1)} %get-tuple-element.35., ...), custom_call_target="tpu_custom_call", output_to_operand_aliasing={{0}: (9, {})} | custom-call | tf_op jit(solution)/shard_map/early/pallas_call | solution.py:575
  25.3 5.5 %collective-permute-start = (f32[2,16,128]{2,1,0:T(8,128)S(1)}, f32[2,16,128]{2,1,0:T(8,128)S(1)}, u32[]{:S(2)}, u32[]{:S(2)}) collective-permute-start(f32[2,16,128]{2,1,0:T(8,128)S(1)} %get-tuple-element.45), channel_id=1, source_target_pairs={{0,126},{126,0},{1,127},{127,1},{2,124},{124,2},{3,125},{125,3},{8... | collective-permute-start | bytes 49160 | tf_op jit(solution)/shard_map/ppermute | solution.py:585
  30.8 2.3 %collective-permute-done.across = f32[2,16,128]{2,1,0:T(8,128)S(1)} collective-permute-done((f32[2,16,128]{2,1,0:T(8,128)S(1)}, f32[2,16,128]{2,1,0:T(8,128)S(1)}, u32[]{:S(2)}, u32[]{:S(2)}) %collective-permute-start) | collective-permute-done | bytes 16416 | tf_op jit(solution)/shard_map/ppermute | solution.py:585
  33.1 8.6 %force.1 = (f32[4,8,128]{2,1,0:T(8,128)S(1)}, bf16[6,256,512]{2,1,0:T(8,128)(2,1)S(1)}, f32[6,4,8,128]{3,2,1,0:T(8,128)S(1)}, f32[6,4,16,128]{3,2,1,0:T(8,128)S(...) custom-call(f32[4,16,128]{2,1,0:T(8,128)S(1)} %get-tuple-element.35., ...), custom_call_target="tpu_custom_call", output_to_operand_aliasing={{1}: (11, {}), {2}: (12, {}), {3}: (13, {}), {4}: (14, {}),... | custom-call | tf_op jit(solution)/shard_map/force/pallas_call | solution.py:597
  41.7 7.0 %all_to_all.10.got = f32[4,8,128]{2,1,0:T(8,128)S(1)} all-to-all(f32[4,8,128]{2,1,0:T(8,128)S(1)} %get-tuple-element.63), channel_id=1, replica_groups={{0,1,2,3},{4,5,6,7},{8,9,10,11},{12,13,14,15},{16,17,18,19},{20,21,22,2..., dimensions={0} | all-to-all | bytes 32768 | tf_op jit(solution)/shard_map/all_to_all | solution.py:607
  48.7 0.7 %finish.1 = (f32[3,4,64]{2,1,0:T(4,128)}, f32[3,4,64]{2,1,0:T(4,128)}, f32[3,4,64]{2,1,0:T(4,128)}) custom-call(f32[4,8,128]{2,1,0:T(8,128)S(1)} %all_to_all.10.got), custom_call_target="tpu_custom_call" | custom-call | tf_op jit(solution)/shard_map/finish/pallas_call | solution.py:608
  (1 shorter events, 0.0 us)
Async XLA Ops:
  2.6 18.1 %all-to-all-start = ((f32[32,8,128]{2,1,0:T(8,128)}), f32[32,8,128]{2,1,0:T(8,128)S(1)}, u32[]{:S(2)}, u32[]{:S(2)}) async-start(f32[32,8,128]{2,1,0:T(8,128)} %pack.1.sent), calls=%async_computation | async-start | bytes 262144 | tf_op jit(solution)/shard_map/all_to_all | solution.py:539
  25.3 7.8 %collective-permute-start = (f32[2,16,128]{2,1,0:T(8,128)S(1)}, f32[2,16,128]{2,1,0:T(8,128)S(1)}, u32[]{:S(2)}, u32[]{:S(2)}) collective-permute-start(f32[2,16,128]{2,1,0:T(8,128)S(1)} %get-tuple-element.45), channel_id=1, source_target_pairs={{0,126},{126,0},{1,127},{127,1},{2,124},{124,2},{3,125},{125,3},{8... | collective-permute-start | bytes 49160 | tf_op jit(solution)/shard_map/ppermute | solution.py:585

commit v4 on v3

--- a/solution.py
+++ b/solution.py
@@ -65,8 +65,14 @@
     return lax.dot_general(a, b, (((1,), (1,)), ((), ())), preferred_element_type=F32)
 
 
+def thrice(x):
+    high, lo = split(x)
+    return jnp.concatenate([high, high, lo], axis=1)
+
+
 def dot3(a, b):
-    return dot(a[0], b[0]) + (dot(a[0], b[1]) + dot(a[1], b[0]))
+    high, lo = split(b)
+    return dot(a, jnp.concatenate([high, lo, high], axis=0))
 
 
 def lanes(rows):
@@ -156,6 +162,19 @@
     return rate
 
 
+def abreast(jobs):
+    results = [None] * len(jobs)
+    left = list(range(len(jobs)))
+    while left:
+        for n in list(left):
+            try:
+                next(jobs[n])
+            except StopIteration as stop:
+                results[n] = stop.value
+                left.remove(n)
+    return results
+
+
 def sigmoid(v):
     return 1.0 / (1.0 + jnp.exp(-v))
 
@@ -168,7 +187,7 @@
     rate = rates()
     spot = lax.broadcasted_iota(jnp.int32, (256, 128), 0).astype(F32)
     ghost_spot = lax.broadcasted_iota(jnp.int32, (32, 128), 0).astype(F32) + 64.0
-    for t in tiles:
+    def one(t):
         here = pk[t + 1, 0:8]
         info = pk[t + 1, 8:16]
         beside = jnp.where(low, pk[t + 2, 0:8], pk[t, 0:8])
@@ -214,8 +233,10 @@
             for l in range(9):
                 term = both if l == 0 else harmonic[l] * both
                 sums[l] = term if sums[l] is None else sums[l] + term
+            yield
         high, lo = split(jnp.concatenate(sums, axis=1))
         moments = dot(w_one_cat, jnp.concatenate([high, lo, high], axis=0))
+        yield
         m = [moments[:, l * 128 : (l + 1) * 128] for l in range(9)]
         for l in range(9):
             mom_one[t, l] = m[l]
@@ -223,11 +244,15 @@
             [m[0] * m[0], sum(m[l] * m[l] for l in (1, 2, 3)), sum(m[l] * m[l] for l in range(4, 9))],
             axis=0,
         )
-        v = dot3(mix1_t, split(inv))
+        v = dot3(mix1_t, inv)
+        yield
         sig = sigmoid(v)
         slope_one[t] = sig * (1.0 + v * (1.0 - sig))
         h = base_col + here[3:4] * step_col + v * sig
-        u_two[t] = dot3(prj_t, split(h))
+        u_two[t] = dot3(prj_t, h)
+        yield
+
+    abreast([one(t) for t in tiles])
 
 
 def forms_kernel(
@@ -244,16 +269,16 @@
     columns[2] = column(readout[1:2])
     columns[3] = column(readout[0:1] + readout[1:2])
     for n, mix in enumerate((mix_one, mix_two)):
-        mix_back[2 * n], mix_back[2 * n + 1] = split(mix[...])
-        mix_fwd[2 * n], mix_fwd[2 * n + 1] = split(mix[...].T)
-    prj_all[0], prj_all[1] = split(proj[...])
-    prj_all[2], prj_all[3] = split(proj[...].T)
+        mix_back[n] = thrice(mix[...])
+        mix_fwd[n] = thrice(mix[...].T)
+    prj_all[0] = thrice(proj[...])
+    prj_all[1] = thrice(proj[...].T)
     base, step = embed[0:1], embed[1:2] - embed[0:1]
     high, lo = split(jnp.concatenate([radial_one[...] * base, radial_one[...] * step], axis=0))
-    first_parts[0], first_parts[1] = high, lo
+    first_parts[...] = jnp.concatenate([high, high, lo], axis=1)
     first_cat[...] = jnp.concatenate([high, high, lo], axis=0).astype(F32).T.astype(BF16)
     high, lo = split(radial_two[...])
-    second_parts[0], second_parts[1] = high, lo
+    second_parts[...] = jnp.concatenate([high, high, lo], axis=1)
     high, lo = high.astype(F32), lo.astype(F32)
     second_cat[...] = jnp.concatenate([high, high, lo, jnp.zeros((8, 128), F32)], axis=0).T.astype(BF16)
 
@@ -297,21 +322,20 @@
         v_one[m, i], v_two[m, i] = va, vb
         inv1 = va * tk[m, i] if inv1 is None else inv1 + va * tk[m, i]
         inv2 = vb * tk[m, i] if inv2 is None else inv2 + vb * tk[m, i]
-    return split(jnp.concatenate([total * total, inv1, inv2], axis=0))
+    return jnp.concatenate([total * total, inv1, inv2], axis=0)
 
 
 def mixing_back(m, inv, mix_back, mix_fwd, columns, dinv):
-    v = dot3((mix_fwd[2], mix_fwd[3]), inv)
+    v = dot3(mix_fwd[1], inv)
     sig = sigmoid(v)
     dv = columns[2] * (sig * (1.0 + v * (1.0 - sig)))
-    dinv[m] = 2.0 * dot3((mix_back[2], mix_back[3]), split(dv))
+    dinv[m] = 2.0 * dot3(mix_back[1], dv)
 
 
 def edges_back(t, m, hot, ys, gp, second_parts, tk, gk, rk, v_one, v_two, dinv, du_two, dvec):
     low_wide = lanes(128) < 64
     edge, scalar, _ = edge_sums(t, ys)
     rate = rates()
-    w_two2 = (second_parts[0], second_parts[1])
     d1, d2 = dinv[m, 128:256], dinv[m, 256:384]
     d0 = dinv[m, 0:128] * ((tk[m, 0] + tk[m, 1]) + (tk[m, 2] + tk[m, 3]))
     pull, bend = {}, {}
@@ -320,13 +344,11 @@
         for j in range(i, 4):
             pull[i, j] = pull[j, i] = jnp.sum(wa * tk[m, j], axis=0, keepdims=True)
             bend[i, j] = bend[j, i] = jnp.sum(wb * tk[m, j], axis=0, keepdims=True)
-    back = None
+    back = []
     for k in range(4):
         dt = d0 + d1 * v_one[m, k] + d2 * v_two[m, k]
-        dg = dot3(w_two2, split(dt * gk[m, k]))
-        high, lo = split(dt * rk[m, k])
-        term = dot_t(jnp.concatenate([high, lo], axis=0), hot[t, :, k * 128 : (k + 1) * 128])
-        back = term if back is None else back + term
+        dg = dot3(second_parts[...], dt * gk[m, k])
+        back.append(jnp.concatenate(split(dt * rk[m, k]), axis=0))
         dq = 0.5 * pull[k, k] + bend[k, k] * scalar[k, k] - jnp.sum(rate * gp[t, k, 0:8] * dg, axis=0, keepdims=True)
         d = [None] * 3
         for j in range(4):
@@ -336,6 +358,7 @@
                 d = [tie * edge[j][c] if d[c] is None else d[c] + tie * edge[j][c] for c in range(3)]
         d = [d[c] + 2.0 * dq * edge[k][c] for c in range(3)]
         dvec[t, k] = jnp.concatenate(d + [jnp.zeros((5, 128), F32)], axis=0)
+    back = dot_t(jnp.concatenate(back, axis=1), hot[t])
     back = back[0:128] + back[128:256]
     du_two[t] += back[:, 0:128]
     aside = back[:, 128:256]
@@ -354,7 +377,7 @@
         pk[t] = packed[0]
         pk[6 + t] = packed[3]
     pk[pl.ds(first + 1, 4)] = packed[...]
-    weights = (first_cat[...], (mix_fwd[0], mix_fwd[1]), (prj_all[2], prj_all[3]), columns[0], columns[1])
+    weights = (first_cat[...], mix_fwd[0], prj_all[1], columns[0], columns[1])
     start = 3 * (1 - side)
     layer_one(pk, [start + i for i in range(3)], weights, hot, ys, gp, mom_one, slope_one, u_two)
 
@@ -397,8 +420,7 @@
     pk[7] = across[1]
     pk[pl.ds(first + 1, 4)] = packed[...]
     pk[pl.ds(other + 1, 2)] = across[...]
-    w_one2 = (first_parts[0], first_parts[1])
-    weights = (first_cat[...], (mix_fwd[0], mix_fwd[1]), (prj_all[2], prj_all[3]), columns[0], columns[1])
+    weights = (first_cat[...], mix_fwd[0], prj_all[1], columns[0], columns[1])
     start = 3 * side
     layer_one(pk, [start + i for i in range(3)], weights, hot, ys, gp, mom_one, slope_one, u_two)
     rate = rates()
@@ -421,13 +443,16 @@
         stage(n, m)
 
     def third(du, slope, mom, gs, harmonics, pushes, spots):
-        dh = columns[3] + dot3((prj_all[0], prj_all[1]), split(du))
-        dinv = 2.0 * dot3((mix_back[0], mix_back[1]), split(dh * slope))
+        dh = columns[3] + dot3(prj_all[0], du)
+        yield
+        dinv = 2.0 * dot3(mix_back[0], dh * slope)
+        yield
         parts = []
         for l in range(9):
             part = 0 if l == 0 else 1 if l < 4 else 2
             parts.append(mom(l) * dinv[part * 128 : (part + 1) * 128])
-        dm = dot3(w_one2, split(jnp.concatenate(parts, axis=1)))
+        dm = dot3(first_parts[...], jnp.concatenate(parts, axis=1))
+        yield
         dm = [dm[:, l * 128 : (l + 1) * 128] for l in range(9)]
         rate2 = jnp.concatenate([rate, rate], axis=0)
         back = None
@@ -451,6 +476,7 @@
             rows = jnp.concatenate([d_high, d - d_high], axis=0).astype(BF16)
             term = dot_t(rows, spots(k))
             back = term if back is None else back + term
+            yield
         return back[0:8] + back[8:16], centre
 
     def own_tile(t):
@@ -469,12 +495,11 @@
         keep = lanes(128) < 64
         return jnp.where(keep, hot[(4,) + at].astype(F32), hot[(1,) + at].astype(F32)).astype(BF16)
 
-    back2, centre2 = own_tile(2)
-    back3, centre3 = own_tile(3)
-    rim, _ = third(
+    rim = third(
         mixed(du_two), mixed(slope_one), lambda l: mixed(mom_one, l), lambda k: mixed(gp, k), lambda k: mixed(ys, k),
         lambda k: mixed(dvec, k), mixed_spots,
     )
+    (back2, centre2), (back3, centre3), (rim, _) = abreast([own_tile(2), own_tile(3), rim])
     f2 = centre2 - back2[:, 0:128] - jnp.where(low, rim, back3[:, 128:256])
     f3 = centre3 - back3[:, 0:128] - jnp.where(low, back2[:, 128:256], rim)
     row = lax.broadcasted_iota(jnp.int32, (8, 128), 0)
@@ -540,9 +565,9 @@
     forms = pl.pallas_call(
         forms_kernel,
         out_shape=(
-            near(4, 384, 128, dtype=BF16), near(4, 128, 384, dtype=BF16),
-            near(4, 128, 128, dtype=BF16), near(4, 128, 128), near(128, 48, dtype=BF16),
-            near(2, 16, 128, dtype=BF16), near(128, 32, dtype=BF16), near(2, 8, 128, dtype=BF16),
+            near(2, 384, 384, dtype=BF16), near(2, 128, 1152, dtype=BF16),
+            near(2, 128, 384, dtype=BF16), near(4, 128, 128), near(128, 48, dtype=BF16),
+            near(16, 384, dtype=BF16), near(128, 32, dtype=BF16), near(8, 384, dtype=BF16),
         ),
         in_specs=[pl.BlockSpec(memory_space=pl.ANY)] + [VM] * 7,
         out_specs=(VM,) * 8,

time: 49.6 us -> 46 us (0.927)
  Pallas kernels: 17.2 us -> 13.6 us
  waiting for transfers between devices: 8.62 us -> 7.45 us
  starting transfers between devices: 15.8 us -> 16.9 us
    pallas_call x1, Pallas kernels: 8.58 us -> 6.06 us  [on_device(): pl.pallas_call(force_kernel, out_shape=(near(4, 8, 128),) + kept, in_spec...]
    ppermute x1, waiting for transfers between devices: 2.31 us -> 1.19 us  [on_device(): across = keep(lax.ppermute(own, both, beside))]
    pallas_call x1, Pallas kernels: 4.44 us -> 3.31 us  [on_device(): pl.pallas_call(early_kernel, out_shape=(near(2, 16, 128),) + kept, in_spe...]
    ppermute x1, starting transfers between devices: 5.46 us -> 6.58 us  [on_device(): across = keep(lax.ppermute(own, both, beside))]
where the time goes in v4:
time: 46 us; the launch traced here: 45.8 us
  starting transfers between devices  16.9 us (37%)
  Pallas kernels  13.6 us (30%)
  waiting for transfers between devices  7.45 us (16%)
  blocking collectives  7.07 us (15%)
  between operations  0.68 us (1%)
    all_to_all x1, starting transfers between devices, on_device(): got = keep(lax.all_to_all(sent, both, 0, 0, axis_index_groups=planes))  10.3 us
    all_to_all x1, blocking collectives, on_device(): back = keep(lax.all_to_all(grad, both, 0, 0, axis_index_groups=quads))  7.07 us
    ppermute x1, starting transfers between devices, on_device(): across = keep(lax.ppermute(own, both, beside))  6.58 us
    all_to_all x1, waiting for transfers between devices, on_device(): got = keep(lax.all_to_all(sent, both, 0, 0, axis_index_groups=planes))  6.26 us
    pallas_call x1, Pallas kernels, on_device(): pl.pallas_call(force_kernel, out_shape=(near(4, 8, 128),) + kept, in_spec...  6.06 us
    pallas_call x1, Pallas kernels, on_device(): pl.pallas_call(early_kernel, out_shape=(near(2, 16, 128),) + kept, in_spe...  3.31 us
    pallas_call x1, Pallas kernels, on_device(): pl.pallas_call(pack_kernel, out_shape=shape(32, 8, 128), in_specs=[VM] *...  1.97 us
    pallas_call x1, Pallas kernels, on_device(): pl.pallas_call(forms_kernel, out_shape=(near(2, 384, 384, dtype=BF16), ne...  1.52 us
  transfers between devices with their start and end apart: 2, of which 2 were waited for; matrix products, arithmetic and copies ran while one was open for 0% of the time, Pallas kernels for 3%

profile of v4, /device:TPU:1, one launch (start us, length us, event | category | flops | bytes accessed | tf_op | source)
XLA Modules:
  0.0 45.8 jit_solution(10449037268262850543)
XLA Ops:
  0.6 2.0 %pack.1.sent = f32[32,8,128]{2,1,0:T(8,128)} custom-call(bf16[4,2,128,96]{3,2,1,0:T(8,128)(2,1)} %constant.2.clone.table, f32[3,4,64]{2,1,0:T(4,128)} %bitcast.7, f32[3,4,64]{2,1,0:T(4,128)} %bitcast.8, f32[3,4,64]{2,1,0:T(4,128)} %bitcast.9, s32[1,64]{1,0:T(1,128)} %bitcast.10, s32[4,4,64]{2,1,0:T(4,128)} %nbr.1, s32[4,64]{1,0:T(4,128)} %counts.1, ...), custom_call_target="tpu_custom_call" | custom-call | tf_op jit(solution)/shard_map/pack/pallas_call | solution.py:561
  2.6 10.3 %all-to-all-start = ((f32[32,8,128]{2,1,0:T(8,128)}), f32[32,8,128]{2,1,0:T(8,128)S(1)}, u32[]{:S(2)}, u32[]{:S(2)}) async-start(f32[32,8,128]{2,1,0:T(8,128)} %pack.1.sent), calls=%async_computation | async-start | bytes 262144 | tf_op jit(solution)/shard_map/all_to_all | solution.py:564
  13.0 1.5 %forms.1 = (bf16[2,384,384]{2,1,0:T(8,128)(2,1)S(1)}, bf16[2,128,1152]{2,1,0:T(8,128)(2,1)S(1)}, bf16[2,128,384]{2,1,0:T(8,128)(2,1)S(1)}, f32[4,128,128]{2,1,0:...) custom-call(f32[32,8,128]{2,1,0:T(8,128)} %pack.1.sent, ...), custom_call_target="tpu_custom_call" | custom-call | flops 2000000000 | bytes 4000000 | tf_op jit(solution)/shard_map/forms/pallas_call | solution.py:565
  14.5 6.3 %all-to-all-done.got = f32[32,8,128]{2,1,0:T(8,128)S(1)} async-done(((f32[32,8,128]{2,1,0:T(8,128)}), f32[32,8,128]{2,1,0:T(8,128)S(1)}, u32[]{:S(2)}, u32[]{:S(2)}) %all-to-all-start) | async-done | bytes 131104 | tf_op jit(solution)/shard_map/all_to_all | solution.py:564
  20.7 0.1 modes.1
  20.8 3.3 %early.1 = (f32[2,16,128]{2,1,0:T(8,128)S(1)}, bf16[6,256,512]{2,1,0:T(8,128)(2,1)S(1)}, f32[6,4,8,128]{3,2,1,0:T(8,128)S(1)}, f32[6,4,16,128]{3,2,1,0:T(8,128)S...) custom-call(f32[4,16,128]{2,1,0:T(8,128)S(1)} %get-tuple-element.35., ...), custom_call_target="tpu_custom_call", output_to_operand_aliasing={{0}: (9, {})} | custom-call | tf_op jit(solution)/shard_map/early/pallas_call | solution.py:600
  24.2 6.6 %collective-permute-start = (f32[2,16,128]{2,1,0:T(8,128)S(1)}, f32[2,16,128]{2,1,0:T(8,128)S(1)}, u32[]{:S(2)}, u32[]{:S(2)}) collective-permute-start(f32[2,16,128]{2,1,0:T(8,128)S(1)} %get-tuple-element.45), channel_id=1, source_target_pairs={{0,126},{126,0},{1,127},{127,1},{2,124},{124,2},{3,125},{125,3},{8... | collective-permute-start | bytes 49160 | tf_op jit(solution)/shard_map/ppermute | solution.py:610
  30.8 1.2 %collective-permute-done.across = f32[2,16,128]{2,1,0:T(8,128)S(1)} collective-permute-done((f32[2,16,128]{2,1,0:T(8,128)S(1)}, f32[2,16,128]{2,1,0:T(8,128)S(1)}, u32[]{:S(2)}, u32[]{:S(2)}) %collective-permute-start) | collective-permute-done | bytes 16416 | tf_op jit(solution)/shard_map/ppermute | solution.py:610
  32.0 6.1 %force.1 = (f32[4,8,128]{2,1,0:T(8,128)S(1)}, bf16[6,256,512]{2,1,0:T(8,128)(2,1)S(1)}, f32[6,4,8,128]{3,2,1,0:T(8,128)S(1)}, f32[6,4,16,128]{3,2,1,0:T(8,128)S(...) custom-call(f32[4,16,128]{2,1,0:T(8,128)S(1)} %get-tuple-element.35., ...), custom_call_target="tpu_custom_call", output_to_operand_aliasing={{1}: (11, {}), {2}: (12, {}), {3}: (13, {}), {4}: (14, {}),... | custom-call | tf_op jit(solution)/shard_map/force/pallas_call | solution.py:622
  38.0 7.1 %all_to_all.10.got = f32[4,8,128]{2,1,0:T(8,128)S(1)} all-to-all(f32[4,8,128]{2,1,0:T(8,128)S(1)} %get-tuple-element.63), channel_id=1, replica_groups={{0,1,2,3},{4,5,6,7},{8,9,10,11},{12,13,14,15},{16,17,18,19},{20,21,22,2..., dimensions={0} | all-to-all | bytes 32768 | tf_op jit(solution)/shard_map/all_to_all | solution.py:632
  45.1 0.7 %finish.1 = (f32[3,4,64]{2,1,0:T(4,128)}, f32[3,4,64]{2,1,0:T(4,128)}, f32[3,4,64]{2,1,0:T(4,128)}) custom-call(f32[4,8,128]{2,1,0:T(8,128)S(1)} %all_to_all.10.got), custom_call_target="tpu_custom_call" | custom-call | tf_op jit(solution)/shard_map/finish/pallas_call | solution.py:633
  (1 shorter events, 0.0 us)
Async XLA Ops:
  2.6 18.1 %all-to-all-start = ((f32[32,8,128]{2,1,0:T(8,128)}), f32[32,8,128]{2,1,0:T(8,128)S(1)}, u32[]{:S(2)}, u32[]{:S(2)}) async-start(f32[32,8,128]{2,1,0:T(8,128)} %pack.1.sent), calls=%async_computation | async-start | bytes 262144 | tf_op jit(solution)/shard_map/all_to_all | solution.py:564
  24.2 7.8 %collective-permute-start = (f32[2,16,128]{2,1,0:T(8,128)S(1)}, f32[2,16,128]{2,1,0:T(8,128)S(1)}, u32[]{:S(2)}, u32[]{:S(2)}) collective-permute-start(f32[2,16,128]{2,1,0:T(8,128)S(1)} %get-tuple-element.45), channel_id=1, source_target_pairs={{0,126},{126,0},{1,127},{127,1},{2,124},{124,2},{3,125},{125,3},{8... | collective-permute-start | bytes 49160 | tf_op jit(solution)/shard_map/ppermute | solution.py:610

commit v5 on v4

--- a/solution.py
+++ b/solution.py
@@ -151,7 +151,7 @@
     own[...] = packed[pl.ds(2 * side, 2)]
 
 
-ORDER = ((0, 0), (0, 1), (1, 0), (2, 0), (0, 2), (1, 1), (2, 1), (3, 0), (1, 2), (2, 2), (3, 1), (3, 2))
+ORDER = ((0, 0), (0, 1), (1, 0), (2, 0), (1, 1), (3, 0), (2, 1), (3, 1))
 
 
 def rates():
@@ -179,7 +179,7 @@
     return 1.0 / (1.0 + jnp.exp(-v))
 
 
-def layer_one(pk, tiles, weights, hot, ys, gp, mom_one, slope_one, u_two):
+def layer_one(pk, jobs, weights, hot, ys, gp, mom_one, slope_one, u_two):
     w_one_cat, mix1_t, prj_t, base_col, step_col = weights
     low = lanes(8) < 64
     low1 = lanes(1) < 64
@@ -187,20 +187,39 @@
     rate = rates()
     spot = lax.broadcasted_iota(jnp.int32, (256, 128), 0).astype(F32)
     ghost_spot = lax.broadcasted_iota(jnp.int32, (32, 128), 0).astype(F32) + 64.0
-    def one(t):
-        here = pk[t + 1, 0:8]
-        info = pk[t + 1, 8:16]
-        beside = jnp.where(low, pk[t + 2, 0:8], pk[t, 0:8])
-        wide = jnp.concatenate([here, beside], axis=1)
+
+    def thirds(wide):
         a = wide.astype(BF16).astype(F32)
         b = (wide - a).astype(BF16).astype(F32)
         c = (wide - a - b).astype(BF16).astype(F32)
-        parts = jnp.concatenate([a, b, c, jnp.zeros((8, 256), F32)], axis=0).astype(BF16)
-        g_prev, g_here, g_next = pk[t, 14:15], info[6:7], pk[t + 2, 14:15]
+        return jnp.concatenate([a, b, c, jnp.zeros((8, 256), F32)], axis=0)
+
+    def one(job):
+        whole = not isinstance(job, tuple)
+        lower, upper, t, outer, mask = (job, job, job, None, None) if whole else job
+
+        def put(ref, at, value):
+            if mask is not None:
+                rows = value.shape[0]
+                mine = jnp.where(lanes(rows) < 64, 0, 1) == mask
+                value = jnp.where(mine, value, ref[at].astype(F32))
+            ref[at] = value.astype(ref.dtype)
+
+        here_low, info = pk[lower + 1, 0:8], pk[lower + 1, 8:16]
+        g_prev, g_low, g_high, g_next = (pk[n, 14:15] for n in (lower, lower + 1, upper + 1, upper + 2))
+        beside = jnp.where(low, pk[upper + 2, 0:8], pk[lower, 0:8])
+        parts = thirds(jnp.concatenate([here_low, beside], axis=1))
+        here = here_low
+        if not whole:
+            here_high = pk[upper + 1, 0:8]
+            here = jnp.where(low, here_low, here_high)
+            info = jnp.where(low, info, pk[upper + 1, 8:16])
+            parts = jnp.concatenate([parts, thirds(jnp.concatenate([here_high, beside], axis=1))], axis=0)
+        parts = parts.astype(BF16)
         table = jnp.concatenate(
             [
-                jnp.where(head, turn(g_prev) + 192.0, turn(g_here) + 64.0),
-                jnp.where(head, g_here, g_next + 128.0),
+                jnp.where(head, turn(g_prev) + 192.0, turn(g_low) + 64.0),
+                jnp.where(head, g_high, g_next + 128.0),
                 jnp.zeros((14, 128), F32),
             ],
             axis=0,
@@ -214,10 +233,12 @@
             n = jnp.where(
                 e < 64.0, e + jnp.where(low1, 0.0, 64.0), jnp.where(low1, far[0:1], far[1:2])
             )
-            one_hot = jnp.where(spot == n, 1.0, 0.0).astype(BF16)
-            hot[t, :, k * 128 : (k + 1) * 128] = one_hot
-            got = dot(parts, one_hot)
+            one_hot = jnp.where(spot == n, 1.0, 0.0)
+            put(hot, (t, slice(None), slice(k * 128, (k + 1) * 128)), one_hot)
+            got = dot(parts, one_hot.astype(BF16))
             there = got[0:8] + (got[8:16] + got[16:24])
+            if not whole:
+                there = jnp.where(low, there, got[32:40] + (got[40:48] + got[48:56]))
             off = there - here
             x, y, z = off[0:1], off[1:2], off[2:3]
             q = x * x + y * y + z * z
@@ -228,8 +249,8 @@
                 None, x, y, z, ROOT3 * x * y, ROOT3 * y * z, 0.5 * (3.0 * z * z - q), ROOT3 * x * z,
                 (0.5 * ROOT3) * (x * x - y * y),
             ]
-            gp[t, k] = both
-            ys[t, k] = jnp.concatenate(harmonic[1:9], axis=0)
+            put(gp, (t, k), both)
+            put(ys, (t, k), jnp.concatenate(harmonic[1:9], axis=0))
             for l in range(9):
                 term = both if l == 0 else harmonic[l] * both
                 sums[l] = term if sums[l] is None else sums[l] + term
@@ -239,7 +260,7 @@
         yield
         m = [moments[:, l * 128 : (l + 1) * 128] for l in range(9)]
         for l in range(9):
-            mom_one[t, l] = m[l]
+            put(mom_one, (t, l), m[l])
         inv = jnp.concatenate(
             [m[0] * m[0], sum(m[l] * m[l] for l in (1, 2, 3)), sum(m[l] * m[l] for l in range(4, 9))],
             axis=0,
@@ -247,12 +268,15 @@
         v = dot3(mix1_t, inv)
         yield
         sig = sigmoid(v)
-        slope_one[t] = sig * (1.0 + v * (1.0 - sig))
+        put(slope_one, (t,), sig * (1.0 + v * (1.0 - sig)))
         h = base_col + here[3:4] * step_col + v * sig
-        u_two[t] = dot3(prj_t, h)
+        u = dot3(prj_t, h)
+        put(u_two, (t,), u)
+        if outer is not None:
+            u_two[outer] = u
         yield
 
-    abreast([one(t) for t in tiles])
+    abreast([one(job) for job in jobs])
 
 
 def forms_kernel(
@@ -366,27 +390,39 @@
     du_two[t - 1] += jnp.where(low_wide, 0.0, aside)
 
 
+def layer_two(
+    tiles, hot, ys, gp, u_two, mix_back, mix_fwd, columns, second_cat, second_parts,
+    tk, gk, rk, v_one, v_two, dinv, du_two, dvec,
+):
+    inv = {}
+    for stage, m in ORDER:
+        t = tiles[m]
+        if stage == 0:
+            nodes_of_edges(t, m, hot, gp, u_two, second_cat, tk, gk, rk)
+        elif stage == 1:
+            inv[m] = invariants_two(t, m, ys, tk, v_one, v_two)
+        elif stage == 2:
+            mixing_back(m, inv[m], mix_back, mix_fwd, columns, dinv)
+        else:
+            edges_back(t, m, hot, ys, gp, second_parts, tk, gk, rk, v_one, v_two, dinv, du_two, dvec)
+
+
 def plane_work(
     packed, forms, hot, ys, gp, mom_one, slope_one, u_two, du_two, dvec,
     pk, tk, gk, rk, v_one, v_two, dinv,
 ):
     mix_back, mix_fwd, prj_all, columns, first_cat, first_parts, second_cat, second_parts = forms
     _, side, _ = whereabouts()
-    first = 2 * (1 - side)
-    for t in range(2):
-        pk[t] = packed[0]
-        pk[6 + t] = packed[3]
-    pk[pl.ds(first + 1, 4)] = packed[...]
+    pk[pl.ds(3 - 2 * side, 4)] = packed[...]
     weights = (first_cat[...], mix_fwd[0], prj_all[1], columns[0], columns[1])
-    start = 3 * (1 - side)
-    layer_one(pk, [start + i for i in range(3)], weights, hot, ys, gp, mom_one, slope_one, u_two)
-
+    start = 3 - 2 * side
+    halves = (5 - 2 * side, 2 - 2 * side, 2 + side, 5 - 5 * side, None)
+    layer_one(pk, [start, start + 1, halves], weights, hot, ys, gp, mom_one, slope_one, u_two)
     du_two[...] = jnp.zeros_like(du_two)
-    t = start + 1
-    nodes_of_edges(t, 0, hot, gp, u_two, second_cat, tk, gk, rk)
-    inv = invariants_two(t, 0, ys, tk, v_one, v_two)
-    mixing_back(0, inv, mix_back, mix_fwd, columns, dinv)
-    edges_back(t, 0, hot, ys, gp, second_parts, tk, gk, rk, v_one, v_two, dinv, du_two, dvec)
+    layer_two(
+        [start, start + 1], hot, ys, gp, u_two, mix_back, mix_fwd, columns, second_cat, second_parts,
+        tk, gk, rk, v_one, v_two, dinv, du_two, dvec,
+    )
 
 
 def is_early(s):
@@ -414,33 +450,16 @@
     out, hot, ys, gp, mom_one, slope_one, u_two, du_two, dvec, pk, tk, gk, rk, v_one, v_two, dinv = refs[16:]
     _, side, _ = whereabouts()
     low = lanes(8) < 64
-    first = 2 * (1 - side)
-    other = 4 * side
-    pk[0] = across[0]
-    pk[7] = across[1]
-    pk[pl.ds(first + 1, 4)] = packed[...]
-    pk[pl.ds(other + 1, 2)] = across[...]
+    pk[pl.ds(3 - 2 * side, 4)] = packed[...]
+    pk[pl.ds(4 * side + 1, 2)] = across[...]
     weights = (first_cat[...], mix_fwd[0], prj_all[1], columns[0], columns[1])
-    start = 3 * side
-    layer_one(pk, [start + i for i in range(3)], weights, hot, ys, gp, mom_one, slope_one, u_two)
+    halves = (2 + 3 * side, 3 * side, 2 + side, 5 * side, side)
+    layer_one(pk, [1 + 3 * side, halves], weights, hot, ys, gp, mom_one, slope_one, u_two)
+    layer_two(
+        [1 + 2 * side, 2 + 2 * side], hot, ys, gp, u_two, mix_back, mix_fwd, columns, second_cat, second_parts,
+        tk, gk, rk, v_one, v_two, dinv, du_two, dvec,
+    )
     rate = rates()
-
-    turns = [side + 1 + i for i in range(3)]
-    inv = {}
-
-    def stage(n, m):
-        t = turns[m]
-        if n == 0:
-            nodes_of_edges(t, m, hot, gp, u_two, second_cat, tk, gk, rk)
-        elif n == 1:
-            inv[m] = invariants_two(t, m, ys, tk, v_one, v_two)
-        elif n == 2:
-            mixing_back(m, inv[m], mix_back, mix_fwd, columns, dinv)
-        else:
-            edges_back(t, m, hot, ys, gp, second_parts, tk, gk, rk, v_one, v_two, dinv, du_two, dvec)
-
-    for n, m in ORDER:
-        stage(n, m)
 
     def third(du, slope, mom, gs, harmonics, pushes, spots):
         dh = columns[3] + dot3(prj_all[0], du)
@@ -594,15 +613,15 @@
         near(TILES, 4, 8, 128),
     )
 
-    def scratch(n):
-        return [near(8, 16, 128)] + [near(n, 4, 128, 128)] * 5 + [near(n, 384, 128)]
+    def scratch():
+        return [near(8, 16, 128)] + [near(2, 4, 128, 128)] * 5 + [near(2, 384, 128)]
 
     own, *state = pl.pallas_call(
         early_kernel,
         out_shape=(near(2, 16, 128),) + kept,
         in_specs=[VM] * 10,
         out_specs=(VM,) * 9,
-        scratch_shapes=scratch(1),
+        scratch_shapes=scratch(),
         input_output_aliases={9: 0},
         compiler_params=room(24),
         name="early",
@@ -613,7 +632,7 @@
         out_shape=kept,
         in_specs=[VM] * 17,
         out_specs=(VM,) * 8,
-        scratch_shapes=scratch(1),
+        scratch_shapes=scratch(),
         input_output_aliases={9 + i: i for i in range(8)},
         compiler_params=room(24),
         cost_estimate=pl.CostEstimate(flops=4_000_000_000, bytes_accessed=8_000_000, transcendentals=0),
@@ -624,7 +643,7 @@
         out_shape=(near(4, 8, 128),) + kept,
         in_specs=[VM] * 19,
         out_specs=(VM,) * 9,
-        scratch_shapes=scratch(3),
+        scratch_shapes=scratch(),
         input_output_aliases={11 + i: 1 + i for i in range(8)},
         compiler_params=room(24),
         name="force",

time: 46 us -> 46 us (level)
  waiting for transfers between devices: 7.45 us -> 8.19 us
  starting transfers between devices: 16.9 us -> 16.2 us
    pallas_call x1, Pallas kernels: 6.06 us -> 5.3 us  [on_device(): pl.pallas_call(force_kernel, out_shape=(near(4, 8, 128),) + kept, in_spec...]
    pallas_call x1, Pallas kernels: 3.31 us -> 4.05 us  [on_device(): pl.pallas_call(early_kernel, out_shape=(near(2, 16, 128),) + kept, in_spe...]
    ppermute x1, starting transfers between devices: 6.58 us -> 5.85 us  [on_device(): across = keep(lax.ppermute(own, both, beside))]
    ppermute x1, waiting for transfers between devices: 1.19 us -> 1.92 us  [on_device(): across = keep(lax.ppermute(own, both, beside))]
where the time goes in v5:
time: 46 us; the launch traced here: 45.7 us
  starting transfers between devices  16.2 us (35%)
  Pallas kernels  13.6 us (30%)
  waiting for transfers between devices  8.19 us (18%)
  blocking collectives  7.07 us (15%)
  between operations  0.68 us (1%)
    all_to_all x1, starting transfers between devices, on_device(): got = keep(lax.all_to_all(sent, both, 0, 0, axis_index_groups=planes))  10.3 us
    all_to_all x1, blocking collectives, on_device(): back = keep(lax.all_to_all(grad, both, 0, 0, axis_index_groups=quads))  7.07 us
    all_to_all x1, waiting for transfers between devices, on_device(): got = keep(lax.all_to_all(sent, both, 0, 0, axis_index_groups=planes))  6.26 us
    ppermute x1, starting transfers between devices, on_device(): across = keep(lax.ppermute(own, both, beside))  5.85 us
    pallas_call x1, Pallas kernels, on_device(): pl.pallas_call(force_kernel, out_shape=(near(4, 8, 128),) + kept, in_spec...  5.3 us
    pallas_call x1, Pallas kernels, on_device(): pl.pallas_call(early_kernel, out_shape=(near(2, 16, 128),) + kept, in_spe...  4.05 us
    pallas_call x1, Pallas kernels, on_device(): pl.pallas_call(pack_kernel, out_shape=shape(32, 8, 128), in_specs=[VM] *...  1.97 us
    ppermute x1, waiting for transfers between devices, on_device(): across = keep(lax.ppermute(own, both, beside))  1.92 us
  transfers between devices with their start and end apart: 2, of which 2 were waited for; matrix products, arithmetic and copies ran while one was open for 0% of the time, Pallas kernels for 3%

profile of v5, /device:TPU:1, one launch (start us, length us, event | category | flops | bytes accessed | tf_op | source)
XLA Modules:
  0.0 45.7 jit_solution(14266528457395347362)
XLA Ops:
  0.6 2.0 %pack.1.sent = f32[32,8,128]{2,1,0:T(8,128)} custom-call(bf16[4,2,128,96]{3,2,1,0:T(8,128)(2,1)} %constant.2.clone.table, f32[3,4,64]{2,1,0:T(4,128)} %bitcast.7, f32[3,4,64]{2,1,0:T(4,128)} %bitcast.8, f32[3,4,64]{2,1,0:T(4,128)} %bitcast.9, s32[1,64]{1,0:T(1,128)} %bitcast.10, s32[4,4,64]{2,1,0:T(4,128)} %nbr.1, s32[4,64]{1,0:T(4,128)} %counts.1, ...), custom_call_target="tpu_custom_call" | custom-call | tf_op jit(solution)/shard_map/pack/pallas_call | solution.py:580
  2.6 10.3 %all-to-all-start = ((f32[32,8,128]{2,1,0:T(8,128)}), f32[32,8,128]{2,1,0:T(8,128)S(1)}, u32[]{:S(2)}, u32[]{:S(2)}) async-start(f32[32,8,128]{2,1,0:T(8,128)} %pack.1.sent), calls=%async_computation | async-start | bytes 262144 | tf_op jit(solution)/shard_map/all_to_all | solution.py:583
  13.0 1.5 %forms.1 = (bf16[2,384,384]{2,1,0:T(8,128)(2,1)S(1)}, bf16[2,128,1152]{2,1,0:T(8,128)(2,1)S(1)}, bf16[2,128,384]{2,1,0:T(8,128)(2,1)S(1)}, f32[4,128,128]{2,1,0:...) custom-call(f32[32,8,128]{2,1,0:T(8,128)} %pack.1.sent, ...), custom_call_target="tpu_custom_call" | custom-call | flops 2000000000 | bytes 4000000 | tf_op jit(solution)/shard_map/forms/pallas_call | solution.py:584
  14.5 6.3 %all-to-all-done.got = f32[32,8,128]{2,1,0:T(8,128)S(1)} async-done(((f32[32,8,128]{2,1,0:T(8,128)}), f32[32,8,128]{2,1,0:T(8,128)S(1)}, u32[]{:S(2)}, u32[]{:S(2)}) %all-to-all-start) | async-done | bytes 131104 | tf_op jit(solution)/shard_map/all_to_all | solution.py:583
  20.7 0.1 modes.1
  20.8 4.0 %early.1 = (f32[2,16,128]{2,1,0:T(8,128)S(1)}, bf16[6,256,512]{2,1,0:T(8,128)(2,1)S(1)}, f32[6,4,8,128]{3,2,1,0:T(8,128)S(1)}, f32[6,4,16,128]{3,2,1,0:T(8,128)S...) custom-call(f32[4,16,128]{2,1,0:T(8,128)S(1)} %get-tuple-element.35., ...), custom_call_target="tpu_custom_call", output_to_operand_aliasing={{0}: (9, {})} | custom-call | tf_op jit(solution)/shard_map/early/pallas_call | solution.py:619
  24.9 5.8 %collective-permute-start = (f32[2,16,128]{2,1,0:T(8,128)S(1)}, f32[2,16,128]{2,1,0:T(8,128)S(1)}, u32[]{:S(2)}, u32[]{:S(2)}) collective-permute-start(f32[2,16,128]{2,1,0:T(8,128)S(1)} %get-tuple-element.45), channel_id=1, source_target_pairs={{0,126},{126,0},{1,127},{127,1},{2,124},{124,2},{3,125},{125,3},{8... | collective-permute-start | bytes 49160 | tf_op jit(solution)/shard_map/ppermute | solution.py:629
  30.8 1.9 %collective-permute-done.across = f32[2,16,128]{2,1,0:T(8,128)S(1)} collective-permute-done((f32[2,16,128]{2,1,0:T(8,128)S(1)}, f32[2,16,128]{2,1,0:T(8,128)S(1)}, u32[]{:S(2)}, u32[]{:S(2)}) %collective-permute-start) | collective-permute-done | bytes 16416 | tf_op jit(solution)/shard_map/ppermute | solution.py:629
  32.7 5.3 %force.1 = (f32[4,8,128]{2,1,0:T(8,128)S(1)}, bf16[6,256,512]{2,1,0:T(8,128)(2,1)S(1)}, f32[6,4,8,128]{3,2,1,0:T(8,128)S(1)}, f32[6,4,16,128]{3,2,1,0:T(8,128)S(...) custom-call(f32[4,16,128]{2,1,0:T(8,128)S(1)} %get-tuple-element.35., ...), custom_call_target="tpu_custom_call", output_to_operand_aliasing={{1}: (11, {}), {2}: (12, {}), {3}: (13, {}), {4}: (14, {}),... | custom-call | tf_op jit(solution)/shard_map/force/pallas_call | solution.py:641
  38.0 7.1 %all_to_all.10.got = f32[4,8,128]{2,1,0:T(8,128)S(1)} all-to-all(f32[4,8,128]{2,1,0:T(8,128)S(1)} %get-tuple-element.63), channel_id=1, replica_groups={{0,1,2,3},{4,5,6,7},{8,9,10,11},{12,13,14,15},{16,17,18,19},{20,21,22,2..., dimensions={0} | all-to-all | bytes 32768 | tf_op jit(solution)/shard_map/all_to_all | solution.py:651
  45.1 0.7 %finish.1 = (f32[3,4,64]{2,1,0:T(4,128)}, f32[3,4,64]{2,1,0:T(4,128)}, f32[3,4,64]{2,1,0:T(4,128)}) custom-call(f32[4,8,128]{2,1,0:T(8,128)S(1)} %all_to_all.10.got), custom_call_target="tpu_custom_call" | custom-call | tf_op jit(solution)/shard_map/finish/pallas_call | solution.py:652
  (1 shorter events, 0.0 us)
Async XLA Ops:
  2.6 18.1 %all-to-all-start = ((f32[32,8,128]{2,1,0:T(8,128)}), f32[32,8,128]{2,1,0:T(8,128)S(1)}, u32[]{:S(2)}, u32[]{:S(2)}) async-start(f32[32,8,128]{2,1,0:T(8,128)} %pack.1.sent), calls=%async_computation | async-start | bytes 262144 | tf_op jit(solution)/shard_map/all_to_all | solution.py:583
  24.9 7.8 %collective-permute-start = (f32[2,16,128]{2,1,0:T(8,128)S(1)}, f32[2,16,128]{2,1,0:T(8,128)S(1)}, u32[]{:S(2)}, u32[]{:S(2)}) collective-permute-start(f32[2,16,128]{2,1,0:T(8,128)S(1)} %get-tuple-element.45), channel_id=1, source_target_pairs={{0,126},{126,0},{1,127},{127,1},{2,124},{124,2},{3,125},{125,3},{8... | collective-permute-start | bytes 49160 | tf_op jit(solution)/shard_map/ppermute | solution.py:629

commit v6 on v5

--- a/solution.py
+++ b/solution.py
@@ -407,21 +407,23 @@
             edges_back(t, m, hot, ys, gp, second_parts, tk, gk, rk, v_one, v_two, dinv, du_two, dvec)
 
 
-def plane_work(
-    packed, forms, hot, ys, gp, mom_one, slope_one, u_two, du_two, dvec,
-    pk, tk, gk, rk, v_one, v_two, dinv,
-):
-    mix_back, mix_fwd, prj_all, columns, first_cat, first_parts, second_cat, second_parts = forms
+def plane_first(packed, forms, pk, *state):
+    mix_fwd, prj_all, columns, first_cat = forms[1:5]
     _, side, _ = whereabouts()
     pk[pl.ds(3 - 2 * side, 4)] = packed[...]
     weights = (first_cat[...], mix_fwd[0], prj_all[1], columns[0], columns[1])
     start = 3 - 2 * side
     halves = (5 - 2 * side, 2 - 2 * side, 2 + side, 5 - 5 * side, None)
-    layer_one(pk, [start, start + 1, halves], weights, hot, ys, gp, mom_one, slope_one, u_two)
+    layer_one(pk, [start, start + 1, halves], weights, *state)
+
+
+def plane_second(forms, hot, ys, gp, u_two, du_two, dvec, *scratch):
+    mix_back, mix_fwd, _, columns, _, _, second_cat, second_parts = forms
+    _, side, _ = whereabouts()
     du_two[...] = jnp.zeros_like(du_two)
     layer_two(
-        [start, start + 1], hot, ys, gp, u_two, mix_back, mix_fwd, columns, second_cat, second_parts,
-        tk, gk, rk, v_one, v_two, dinv, du_two, dvec,
+        [3 - 2 * side, 4 - 2 * side], hot, ys, gp, u_two, mix_back, mix_fwd, columns, second_cat, second_parts,
+        *scratch, du_two, dvec,
     )
 
 
@@ -430,19 +432,22 @@
 
 
 def early_kernel(packed, *refs):
-    forms, rest = refs[0:8], refs[10:]
+    forms, state, pk = refs[0:8], refs[10:16], refs[16]
 
     @pl.when(is_early(whereabouts()[2]))
     def _():
-        plane_work(packed, forms, *rest)
+        plane_first(packed, forms, pk, *state)
 
 
 def late_kernel(packed, *refs):
-    forms, rest = refs[0:8], refs[16:]
+    forms = refs[0:8]
+    hot, ys, gp, mom_one, slope_one, u_two, du_two, dvec, pk = refs[14:23]
 
     @pl.when(jnp.logical_not(is_early(whereabouts()[2])))
     def _():
-        plane_work(packed, forms, *rest)
+        plane_first(packed, forms, pk, hot, ys, gp, mom_one, slope_one, u_two)
+
+    plane_second(forms, hot, ys, gp, u_two, du_two, dvec, *refs[23:])
 
 
 def force_kernel(packed, across, moment, *refs):
@@ -618,10 +623,10 @@
 
     own, *state = pl.pallas_call(
         early_kernel,
-        out_shape=(near(2, 16, 128),) + kept,
+        out_shape=(near(2, 16, 128),) + kept[:6],
         in_specs=[VM] * 10,
-        out_specs=(VM,) * 9,
-        scratch_shapes=scratch(),
+        out_specs=(VM,) * 7,
+        scratch_shapes=[near(8, 16, 128)],
         input_output_aliases={9: 0},
         compiler_params=room(24),
         name="early",
@@ -630,10 +635,10 @@
     state = pl.pallas_call(
         late_kernel,
         out_shape=kept,
-        in_specs=[VM] * 17,
+        in_specs=[VM] * 15,
         out_specs=(VM,) * 8,
         scratch_shapes=scratch(),
-        input_output_aliases={9 + i: i for i in range(8)},
+        input_output_aliases={9 + i: i for i in range(6)},
         compiler_params=room(24),
         cost_estimate=pl.CostEstimate(flops=4_000_000_000, bytes_accessed=8_000_000, transcendentals=0),
         name="late",

time: 46 us -> 45.4 us (0.987)
  starting transfers between devices: 16.2 us -> 18.5 us
  waiting for transfers between devices: 8.19 us -> 6.27 us
  blocking collectives: 7.07 us -> 6.21 us
    ppermute x1, starting transfers between devices: 5.85 us -> 8.14 us  [on_device(): across = keep(lax.ppermute(own, both, beside))]
    ppermute x1, waiting for transfers between devices: 1.92 us -> 0.01 us  [on_device(): across = keep(lax.ppermute(own, both, beside))]
    all_to_all x1, blocking collectives: 7.07 us -> 6.21 us  [on_device(): back = keep(lax.all_to_all(grad, both, 0, 0, axis_index_groups=quads))]
  transfers between devices with their start and end apart: 2 -> 2, of which waited for: 2 -> 1; matrix products, arithmetic and copies ran while one was open for 0% -> 0% of each run, Pallas kernels for 3% -> 8%
where the time goes in v6:
time: 45.4 us; the launch traced here: 45.2 us
  starting transfers between devices  18.5 us (41%)
  Pallas kernels  13.5 us (30%)
  waiting for transfers between devices  6.27 us (14%)
  blocking collectives  6.21 us (14%)
  between operations  0.69 us (2%)
    all_to_all x1, starting transfers between devices, on_device(): got = keep(lax.all_to_all(sent, both, 0, 0, axis_index_groups=planes))  10.3 us
    ppermute x1, starting transfers between devices, on_device(): across = keep(lax.ppermute(own, both, beside))  8.14 us
    all_to_all x1, waiting for transfers between devices, on_device(): got = keep(lax.all_to_all(sent, both, 0, 0, axis_index_groups=planes))  6.26 us
    all_to_all x1, blocking collectives, on_device(): back = keep(lax.all_to_all(grad, both, 0, 0, axis_index_groups=quads))  6.21 us
    pallas_call x1, Pallas kernels, on_device(): pl.pallas_call(force_kernel, out_shape=(near(4, 8, 128),) + kept, in_spec...  5.25 us
    pallas_call x1, Pallas kernels, on_device(): pl.pallas_call(late_kernel, out_shape=kept, in_specs=[VM] * 15, out_specs...  2.27 us
    pallas_call x1, Pallas kernels, on_device(): pl.pallas_call(pack_kernel, out_shape=shape(32, 8, 128), in_specs=[VM] *...  1.97 us
    pallas_call x1, Pallas kernels, on_device(): pl.pallas_call(early_kernel, out_shape=(near(2, 16, 128),) + kept[:6], in...  1.75 us
  transfers between devices with their start and end apart: 2, of which 1 were waited for; matrix products, arithmetic and copies ran while one was open for 0% of the time, Pallas kernels for 8%

profile of v6, /device:TPU:1, one launch (start us, length us, event | category | flops | bytes accessed | tf_op | source)
XLA Modules:
  0.0 45.2 jit_solution(12777052124468193033)
XLA Ops:
  0.6 2.0 %pack.1.sent = f32[32,8,128]{2,1,0:T(8,128)} custom-call(bf16[4,2,128,96]{3,2,1,0:T(8,128)(2,1)} %constant.2.clone.table, f32[3,4,64]{2,1,0:T(4,128)} %bitcast.7, f32[3,4,64]{2,1,0:T(4,128)} %bitcast.8, f32[3,4,64]{2,1,0:T(4,128)} %bitcast.9, s32[1,64]{1,0:T(1,128)} %bitcast.10, s32[4,4,64]{2,1,0:T(4,128)} %nbr.1, s32[4,64]{1,0:T(4,128)} %counts.1, ...), custom_call_target="tpu_custom_call" | custom-call | tf_op jit(solution)/shard_map/pack/pallas_call | solution.py:585
  2.6 10.3 %all-to-all-start = ((f32[32,8,128]{2,1,0:T(8,128)}), f32[32,8,128]{2,1,0:T(8,128)S(1)}, u32[]{:S(2)}, u32[]{:S(2)}) async-start(f32[32,8,128]{2,1,0:T(8,128)} %pack.1.sent), calls=%async_computation | async-start | bytes 262144 | tf_op jit(solution)/shard_map/all_to_all | solution.py:588
  13.0 1.5 %forms.1 = (bf16[2,384,384]{2,1,0:T(8,128)(2,1)S(1)}, bf16[2,128,1152]{2,1,0:T(8,128)(2,1)S(1)}, bf16[2,128,384]{2,1,0:T(8,128)(2,1)S(1)}, f32[4,128,128]{2,1,0:...) custom-call(f32[32,8,128]{2,1,0:T(8,128)} %pack.1.sent, ...), custom_call_target="tpu_custom_call" | custom-call | flops 2000000000 | bytes 4000000 | tf_op jit(solution)/shard_map/forms/pallas_call | solution.py:589
  14.5 6.3 %all-to-all-done.got = f32[32,8,128]{2,1,0:T(8,128)S(1)} async-done(((f32[32,8,128]{2,1,0:T(8,128)}), f32[32,8,128]{2,1,0:T(8,128)S(1)}, u32[]{:S(2)}, u32[]{:S(2)}) %all-to-all-start) | async-done | bytes 131104 | tf_op jit(solution)/shard_map/all_to_all | solution.py:588
  20.7 0.1 modes.1
  20.8 1.8 %early.1 = (f32[2,16,128]{2,1,0:T(8,128)S(1)}, bf16[6,256,512]{2,1,0:T(8,128)(2,1)S(1)}, f32[6,4,8,128]{3,2,1,0:T(8,128)S(1)}, f32[6,4,16,128]{3,2,1,0:T(8,128)S...) custom-call(f32[4,16,128]{2,1,0:T(8,128)S(1)} %get-tuple-element.33., ...), custom_call_target="tpu_custom_call", output_to_operand_aliasing={{0}: (9, {})} | custom-call | tf_op jit(solution)/shard_map/early/pallas_call | solution.py:624
  22.6 8.1 %collective-permute-start = (f32[2,16,128]{2,1,0:T(8,128)S(1)}, f32[2,16,128]{2,1,0:T(8,128)S(1)}, u32[]{:S(2)}, u32[]{:S(2)}) collective-permute-start(f32[2,16,128]{2,1,0:T(8,128)S(1)} %get-tuple-element.43), channel_id=1, source_target_pairs={{0,126},{126,0},{1,127},{127,1},{2,124},{124,2},{3,125},{125,3},{8... | collective-permute-start | bytes 49160 | tf_op jit(solution)/shard_map/ppermute | solution.py:634
  30.8 2.3 %late.1 = (bf16[6,256,512]{2,1,0:T(8,128)(2,1)S(1)}, f32[6,4,8,128]{3,2,1,0:T(8,128)S(1)}, f32[6,4,16,128]{3,2,1,0:T(8,128)S(1)}, f32[6,9,128,128]{3,2,1,0:T(8,1...) custom-call(f32[4,16,128]{2,1,0:T(8,128)S(1)} %get-tuple-element.33., ...), custom_call_target="tpu_custom_call", output_to_operand_aliasing={{0}: (9, {}), {1}: (10, {}), {2}: (11, {}), {3}: (12, {}), ... | custom-call | flops 4000000000 | bytes 8000000 | tf_op jit(solution)/shard_map/late/pallas_call | solution.py:635
  33.0 0.0 collective-permute-done.across
  33.0 5.2 %force.1 = (f32[4,8,128]{2,1,0:T(8,128)S(1)}, bf16[6,256,512]{2,1,0:T(8,128)(2,1)S(1)}, f32[6,4,8,128]{3,2,1,0:T(8,128)S(1)}, f32[6,4,16,128]{3,2,1,0:T(8,128)S(...) custom-call(f32[4,16,128]{2,1,0:T(8,128)S(1)} %get-tuple-element.33., ...), custom_call_target="tpu_custom_call", output_to_operand_aliasing={{1}: (11, {}), {2}: (12, {}), {3}: (13, {}), {4}: (14, {}),... | custom-call | tf_op jit(solution)/shard_map/force/pallas_call | solution.py:646
  38.3 6.2 %all_to_all.10.got = f32[4,8,128]{2,1,0:T(8,128)S(1)} all-to-all(f32[4,8,128]{2,1,0:T(8,128)S(1)} %get-tuple-element.59), channel_id=1, replica_groups={{0,1,2,3},{4,5,6,7},{8,9,10,11},{12,13,14,15},{16,17,18,19},{20,21,22,2..., dimensions={0} | all-to-all | bytes 32768 | tf_op jit(solution)/shard_map/all_to_all | solution.py:656
  44.5 0.7 %finish.1 = (f32[3,4,64]{2,1,0:T(4,128)}, f32[3,4,64]{2,1,0:T(4,128)}, f32[3,4,64]{2,1,0:T(4,128)}) custom-call(f32[4,8,128]{2,1,0:T(8,128)S(1)} %all_to_all.10.got), custom_call_target="tpu_custom_call" | custom-call | tf_op jit(solution)/shard_map/finish/pallas_call | solution.py:657
Async XLA Ops:
  2.6 18.1 %all-to-all-start = ((f32[32,8,128]{2,1,0:T(8,128)}), f32[32,8,128]{2,1,0:T(8,128)S(1)}, u32[]{:S(2)}, u32[]{:S(2)}) async-start(f32[32,8,128]{2,1,0:T(8,128)} %pack.1.sent), calls=%async_computation | async-start | bytes 262144 | tf_op jit(solution)/shard_map/all_to_all | solution.py:588
  22.6 10.4 %collective-permute-start = (f32[2,16,128]{2,1,0:T(8,128)S(1)}, f32[2,16,128]{2,1,0:T(8,128)S(1)}, u32[]{:S(2)}, u32[]{:S(2)}) collective-permute-start(f32[2,16,128]{2,1,0:T(8,128)S(1)} %get-tuple-element.43), channel_id=1, source_target_pairs={{0,126},{126,0},{1,127},{127,1},{2,124},{124,2},{3,125},{125,3},{8... | collective-permute-start | bytes 49160 | tf_op jit(solution)/shard_map/ppermute | solution.py:634

commit v7 on v6

--- a/solution.py
+++ b/solution.py
@@ -151,7 +151,7 @@
     own[...] = packed[pl.ds(2 * side, 2)]
 
 
-ORDER = ((0, 0), (0, 1), (1, 0), (2, 0), (1, 1), (3, 0), (2, 1), (3, 1))
+ORDER = ((0, 0), (0, 1), (1, 0), (1, 1), (2, 0), (2, 1), (3, 0), (3, 1))
 
 
 def rates():

time: 45.4 us -> 44.7 us (0.985)
  Pallas kernels: 13.5 us -> 12.8 us
where the time goes in v7:
time: 44.7 us; the launch traced here: 44.4 us
  starting transfers between devices  18.5 us (41%)
  Pallas kernels  12.8 us (29%)
  waiting for transfers between devices  6.27 us (14%)
  blocking collectives  6.2 us (14%)
  between operations  0.69 us (2%)
    all_to_all x1, starting transfers between devices, on_device(): got = keep(lax.all_to_all(sent, both, 0, 0, axis_index_groups=planes))  10.3 us
    ppermute x1, starting transfers between devices, on_device(): across = keep(lax.ppermute(own, both, beside))  8.14 us
    all_to_all x1, waiting for transfers between devices, on_device(): got = keep(lax.all_to_all(sent, both, 0, 0, axis_index_groups=planes))  6.26 us
    all_to_all x1, blocking collectives, on_device(): back = keep(lax.all_to_all(grad, both, 0, 0, axis_index_groups=quads))  6.2 us
    pallas_call x1, Pallas kernels, on_device(): pl.pallas_call(force_kernel, out_shape=(near(4, 8, 128),) + kept, in_spec...  4.96 us
    pallas_call x1, Pallas kernels, on_device(): pl.pallas_call(pack_kernel, out_shape=shape(32, 8, 128), in_specs=[VM] *...  1.97 us
    pallas_call x1, Pallas kernels, on_device(): pl.pallas_call(late_kernel, out_shape=kept, in_specs=[VM] * 15, out_specs...  1.83 us
    pallas_call x1, Pallas kernels, on_device(): pl.pallas_call(early_kernel, out_shape=(near(2, 16, 128),) + kept[:6], in...  1.75 us
  transfers between devices with their start and end apart: 2, of which 1 were waited for; matrix products, arithmetic and copies ran while one was open for 0% of the time, Pallas kernels for 8%

profile of v7, /device:TPU:1, one launch (start us, length us, event | category | flops | bytes accessed | tf_op | source)
XLA Modules:
  0.0 44.4 jit_solution(11892280334979952268)
XLA Ops:
  0.6 2.0 %pack.1.sent = f32[32,8,128]{2,1,0:T(8,128)} custom-call(bf16[4,2,128,96]{3,2,1,0:T(8,128)(2,1)} %constant.2.clone.table, f32[3,4,64]{2,1,0:T(4,128)} %bitcast.7, f32[3,4,64]{2,1,0:T(4,128)} %bitcast.8, f32[3,4,64]{2,1,0:T(4,128)} %bitcast.9, s32[1,64]{1,0:T(1,128)} %bitcast.10, s32[4,4,64]{2,1,0:T(4,128)} %nbr.1, s32[4,64]{1,0:T(4,128)} %counts.1, ...), custom_call_target="tpu_custom_call" | custom-call | tf_op jit(solution)/shard_map/pack/pallas_call | solution.py:585
  2.6 10.3 %all-to-all-start = ((f32[32,8,128]{2,1,0:T(8,128)}), f32[32,8,128]{2,1,0:T(8,128)S(1)}, u32[]{:S(2)}, u32[]{:S(2)}) async-start(f32[32,8,128]{2,1,0:T(8,128)} %pack.1.sent), calls=%async_computation | async-start | bytes 262144 | tf_op jit(solution)/shard_map/all_to_all | solution.py:588
  13.0 1.5 %forms.1 = (bf16[2,384,384]{2,1,0:T(8,128)(2,1)S(1)}, bf16[2,128,1152]{2,1,0:T(8,128)(2,1)S(1)}, bf16[2,128,384]{2,1,0:T(8,128)(2,1)S(1)}, f32[4,128,128]{2,1,0:...) custom-call(f32[32,8,128]{2,1,0:T(8,128)} %pack.1.sent, ...), custom_call_target="tpu_custom_call" | custom-call | flops 2000000000 | bytes 4000000 | tf_op jit(solution)/shard_map/forms/pallas_call | solution.py:589
  14.5 6.3 %all-to-all-done.got = f32[32,8,128]{2,1,0:T(8,128)S(1)} async-done(((f32[32,8,128]{2,1,0:T(8,128)}), f32[32,8,128]{2,1,0:T(8,128)S(1)}, u32[]{:S(2)}, u32[]{:S(2)}) %all-to-all-start) | async-done | bytes 131104 | tf_op jit(solution)/shard_map/all_to_all | solution.py:588
  20.7 0.1 modes.1
  20.8 1.8 %early.1 = (f32[2,16,128]{2,1,0:T(8,128)S(1)}, bf16[6,256,512]{2,1,0:T(8,128)(2,1)S(1)}, f32[6,4,8,128]{3,2,1,0:T(8,128)S(1)}, f32[6,4,16,128]{3,2,1,0:T(8,128)S...) custom-call(f32[4,16,128]{2,1,0:T(8,128)S(1)} %get-tuple-element.33., ...), custom_call_target="tpu_custom_call", output_to_operand_aliasing={{0}: (9, {})} | custom-call | tf_op jit(solution)/shard_map/early/pallas_call | solution.py:624
  22.6 8.1 %collective-permute-start = (f32[2,16,128]{2,1,0:T(8,128)S(1)}, f32[2,16,128]{2,1,0:T(8,128)S(1)}, u32[]{:S(2)}, u32[]{:S(2)}) collective-permute-start(f32[2,16,128]{2,1,0:T(8,128)S(1)} %get-tuple-element.43), channel_id=1, source_target_pairs={{0,126},{126,0},{1,127},{127,1},{2,124},{124,2},{3,125},{125,3},{8... | collective-permute-start | bytes 49160 | tf_op jit(solution)/shard_map/ppermute | solution.py:634
  30.8 1.8 %late.1 = (bf16[6,256,512]{2,1,0:T(8,128)(2,1)S(1)}, f32[6,4,8,128]{3,2,1,0:T(8,128)S(1)}, f32[6,4,16,128]{3,2,1,0:T(8,128)S(1)}, f32[6,9,128,128]{3,2,1,0:T(8,1...) custom-call(f32[4,16,128]{2,1,0:T(8,128)S(1)} %get-tuple-element.33., ...), custom_call_target="tpu_custom_call", output_to_operand_aliasing={{0}: (9, {}), {1}: (10, {}), {2}: (11, {}), {3}: (12, {}), ... | custom-call | flops 4000000000 | bytes 8000000 | tf_op jit(solution)/shard_map/late/pallas_call | solution.py:635
  32.6 0.0 collective-permute-done.across
  32.6 5.0 %force.1 = (f32[4,8,128]{2,1,0:T(8,128)S(1)}, bf16[6,256,512]{2,1,0:T(8,128)(2,1)S(1)}, f32[6,4,8,128]{3,2,1,0:T(8,128)S(1)}, f32[6,4,16,128]{3,2,1,0:T(8,128)S(...) custom-call(f32[4,16,128]{2,1,0:T(8,128)S(1)} %get-tuple-element.33., ...), custom_call_target="tpu_custom_call", output_to_operand_aliasing={{1}: (11, {}), {2}: (12, {}), {3}: (13, {}), {4}: (14, {}),... | custom-call | tf_op jit(solution)/shard_map/force/pallas_call | solution.py:646
  37.6 6.2 %all_to_all.10.got = f32[4,8,128]{2,1,0:T(8,128)S(1)} all-to-all(f32[4,8,128]{2,1,0:T(8,128)S(1)} %get-tuple-element.59), channel_id=1, replica_groups={{0,1,2,3},{4,5,6,7},{8,9,10,11},{12,13,14,15},{16,17,18,19},{20,21,22,2..., dimensions={0} | all-to-all | bytes 32768 | tf_op jit(solution)/shard_map/all_to_all | solution.py:656
  43.8 0.7 %finish.1 = (f32[3,4,64]{2,1,0:T(4,128)}, f32[3,4,64]{2,1,0:T(4,128)}, f32[3,4,64]{2,1,0:T(4,128)}) custom-call(f32[4,8,128]{2,1,0:T(8,128)S(1)} %all_to_all.10.got), custom_call_target="tpu_custom_call" | custom-call | tf_op jit(solution)/shard_map/finish/pallas_call | solution.py:657
Async XLA Ops:
  2.6 18.1 %all-to-all-start = ((f32[32,8,128]{2,1,0:T(8,128)}), f32[32,8,128]{2,1,0:T(8,128)S(1)}, u32[]{:S(2)}, u32[]{:S(2)}) async-start(f32[32,8,128]{2,1,0:T(8,128)} %pack.1.sent), calls=%async_computation | async-start | bytes 262144 | tf_op jit(solution)/shard_map/all_to_all | solution.py:588
  22.6 10.0 %collective-permute-start = (f32[2,16,128]{2,1,0:T(8,128)S(1)}, f32[2,16,128]{2,1,0:T(8,128)S(1)}, u32[]{:S(2)}, u32[]{:S(2)}) collective-permute-start(f32[2,16,128]{2,1,0:T(8,128)S(1)} %get-tuple-element.43), channel_id=1, source_target_pairs={{0,126},{126,0},{1,127},{127,1},{2,124},{124,2},{3,125},{125,3},{8... | collective-permute-start | bytes 49160 | tf_op jit(solution)/shard_map/ppermute | solution.py:634

commit v8 on v7

--- a/solution.py
+++ b/solution.py
@@ -254,7 +254,7 @@
             for l in range(9):
                 term = both if l == 0 else harmonic[l] * both
                 sums[l] = term if sums[l] is None else sums[l] + term
-            yield
+        yield
         high, lo = split(jnp.concatenate(sums, axis=1))
         moments = dot(w_one_cat, jnp.concatenate([high, lo, high], axis=0))
         yield
@@ -500,7 +500,6 @@
             rows = jnp.concatenate([d_high, d - d_high], axis=0).astype(BF16)
             term = dot_t(rows, spots(k))
             back = term if back is None else back + term
-            yield
         return back[0:8] + back[8:16], centre
 
     def own_tile(t):

time: 44.7 us -> 44.6 us (level)
  no operation moved by 1% of the time
where the time goes in v8:
time: 44.6 us; the launch traced here: 44.3 us
  starting transfers between devices  18.4 us (41%)
  Pallas kernels  12.8 us (29%)
  waiting for transfers between devices  6.27 us (14%)
  blocking collectives  6.2 us (14%)
  between operations  0.69 us (2%)
    all_to_all x1, starting transfers between devices, on_device(): got = keep(lax.all_to_all(sent, both, 0, 0, axis_index_groups=planes))  10.3 us
    ppermute x1, starting transfers between devices, on_device(): across = keep(lax.ppermute(own, both, beside))  8.04 us
    all_to_all x1, waiting for transfers between devices, on_device(): got = keep(lax.all_to_all(sent, both, 0, 0, axis_index_groups=planes))  6.26 us
    all_to_all x1, blocking collectives, on_device(): back = keep(lax.all_to_all(grad, both, 0, 0, axis_index_groups=quads))  6.2 us
    pallas_call x1, Pallas kernels, on_device(): pl.pallas_call(force_kernel, out_shape=(near(4, 8, 128),) + kept, in_spec...  4.83 us
    pallas_call x1, Pallas kernels, on_device(): pl.pallas_call(pack_kernel, out_shape=shape(32, 8, 128), in_specs=[VM] *...  1.97 us
    pallas_call x1, Pallas kernels, on_device(): pl.pallas_call(early_kernel, out_shape=(near(2, 16, 128),) + kept[:6], in...  1.85 us
    pallas_call x1, Pallas kernels, on_device(): pl.pallas_call(late_kernel, out_shape=kept, in_specs=[VM] * 15, out_specs...  1.83 us
  transfers between devices with their start and end apart: 2, of which 1 were waited for; matrix products, arithmetic and copies ran while one was open for 0% of the time, Pallas kernels for 8%

profile of v8, /device:TPU:1, one launch (start us, length us, event | category | flops | bytes accessed | tf_op | source)
XLA Modules:
  0.0 44.3 jit_solution(12381664438123668108)
XLA Ops:
  0.6 2.0 %pack.1.sent = f32[32,8,128]{2,1,0:T(8,128)} custom-call(bf16[4,2,128,96]{3,2,1,0:T(8,128)(2,1)} %constant.2.clone.table, f32[3,4,64]{2,1,0:T(4,128)} %bitcast.7, f32[3,4,64]{2,1,0:T(4,128)} %bitcast.8, f32[3,4,64]{2,1,0:T(4,128)} %bitcast.9, s32[1,64]{1,0:T(1,128)} %bitcast.10, s32[4,4,64]{2,1,0:T(4,128)} %nbr.1, s32[4,64]{1,0:T(4,128)} %counts.1, ...), custom_call_target="tpu_custom_call" | custom-call | tf_op jit(solution)/shard_map/pack/pallas_call | solution.py:584
  2.6 10.3 %all-to-all-start = ((f32[32,8,128]{2,1,0:T(8,128)}), f32[32,8,128]{2,1,0:T(8,128)S(1)}, u32[]{:S(2)}, u32[]{:S(2)}) async-start(f32[32,8,128]{2,1,0:T(8,128)} %pack.1.sent), calls=%async_computation | async-start | bytes 262144 | tf_op jit(solution)/shard_map/all_to_all | solution.py:587
  13.0 1.5 %forms.1 = (bf16[2,384,384]{2,1,0:T(8,128)(2,1)S(1)}, bf16[2,128,1152]{2,1,0:T(8,128)(2,1)S(1)}, bf16[2,128,384]{2,1,0:T(8,128)(2,1)S(1)}, f32[4,128,128]{2,1,0:...) custom-call(f32[32,8,128]{2,1,0:T(8,128)} %pack.1.sent, ...), custom_call_target="tpu_custom_call" | custom-call | flops 2000000000 | bytes 4000000 | tf_op jit(solution)/shard_map/forms/pallas_call | solution.py:588
  14.5 6.3 %all-to-all-done.got = f32[32,8,128]{2,1,0:T(8,128)S(1)} async-done(((f32[32,8,128]{2,1,0:T(8,128)}), f32[32,8,128]{2,1,0:T(8,128)S(1)}, u32[]{:S(2)}, u32[]{:S(2)}) %all-to-all-start) | async-done | bytes 131104 | tf_op jit(solution)/shard_map/all_to_all | solution.py:587
  20.7 0.1 modes.1
  20.8 1.9 %early.1 = (f32[2,16,128]{2,1,0:T(8,128)S(1)}, bf16[6,256,512]{2,1,0:T(8,128)(2,1)S(1)}, f32[6,4,8,128]{3,2,1,0:T(8,128)S(1)}, f32[6,4,16,128]{3,2,1,0:T(8,128)S...) custom-call(f32[4,16,128]{2,1,0:T(8,128)S(1)} %get-tuple-element.33., ...), custom_call_target="tpu_custom_call", output_to_operand_aliasing={{0}: (9, {})} | custom-call | tf_op jit(solution)/shard_map/early/pallas_call | solution.py:623
  22.7 8.0 %collective-permute-start = (f32[2,16,128]{2,1,0:T(8,128)S(1)}, f32[2,16,128]{2,1,0:T(8,128)S(1)}, u32[]{:S(2)}, u32[]{:S(2)}) collective-permute-start(f32[2,16,128]{2,1,0:T(8,128)S(1)} %get-tuple-element.43), channel_id=1, source_target_pairs={{0,126},{126,0},{1,127},{127,1},{2,124},{124,2},{3,125},{125,3},{8... | collective-permute-start | bytes 49160 | tf_op jit(solution)/shard_map/ppermute | solution.py:633
  30.8 1.8 %late.1 = (bf16[6,256,512]{2,1,0:T(8,128)(2,1)S(1)}, f32[6,4,8,128]{3,2,1,0:T(8,128)S(1)}, f32[6,4,16,128]{3,2,1,0:T(8,128)S(1)}, f32[6,9,128,128]{3,2,1,0:T(8,1...) custom-call(f32[4,16,128]{2,1,0:T(8,128)S(1)} %get-tuple-element.33., ...), custom_call_target="tpu_custom_call", output_to_operand_aliasing={{0}: (9, {}), {1}: (10, {}), {2}: (11, {}), {3}: (12, {}), ... | custom-call | flops 4000000000 | bytes 8000000 | tf_op jit(solution)/shard_map/late/pallas_call | solution.py:634
  32.6 0.0 collective-permute-done.across
  32.6 4.8 %force.1 = (f32[4,8,128]{2,1,0:T(8,128)S(1)}, bf16[6,256,512]{2,1,0:T(8,128)(2,1)S(1)}, f32[6,4,8,128]{3,2,1,0:T(8,128)S(1)}, f32[6,4,16,128]{3,2,1,0:T(8,128)S(...) custom-call(f32[4,16,128]{2,1,0:T(8,128)S(1)} %get-tuple-element.33., ...), custom_call_target="tpu_custom_call", output_to_operand_aliasing={{1}: (11, {}), {2}: (12, {}), {3}: (13, {}), {4}: (14, {}),... | custom-call | tf_op jit(solution)/shard_map/force/pallas_call | solution.py:645
  37.4 6.2 %all_to_all.10.got = f32[4,8,128]{2,1,0:T(8,128)S(1)} all-to-all(f32[4,8,128]{2,1,0:T(8,128)S(1)} %get-tuple-element.59), channel_id=1, replica_groups={{0,1,2,3},{4,5,6,7},{8,9,10,11},{12,13,14,15},{16,17,18,19},{20,21,22,2..., dimensions={0} | all-to-all | bytes 32768 | tf_op jit(solution)/shard_map/all_to_all | solution.py:655
  43.6 0.7 %finish.1 = (f32[3,4,64]{2,1,0:T(4,128)}, f32[3,4,64]{2,1,0:T(4,128)}, f32[3,4,64]{2,1,0:T(4,128)}) custom-call(f32[4,8,128]{2,1,0:T(8,128)S(1)} %all_to_all.10.got), custom_call_target="tpu_custom_call" | custom-call | tf_op jit(solution)/shard_map/finish/pallas_call | solution.py:656
Async XLA Ops:
  2.6 18.1 %all-to-all-start = ((f32[32,8,128]{2,1,0:T(8,128)}), f32[32,8,128]{2,1,0:T(8,128)S(1)}, u32[]{:S(2)}, u32[]{:S(2)}) async-start(f32[32,8,128]{2,1,0:T(8,128)} %pack.1.sent), calls=%async_computation | async-start | bytes 262144 | tf_op jit(solution)/shard_map/all_to_all | solution.py:587
  22.7 9.9 %collective-permute-start = (f32[2,16,128]{2,1,0:T(8,128)S(1)}, f32[2,16,128]{2,1,0:T(8,128)S(1)}, u32[]{:S(2)}, u32[]{:S(2)}) collective-permute-start(f32[2,16,128]{2,1,0:T(8,128)S(1)} %get-tuple-element.43), channel_id=1, source_target_pairs={{0,126},{126,0},{1,127},{127,1},{2,124},{124,2},{3,125},{125,3},{8... | collective-permute-start | bytes 49160 | tf_op jit(solution)/shard_map/ppermute | solution.py:633
